TPU v7x, 32 devices: a whole 2x2x4 slice. The times are simulated.
32 devices in a mesh: expert: 8 (over z, y), hidden: 4 (over x, core).
Axes of the slice: x: 2, y: 2, z: 4, core: 2. Of those that a mesh axis runs over, the one named last changes fastest.
Arguments:
- tokens: bfloat16 [2, 6144, 768], P(None, 'expert'), may hold values from -6 to 6
- doc_ids: int32 [2, 8, 768], P(None, 'expert'), may hold values from 0 to 3, never falling along the last dimension, each value on 1 to 384 neighbouring positions
- pad_mask: int32 [2, 6144], P(None, 'expert'), may hold values 0 or 1
- norm1_gain: float32 [768], replicated, may hold values from 0.5 to 1.5
- norm1_bias: float32 [768], replicated, may hold values from -1 to 1
- qkv_weight: bfloat16 [3, 768, 768], P(None, None, 'hidden'), may hold values from -0.3125 to 0.3125
- out_weight: bfloat16 [768, 768], P('hidden'), may hold values from -0.875 to 0.875
- norm2_gain: float32 [768], replicated, may hold values from 0.5 to 1.5
- norm2_bias: float32 [768], replicated, may hold values from -1 to 1
- router: bfloat16 [768, 8], replicated, may hold values from -0.15625 to 0.15625
- routes: int32 [2, 6144, 2], P(None, 'expert'), may hold values from 0 to 7, all different within a row; in each aligned block of 768 rows (0 to 767, 768 to 1535, ..., all dimensions but the last counted through in order) at most 384 rows name the same one
- up_weight: bfloat16 [8, 768, 3072], P('expert', None, 'hidden'), may hold values from -0.21875 to 0.21875
- down_weight: bfloat16 [8, 768, 3072], P('expert', None, 'hidden'), may hold values from -0.15625 to 0.15625
- cotangent: bfloat16 [2, 6144, 768], P(None, 'expert'), may hold values from -6 to 6
Outputs:
- block_out: float32 [2, 6144, 768], P(None, 'expert')
- grad_tokens: float32 [2, 6144, 768], P(None, 'expert')
- grad_norm1_gain: float32 [768], replicated
- grad_norm1_bias: float32 [768], replicated
- grad_qkv: float32 [3, 768, 768], P(None, None, 'hidden')
- grad_out: float32 [768, 768], P('hidden')
- grad_norm2_gain: float32 [768], replicated
- grad_norm2_bias: float32 [768], replicated
- grad_router: float32 [768, 8], replicated
- grad_up: float32 [4, 768, 3072], P(None, 'expert', 'hidden')
- grad_down: float32 [4, 768, 3072], P(None, 'expert', 'hidden')
Inputs may be any that keep to these rules, and one draw needn't show every extreme that they name: `routes`: each token names 2 different experts. In each micro-batch the tokens of one pack name any one expert at most 384 times, a bound that some block reaches. `doc_ids`: within a pack document numbers never fall; each document covers 1 to 384 consecutive tokens, and some covers exactly 384. `pad_mask`: 1 marks a real token, 0 a padding token.
All inputs are finite; a program needn't handle non-finite values. No bound on the sum of `pad_mask` on one device may be relied on, other than what follows from the above.
Results may differ from a plain program's by a relative error of at most 0.028.
Values may be sent and summed in bfloat16 or wider, within the bound.
No kernel may reach another device: no remote copies, remote signals or barrier semaphores. Data moves between devices by JAX's collectives and lax.ppermute only.
A program may use at most 256 MiB of HBM per device.

v0:
```python
import jax
import jax.numpy as jnp
from jax import lax
from jax.sharding import PartitionSpec as P

HEAD_DIM = 64


EPSILON = 1e-05
PRECISE = lax.Precision.HIGHEST
MASKED = -1e30


def layer_norm(values, norm_gain, norm_bias):
    centre = values - jnp.mean(values, -1, keepdims=True)
    spread = jnp.mean(centre * centre, -1, keepdims=True)
    return centre * lax.rsqrt(spread + EPSILON) * norm_gain + norm_bias


def gelu_tanh(values):
    return jax.nn.gelu(values, approximate=True)


def visible(doc_row, pad_row):
    total_rows = doc_row.shape[0]
    query_pos = jnp.arange(total_rows)[:, None]
    key_pos = jnp.arange(total_rows)[None, :]
    same_doc = doc_row[:, None] == doc_row[None, :]
    is_real = (pad_row[None, :] == 1) | (query_pos == key_pos)
    return (key_pos <= query_pos) & same_doc & is_real


def slot_tables(route_rows, experts, capacity):
    flat_routes = route_rows.reshape(-1)
    onehot = (flat_routes[:, None] == jnp.arange(experts, dtype=jnp.int32)[None, :]).astype(
        jnp.int32
    )
    before = jnp.cumsum(onehot, 0) - onehot
    placed = jnp.sum(before * onehot, 1)
    slot_index = flat_routes * capacity + placed
    total_rows = flat_routes.shape[0]
    source = (
        jnp.full((experts * capacity,), total_rows, jnp.int32)
        .at[slot_index]
        .set(jnp.arange(total_rows, dtype=jnp.int32))
    )
    return (slot_index, source)


def masked_scores(queries, key_rows, allowed, score_scale):
    scores = (
        jnp.einsum("qhd,khd->hqk", queries, key_rows, preferred_element_type=jnp.float32)
        * score_scale
    )
    return jnp.where(allowed[None], scores, MASKED)


def attend_forward(queries, key_rows, value_rows, allowed, score_scale):
    scores = masked_scores(queries, key_rows, allowed, score_scale)
    row_peak = jnp.max(scores, -1, keepdims=True)
    exponent = jnp.exp(scores - row_peak)
    row_total = jnp.sum(exponent, -1, keepdims=True)
    attn_weights = (exponent / row_total).astype(jnp.bfloat16)
    output = jnp.einsum(
        "hqk,khd->qhd", attn_weights, value_rows, preferred_element_type=jnp.float32
    )
    return (output, row_peak + jnp.log(row_total))


def attend_backward(queries, key_rows, value_rows, allowed, score_scale, log_total, heads_grad):
    scores = masked_scores(queries, key_rows, allowed, score_scale)
    attn_weights = jnp.exp(scores - log_total)
    weight_grad = jnp.einsum(
        "qhd,khd->hqk", heads_grad, value_rows, preferred_element_type=jnp.float32
    )
    row_delta = jnp.sum(attn_weights * weight_grad, -1, keepdims=True)
    score_grad = (attn_weights * (weight_grad - row_delta)).astype(jnp.bfloat16)
    query_grad = (
        jnp.einsum("hqk,khd->qhd", score_grad, key_rows, preferred_element_type=jnp.float32)
        * score_scale
    )
    key_grad = (
        jnp.einsum("hqk,qhd->khd", score_grad, queries, preferred_element_type=jnp.float32)
        * score_scale
    )
    value_grad = jnp.einsum(
        "hqk,qhd->khd",
        attn_weights.astype(jnp.bfloat16),
        heads_grad,
        preferred_element_type=jnp.float32,
    )
    return (query_grad, key_grad, value_grad)


def shards(
    tokens,
    doc_ids,
    pad_mask,
    norm1_gain,
    norm1_bias,
    qkv_weight,
    out_weight,
    norm2_gain,
    norm2_bias,
    router,
    routes,
    up_weight,
    down_weight,
    cotangent,
):
    micro_count, row_count, feat_width = tokens.shape
    expert_count = router.shape[1]
    top_count = routes.shape[2]
    capacity = 2 * row_count * top_count // expert_count
    local_heads = qkv_weight.shape[2] // HEAD_DIM
    score_scale = HEAD_DIM ** (-0.5)
    trainable = lax.axis_index("expert") >= lax.axis_size("expert") // 2
    up_local = up_weight[0]
    down_local = down_weight[0]
    router_wide = router.astype(jnp.float32)
    zero_row = jnp.zeros((1, feat_width), jnp.bfloat16)
    grad_qkv = jnp.zeros(qkv_weight.shape, jnp.float32)
    grad_proj = jnp.zeros(out_weight.shape, jnp.float32)
    grad_router = jnp.zeros(router.shape, jnp.float32)
    gain1_total = jnp.zeros((feat_width,), jnp.float32)
    bias1_total = jnp.zeros((feat_width,), jnp.float32)
    gain2_total = jnp.zeros((feat_width,), jnp.float32)
    bias2_total = jnp.zeros((feat_width,), jnp.float32)
    expert_acc = (jnp.zeros(up_local.shape, jnp.float32), jnp.zeros(down_local.shape, jnp.float32))
    outputs = []
    input_grads = []
    for micro_idx in range(micro_count):
        inputs = tokens[micro_idx].astype(jnp.float32)
        allowed = visible(doc_ids[micro_idx, 0], pad_mask[micro_idx])
        normed1, norm1_pull = jax.vjp(layer_norm, inputs, norm1_gain, norm1_bias)
        attn_in = normed1.astype(jnp.bfloat16)
        projected = jnp.einsum(
            "rd,cdf->crf", attn_in, qkv_weight, preferred_element_type=jnp.float32
        ).astype(jnp.bfloat16)
        head_view = projected.reshape(3, row_count, local_heads, HEAD_DIM)
        queries, key_rows, value_rows = (head_view[0], head_view[1], head_view[2])
        heads_out, log_total = attend_forward(queries, key_rows, value_rows, allowed, score_scale)
        heads_low = heads_out.reshape(row_count, -1).astype(jnp.bfloat16)
        attn_term = jnp.dot(heads_low, out_weight, preferred_element_type=jnp.float32)
        attention = lax.psum(attn_term.astype(jnp.bfloat16), "hidden").astype(jnp.float32)
        residual = inputs + attention
        normed2, norm2_pull = jax.vjp(layer_norm, residual, norm2_gain, norm2_bias)
        moe_in = normed2.astype(jnp.bfloat16)
        logits = jnp.dot(moe_in, router, preferred_element_type=jnp.float32)
        route_rows = routes[micro_idx]
        picker = (
            route_rows[:, :, None] == jnp.arange(expert_count, dtype=jnp.int32)[None, None, :]
        ).astype(jnp.float32)
        chosen = jnp.sum(picker * logits[:, None, :], -1)
        gate_vals = jax.nn.softmax(chosen, -1)
        slot_index, source = slot_tables(route_rows, expert_count, capacity)
        padded_in = jnp.concatenate([moe_in, zero_row], 0)
        send_rows = padded_in[source // top_count].reshape(expert_count, capacity, feat_width)
        received = lax.all_to_all(
            send_rows, "expert", split_axis=0, concat_axis=0, tiled=True
        ).reshape(-1, feat_width)
        hidden_pre = jnp.dot(received, up_local, preferred_element_type=jnp.float32)
        hidden_act = gelu_tanh(hidden_pre).astype(jnp.bfloat16)
        slice_out = jnp.einsum(
            "rf,df->rd", hidden_act, down_local, preferred_element_type=jnp.float32
        )
        summed = lax.psum(slice_out.astype(jnp.bfloat16), "hidden")
        returned = lax.all_to_all(
            summed.reshape(expert_count, capacity, feat_width),
            "expert",
            split_axis=0,
            concat_axis=0,
            tiled=True,
        )
        flat_back = jnp.concatenate([returned.reshape(-1, feat_width), zero_row], 0)
        expert_rows = flat_back[slot_index].reshape(row_count, top_count, feat_width)
        expert_wide = expert_rows.astype(jnp.float32)
        mixture = jnp.sum(gate_vals[:, :, None] * expert_wide, 1)
        outputs.append(residual + mixture)
        upstream = cotangent[micro_idx].astype(jnp.float32)
        expert_grad = (gate_vals[:, :, None] * upstream[:, None, :]).astype(jnp.bfloat16)
        gate_grad = jnp.sum(upstream[:, None, :] * expert_wide, -1)
        chosen_grad = gate_vals * (gate_grad - jnp.sum(gate_vals * gate_grad, -1, keepdims=True))
        logit_grad = jnp.sum(picker * chosen_grad[:, :, None], 1)
        padded_grad = jnp.concatenate([expert_grad.reshape(-1, feat_width), zero_row], 0)
        send_grad = padded_grad[source].reshape(expert_count, capacity, feat_width)
        grad_rows = lax.all_to_all(
            send_grad, "expert", split_axis=0, concat_axis=0, tiled=True
        ).reshape(-1, feat_width)
        act_grad = jnp.dot(grad_rows, down_local, preferred_element_type=jnp.float32)
        gelu_grad = jax.vjp(gelu_tanh, hidden_pre)[1](act_grad)[0]
        pre_grad = gelu_grad.astype(jnp.bfloat16)
        in_term = jnp.einsum("rf,df->rd", pre_grad, up_local, preferred_element_type=jnp.float32)
        in_summed = lax.psum(in_term.astype(jnp.bfloat16), "hidden")
        in_back = lax.all_to_all(
            in_summed.reshape(expert_count, capacity, feat_width),
            "expert",
            split_axis=0,
            concat_axis=0,
            tiled=True,
        )
        flat_in = jnp.concatenate([in_back.reshape(-1, feat_width), zero_row], 0)
        copies_low = flat_in[slot_index].reshape(row_count, top_count, feat_width)
        copies_grad = copies_low.astype(jnp.float32)
        normed2_grad = jnp.sum(copies_grad, 1) + jnp.dot(
            logit_grad, router_wide.T, precision=PRECISE
        )

        def expert_update(acc_pair):
            return (
                acc_pair[0]
                + jnp.einsum("rd,rf->df", received, pre_grad, preferred_element_type=jnp.float32),
                acc_pair[1]
                + jnp.einsum(
                    "rd,rf->df", grad_rows, hidden_act, preferred_element_type=jnp.float32
                ),
            )

        def expert_keep(acc_pair):
            return acc_pair

        expert_acc = lax.cond(trainable, expert_update, expert_keep, expert_acc)
        grad_router = grad_router + jnp.dot(
            moe_in.astype(jnp.float32).T, logit_grad, precision=PRECISE
        )
        resid_grad, gain2_grad, bias2_grad = norm2_pull(normed2_grad)
        gain2_total = gain2_total + gain2_grad
        bias2_total = bias2_total + bias2_grad
        resid_grad = upstream + resid_grad
        attn_grad = resid_grad.astype(jnp.bfloat16)
        grad_proj = grad_proj + jnp.einsum(
            "rf,rd->fd", heads_low, attn_grad, preferred_element_type=jnp.float32
        )
        heads_grad = jnp.einsum(
            "rd,fd->rf", attn_grad, out_weight, preferred_element_type=jnp.float32
        ).astype(jnp.bfloat16)
        query_grad, key_grad, value_grad = attend_backward(
            queries,
            key_rows,
            value_rows,
            allowed,
            score_scale,
            log_total,
            heads_grad.reshape(row_count, local_heads, HEAD_DIM),
        )
        qkv_grad = (
            jnp.stack([query_grad, key_grad, value_grad])
            .reshape(3, row_count, -1)
            .astype(jnp.bfloat16)
        )
        grad_qkv = grad_qkv + jnp.einsum(
            "rd,crf->cdf", attn_in, qkv_grad, preferred_element_type=jnp.float32
        )
        normed1_term = jnp.einsum(
            "crf,cdf->rd", qkv_grad, qkv_weight, preferred_element_type=jnp.float32
        )
        normed1_grad = lax.psum(normed1_term.astype(jnp.bfloat16), "hidden").astype(jnp.float32)
        input_grad, gain1_grad, bias1_grad = norm1_pull(normed1_grad)
        gain1_total = gain1_total + gain1_grad
        bias1_total = bias1_total + bias1_grad
        input_grads.append(resid_grad + input_grad)
    reduced = (
        lax.psum(gain1_total.astype(jnp.bfloat16), "expert").astype(jnp.float32),
        lax.psum(bias1_total.astype(jnp.bfloat16), "expert").astype(jnp.float32),
        lax.psum(grad_qkv.astype(jnp.bfloat16), "expert").astype(jnp.float32),
        lax.psum(grad_proj.astype(jnp.bfloat16), "expert").astype(jnp.float32),
        lax.psum(gain2_total.astype(jnp.bfloat16), "expert").astype(jnp.float32),
        lax.psum(bias2_total.astype(jnp.bfloat16), "expert").astype(jnp.float32),
        lax.psum(grad_router.astype(jnp.bfloat16), "expert").astype(jnp.float32),
    )
    expert_parts = (
        lax.all_to_all(
            expert_acc[0][None].astype(jnp.bfloat16),
            "expert",
            split_axis=1,
            concat_axis=0,
            tiled=True,
        ).astype(jnp.float32),
        lax.all_to_all(
            expert_acc[1][None].astype(jnp.bfloat16),
            "expert",
            split_axis=1,
            concat_axis=0,
            tiled=True,
        ).astype(jnp.float32),
    )
    half_count = expert_count // 2
    return (
        jnp.stack(outputs),
        jnp.stack(input_grads),
        reduced[0],
        reduced[1],
        reduced[2],
        reduced[3],
        reduced[4],
        reduced[5],
        reduced[6],
        expert_parts[0][half_count:],
        expert_parts[1][half_count:],
    )


def solution(mesh):
    placed = (
        P(None, "expert", None),
        P(None, "expert", None),
        P(None, "expert"),
        P(),
        P(),
        P(None, None, "hidden"),
        P("hidden", None),
        P(),
        P(),
        P(),
        P(None, "expert", None),
        P("expert", None, "hidden"),
        P("expert", None, "hidden"),
        P(None, "expert", None),
    )
    return jax.shard_map(
        shards,
        mesh=mesh,
        in_specs=placed,
        out_specs=(
            P(None, "expert", None),
            P(None, "expert", None),
            P(),
            P(),
            P(None, None, "hidden"),
            P("hidden", None),
            P(),
            P(),
            P(),
            P(None, "expert", "hidden"),
            P(None, "expert", "hidden"),
        ),
        check_vma=False,
    )
```

profile of v0, /device:TPU:0, one launch (start us, length us, event | category | flops | bytes accessed | tf_op | source)
XLA Modules:
  0.0 1665.2 jit_solution(2692091185587568231)
XLA Ops:
  46.5 18.1 %all-reduce.18.cloned.1.call-done = bf16[768,768]{1,0:T(8,128)(2,1)} async-done(((bf16[768,768]{1,0:T(8,128)(2,1)}), bf16[768,768]{1,0:T(8,128)(2,1)}) %all-reduce.18.cloned.1.call-update) | async-done | bytes 1179664 | tf_op jit(solution)/shard_map/psum | solution.py:145
  128.1 14.5 gather_fusion.4
  159.9 14.5 gather_fusion.2
  174.4 78.2 %all-to-all-done.4 = bf16[8,384,768]{2,1,0:T(8,128)(2,1)} async-done(((bf16[8,384,768]{2,1,0:T(8,128)(2,1)}), bf16[8,384,768]{2,1,0:T(8,128)(2,1)}, u32[]{:S(2)}, u32[]{:S(2)}) %all-to-all-start.4) | async-done | bytes 4718624 | tf_op jit(solution)/shard_map/all_to_all | solution.py:187
  257.5 14.5 gather_fusion
  272.1 89.1 %all-to-all-done.2 = bf16[8,384,768]{2,1,0:T(8,128)(2,1)} async-done(((bf16[8,384,768]{2,1,0:T(8,128)(2,1)}), bf16[8,384,768]{2,1,0:T(8,128)(2,1)}, u32[]{:S(2)}, u32[]{:S(2)}) %all-to-all-start.2) | async-done | bytes 4718624 | tf_op jit(solution)/shard_map/all_to_all | solution.py:159
  382.2 14.6 gather_fusion.6
  396.8 72.8 %all-to-all-done = bf16[8,384,768]{2,1,0:T(8,128)(2,1)} async-done(((bf16[8,384,768]{2,1,0:T(8,128)(2,1)}), bf16[8,384,768]{2,1,0:T(8,128)(2,1)}, u32[]{:S(2)}, u32[]{:S(2)}) %all-to-all-start) | async-done | bytes 4718624 | tf_op jit(solution)/shard_map/all_to_all | solution.py:159
  481.9 12.1 fusion.6
  515.2 62.7 %all-to-all-done.6 = bf16[8,384,768]{2,1,0:T(8,128)(2,1)} async-done(((bf16[8,384,768]{2,1,0:T(8,128)(2,1)}), bf16[8,384,768]{2,1,0:T(8,128)(2,1)}, u32[]{:S(2)}, u32[]{:S(2)}) %all-to-all-start.6) | async-done | bytes 4718624 | tf_op jit(solution)/shard_map/all_to_all | solution.py:187
  578.0 12.1 fusion.13
  618.3 32.7 %all-to-all-start.8 = ((bf16[8,2,36864]{2,1,0:T(2,128)(2,1)}), bf16[8,2,36864]{2,1,0:T(2,128)(2,1)}, u32[]{:S(2)}, u32[]{:S(2)}) async-start(bf16[8,2,36864]{2,1,0:T(2,128)(2,1)} %reshape.916), calls=%async_computation.8 | async-start | bytes 2359296 | tf_op jit(solution)/shard_map/all_to_all | solution.py:272
  661.1 18.7 %all-to-all-done.8 = bf16[8,2,36864]{2,1,0:T(2,128)(2,1)} async-done(((bf16[8,2,36864]{2,1,0:T(2,128)(2,1)}), bf16[8,2,36864]{2,1,0:T(2,128)(2,1)}, u32[]{:S(2)}, u32[]{:S(2)}) %all-to-all-start.8) | async-done | bytes 1179680 | tf_op jit(solution)/shard_map/all_to_all | solution.py:272
  679.8 32.5 %all_to_all.58 = bf16[8,2,36864]{2,1,0:T(2,128)(2,1)S(1)} all-to-all(bf16[8,2,36864]{2,1,0:T(2,128)(2,1)S(1)} %reshape.918), channel_id=1, replica_groups=mesh['expert'=8,'hidden'=4] {'expert'}, dimensions={0} | all-to-all | bytes 2359296 | tf_op jit(solution)/shard_map/all_to_all | solution.py:279
  712.3 209.2 %all-reduce.26.cloned.1.call-done = (bf16[8,384,768]{2,1,0:T(8,128)(2,1)}, bf16[8,384,768]{2,1,0:T(8,128)(2,1)}, bf16[8,384,768]{2,1,0:T(8,128)(2,1)}, bf16[8,384,768]{2,1,0:T(8,128)(2,1)}) async-done(((bf16[8,384,768]{2,1,0:T(8,128)(2,1)}, bf16[8,384,768]{2,1,0:T(8,128)(2,1)}, bf16[8,384,768]{2,1,0:T(8,128)(2,1)}, bf16[8,384,768]{2,1,0:T(8,128)(2,1)}), (bf16[8,384,768]{2,1,0:T(8,128)(2,1)}, ...) | async-done | bytes 18874384 | tf_op jit(solution)/shard_map/psum | solution.py:167
  921.5 110.1 %all_to_all.59 = bf16[8,384,768]{2,1,0:T(8,128)(2,1)} all-to-all(bf16[8,384,768]{2,1,0:T(8,128)(2,1)} %get-tuple-element.99), channel_id=1, replica_groups=mesh['expert'=8,'hidden'=4] {'expert'}, dimensions={0} | all-to-all | bytes 9437184 | tf_op jit(solution)/shard_map/all_to_all | solution.py:168
  1031.6 107.6 %all_to_all.60 = bf16[8,384,768]{2,1,0:T(8,128)(2,1)} all-to-all(bf16[8,384,768]{2,1,0:T(8,128)(2,1)S(1)} %copy-done.38), channel_id=1, replica_groups=mesh['expert'=8,'hidden'=4] {'expert'}, dimensions={0} | all-to-all | bytes 9437184 | tf_op jit(solution)/shard_map/all_to_all | solution.py:195
  1139.3 107.5 %all_to_all.61 = bf16[8,384,768]{2,1,0:T(8,128)(2,1)} all-to-all(bf16[8,384,768]{2,1,0:T(8,128)(2,1)S(1)} %bitcast.379), channel_id=1, replica_groups=mesh['expert'=8,'hidden'=4] {'expert'}, dimensions={0} | all-to-all | bytes 9437184 | tf_op jit(solution)/shard_map/all_to_all | solution.py:195
  1296.7 58.3 %all-to-all-done.3 = bf16[8,384,768]{2,1,0:T(8,128)(2,1)} async-done(((bf16[8,384,768]{2,1,0:T(8,128)(2,1)}), bf16[8,384,768]{2,1,0:T(8,128)(2,1)}, u32[]{:S(2)}, u32[]{:S(2)}) %all-to-all-start.3) | async-done | bytes 4718624 | tf_op jit(solution)/shard_map/all_to_all | solution.py:168
  1385.8 13.4 multiply_reduce_fusion.2
  1406.4 13.7 multiply_reduce_fusion.3
  1515.2 47.1 %all-reduce.24.cloned.1.call-done = (bf16[768,768]{1,0:T(8,128)(2,1)}, bf16[768,768]{1,0:T(8,128)(2,1)}) async-done(((bf16[768,768]{1,0:T(8,128)(2,1)}, bf16[768,768]{1,0:T(8,128)(2,1)}), (bf16[768,768]{1,0:T(8,128)(2,1)}, bf16[768,768]{1,0:T(8,128)(2,1)})) %all-reduce.24.cloned.1.call-update) | async-done | bytes 2359312 | tf_op jit(solution)/shard_map/psum | solution.py:257
  1570.2 38.8 %all-reduce.8 = (bf16[768]{0:T(1024)(128)(2,1)}, bf16[768]{0:T(1024)(128)(2,1)}, bf16[768]{0:T(1024)(128)(2,1)}, bf16[768]{0:T(1024)(128)(2,1)}, bf16[768,8]{0,1:T(8,128)(2,1)}) all-reduce(bf16[768]{0:T(1024)(128)(2,1)} %add_convert_fusion.6, ...), channel_id=1, replica_groups=mesh['expert'=8,'hidden'=4] {'expert'}, use_global_device_ids=true, to_apply=%region_56.57 | all-reduce | flops 9216 | bytes 36864 | tf_op jit(solution)/shard_map/psum | solution.py:263
  1617.9 29.0 %all-reduce.22.cloned.1.call-done = (bf16[3,768,192]{1,2,0:T(8,128)(2,1)}, bf16[192,768]{1,0:T(8,128)(2,1)}) async-done(((bf16[3,768,192]{1,2,0:T(8,128)(2,1)}, bf16[192,768]{1,0:T(8,128)(2,1)}), (bf16[3,768,192]{1,2,0:T(8,128)(2,1)}, bf16[192,768]{1,0:T(8,128)(2,1)})) %all-reduce.22.cloned.1.call-update) | async-done | bytes 1179664 | tf_op jit(solution)/shard_map/psum | solution.py:265
  (532 shorter events, 428.8 us)
Async XLA Ops:
  7.2 467.2 %copy-start = (bf16[1,768,768]{2,1,0:T(8,128)(2,1)S(1)}, bf16[1,768,768]{2,1,0:T(8,128)(2,1)}, u32[]{:S(2)}) copy-start(bf16[1,768,768]{2,1,0:T(8,128)(2,1)} %param.29) | copy-start | bytes 3538948
  7.2 57.4 %all-reduce.18.cloned.1.call-start = ((), (), s32[]{:S(2)}) async-start(), calls=%async_computation.10 | async-start | bytes 2359296 | tf_op jit(solution)/shard_map/psum | solution.py:145
  24.2 91.2 %all-reduce.20.cloned.1.call-start = ((), (), s32[]{:S(2)}) async-start(), calls=%async_computation.11 | async-start | bytes 2359296 | tf_op jit(solution)/shard_map/psum | solution.py:145
  25.8 97.3 %copy-start.102 = (s32[768,2]{0,1:T(2,128)}, s32[768,2]{0,1:T(2,128)S(1)}, u32[]{:S(2)}) copy-start(s32[768,2]{0,1:T(2,128)S(1)} %get-tuple-element.125) | copy-start | bytes 18436
  42.3 25.0 %copy-start.89 = (f32[768]{0:T(1024)}, f32[768]{0:T(1024)S(1)}, u32[]{:S(2)}) copy-start(f32[768]{0:T(1024)S(1)} %broadcast_multiply_fusion.3) | copy-start | bytes 9220
  88.1 17.5 %copy-start.138 = (f32[768]{0:T(1024)S(1)}, f32[768]{0:T(1024)}, u32[]{:S(2)}) copy-start(f32[768]{0:T(1024)} %get-tuple-element.75) | copy-start | bytes 9220
  142.7 110.0 %all-to-all-start.4 = ((bf16[8,384,768]{2,1,0:T(8,128)(2,1)}), bf16[8,384,768]{2,1,0:T(8,128)(2,1)}, u32[]{:S(2)}, u32[]{:S(2)}) async-start(bf16[8,384,768]{2,1,0:T(8,128)(2,1)} %bitcast.363), calls=%async_computation.4 | async-start | bytes 9437184 | tf_op jit(solution)/shard_map/all_to_all | solution.py:187
  252.7 108.5 %all-to-all-start.2 = ((bf16[8,384,768]{2,1,0:T(8,128)(2,1)}), bf16[8,384,768]{2,1,0:T(8,128)(2,1)}, u32[]{:S(2)}, u32[]{:S(2)}) async-start(bf16[8,384,768]{2,1,0:T(8,128)(2,1)} %bitcast.366), calls=%async_computation.2 | async-start | bytes 9437184 | tf_op jit(solution)/shard_map/all_to_all | solution.py:159
  361.2 108.5 %all-to-all-start = ((bf16[8,384,768]{2,1,0:T(8,128)(2,1)}), bf16[8,384,768]{2,1,0:T(8,128)(2,1)}, u32[]{:S(2)}, u32[]{:S(2)}) async-start(bf16[8,384,768]{2,1,0:T(8,128)(2,1)} %bitcast.364), calls=%async_computation | async-start | bytes 9437184 | tf_op jit(solution)/shard_map/all_to_all | solution.py:159
  469.6 108.3 %all-to-all-start.6 = ((bf16[8,384,768]{2,1,0:T(8,128)(2,1)}), bf16[8,384,768]{2,1,0:T(8,128)(2,1)}, u32[]{:S(2)}, u32[]{:S(2)}) async-start(bf16[8,384,768]{2,1,0:T(8,128)(2,1)} %bitcast.365), calls=%async_computation.6 | async-start | bytes 9437184 | tf_op jit(solution)/shard_map/all_to_all | solution.py:187
  474.3 447.2 %all-reduce.26.cloned.1.call-start = ((), (), s32[]{:S(2)}) async-start(), calls=%async_computation.14 | async-start | bytes 37748736 | tf_op jit(solution)/shard_map/psum | solution.py:167
  481.9 17.7 %copy-start.152 = (bf16[3072,768]{1,0:T(8,128)(2,1)}, bf16[3072,768]{1,0:T(8,128)(2,1)S(1)}, u32[]{:S(2)}) copy-start(bf16[3072,768]{1,0:T(8,128)(2,1)S(1)} %get-tuple-element.139) | copy-start | bytes 14155780
  617.1 33.9 %copy-start.34 = (f32[768,768]{1,0:T(8,128)S(1)}, f32[768,768]{1,0:T(8,128)}, u32[]{:S(2)}) copy-start(f32[768,768]{1,0:T(8,128)} %copy-done.33) | copy-start | bytes 7077892
  618.3 61.5 %all-to-all-start.8 = ((bf16[8,2,36864]{2,1,0:T(2,128)(2,1)}), bf16[8,2,36864]{2,1,0:T(2,128)(2,1)}, u32[]{:S(2)}, u32[]{:S(2)}) async-start(bf16[8,2,36864]{2,1,0:T(2,128)(2,1)} %reshape.916), calls=%async_computation.8 | async-start | bytes 2359296 | tf_op jit(solution)/shard_map/all_to_all | solution.py:272
  921.5 110.1 %copy-start.38 = (bf16[8,384,768]{2,1,0:T(8,128)(2,1)S(1)}, bf16[8,384,768]{2,1,0:T(8,128)(2,1)}, u32[]{:S(2)}) copy-start(bf16[8,384,768]{2,1,0:T(8,128)(2,1)} %get-tuple-element.100) | copy-start | bytes 14155780
  921.5 217.8 %slice-start.8 = ((s8[4718592]{0:T(1024)(128)(4,1)}), s8[4194304]{0:T(1024)(128)(4,1)S(1)}, s32[]{:S(2)}) async-start(s8[4718592]{0:T(1024)(128)(4,1)} %bitcast.378), calls=%async_computation.23 | async-start | bytes 8388608
  1031.6 107.6 %slice-start.9 = ((s8[4718592]{0:T(1024)(128)(4,1)}), s8[524288]{0:T(1024)(128)(4,1)S(1)}, s32[]{:S(2)}) async-start(s8[4718592]{0:T(1024)(128)(4,1)} %bitcast.378), calls=%async_computation.24 | async-start | bytes 1048576
  1246.8 108.2 %all-to-all-start.3 = ((bf16[8,384,768]{2,1,0:T(8,128)(2,1)}), bf16[8,384,768]{2,1,0:T(8,128)(2,1)}, u32[]{:S(2)}, u32[]{:S(2)}) async-start(bf16[8,384,768]{2,1,0:T(8,128)(2,1)} %get-tuple-element.98), calls=%async_computation.3 | async-start | bytes 9437184 | tf_op jit(solution)/shard_map/all_to_all | solution.py:168
  1251.5 310.8 %all-reduce.24.cloned.1.call-start = ((), (), s32[]{:S(2)}) async-start(), calls=%async_computation.13 | async-start | bytes 4718592 | tf_op jit(solution)/shard_map/psum | solution.py:257
  1406.4 14.9 copy-start.71
  1406.4 14.9 copy-start.84
  1406.4 14.9 copy-start.97
  1406.4 16.3 copy-start.24
  1507.7 139.3 %all-reduce.22.cloned.1.call-start = ((), (), s32[]{:S(2)}) async-start(), calls=%async_computation.12 | async-start | bytes 2359296 | tf_op jit(solution)/shard_map/psum | solution.py:265
  (150 other events, 596.0 us)
Sparse Core Ops, SparseCore 0:
  24.3 40.2 all-reduce.17
  77.7 37.7 all-reduce.19
  601.4 320.0 all-reduce.25
  1507.8 54.4 all-reduce.23
  1566.2 80.6 all-reduce.21
where the time goes:
time: 1670 us
  waiting for transfers between devices  693 us (41%)
  blocking collectives  397 us (24%)
  local copies, waits for them, and re-layouts  221 us (13%)
  other arithmetic  160 us (10%)
  matrix products  120 us (7%)
  starting transfers between devices  57.6 us (3%)
    all_to_all x2, blocking collectives, shards(): lax.all_to_all(in_summed.reshape(expert_count, capacity, feat_width), 'ex...  215 us
    psum x1, waiting for transfers between devices, shards(): summed = lax.psum(slice_out.astype(jnp.bfloat16), 'hidden')  209 us
    all_to_all x2, waiting for transfers between devices, shards(): lax.all_to_all(send_rows, 'expert', split_axis=0, concat_axis=0, tiled=True)  162 us
    all_to_all x2, waiting for transfers between devices, shards(): lax.all_to_all(send_grad, 'expert', split_axis=0, concat_axis=0, tiled=True)  141 us
    all_to_all x1, blocking collectives, shards(): lax.all_to_all(summed.reshape(expert_count, capacity, feat_width), 'exper...  110 us
    all_to_all x1, waiting for transfers between devices, shards(): lax.all_to_all(summed.reshape(expert_count, capacity, feat_width), 'exper...  58.3 us
    psum x1, waiting for transfers between devices, shards(): lax.psum(normed1_term.astype(jnp.bfloat16), 'hidden').astype(jnp.float32)  47.1 us
    psum x1, blocking collectives, shards(): lax.psum(gain1_total.astype(jnp.bfloat16), 'expert').astype(jnp.float32)  38.8 us
  transfers between devices with their start and end apart: 11, of which 11 were waited for; matrix products, arithmetic and copies ran while one was open for 15% of the time, Pallas kernels for 0%

commit v1 on v0

v1 whole, which is shorter than its diff:
```python
import jax
import jax.numpy as jnp
from jax import lax
from jax.sharding import PartitionSpec as P

HEAD_DIM = 64
EPSILON = 1e-05
PRECISE = lax.Precision.HIGHEST
MASKED = -1e30
EXTRA = 8
BF = jnp.bfloat16
F32 = jnp.float32


def round_up(value, step):
    return -(-value // step) * step


def swap(values, axis, bit):
    size = lax.axis_size(axis)
    return lax.ppermute(values, axis, [(i, i ^ bit) for i in range(size)])


def ordered(flag, mine, other):
    return jnp.where(
        flag == 0, jnp.concatenate([mine, other], 0), jnp.concatenate([other, mine], 0)
    )


def normalize(values):
    centre = values - jnp.mean(values, -1, keepdims=True)
    spread = jnp.mean(centre * centre, -1, keepdims=True)
    scale = lax.rsqrt(spread + EPSILON)
    return centre * scale, scale


def normalize_pull(normed, scale, gain, grad):
    wide = grad * gain
    return scale * (
        wide
        - jnp.mean(wide, -1, keepdims=True)
        - normed * jnp.mean(wide * normed, -1, keepdims=True)
    )


def gelu_pair(v):
    c0 = 0.7978845608028654
    inner = c0 * (v + 0.044715 * v * v * v)
    t = jnp.tanh(inner)
    act = 0.5 * v * (1.0 + t)
    slope = 0.5 * (1.0 + t) + 0.5 * v * (1.0 - t * t) * (c0 * (1.0 + 3 * 0.044715 * v * v))
    return act, slope


def visible(doc_row, pad_row):
    total_rows = doc_row.shape[0]
    query_pos = jnp.arange(total_rows)[:, None]
    key_pos = jnp.arange(total_rows)[None, :]
    same_doc = doc_row[:, None] == doc_row[None, :]
    is_real = (pad_row[None, :] == 1) | (query_pos == key_pos)
    return (key_pos <= query_pos) & same_doc & is_real


def masked_scores(queries, key_rows, allowed):
    scores = jnp.einsum("qhd,khd->hqk", queries, key_rows, preferred_element_type=F32)
    return jnp.where(allowed[None], scores * HEAD_DIM**-0.5, MASKED)


def attend_forward(queries, key_rows, value_rows, allowed):
    scores = masked_scores(queries, key_rows, allowed)
    row_peak = jnp.max(scores, -1, keepdims=True)
    exponent = jnp.exp(scores - row_peak)
    row_total = jnp.sum(exponent, -1, keepdims=True)
    weights = (exponent / row_total).astype(BF)
    output = jnp.einsum("hqk,khd->qhd", weights, value_rows, preferred_element_type=F32)
    return output, row_peak + jnp.log(row_total)


def attend_backward(queries, key_rows, value_rows, allowed, log_total, heads_grad):
    scale = HEAD_DIM**-0.5
    scores = masked_scores(queries, key_rows, allowed)
    weights = jnp.exp(scores - log_total)
    weight_grad = jnp.einsum("qhd,khd->hqk", heads_grad, value_rows, preferred_element_type=F32)
    row_delta = jnp.sum(weights * weight_grad, -1, keepdims=True)
    score_grad = (weights * (weight_grad - row_delta)).astype(BF)
    query_grad = scale * jnp.einsum("hqk,khd->qhd", score_grad, key_rows, preferred_element_type=F32)
    key_grad = scale * jnp.einsum("hqk,qhd->khd", score_grad, queries, preferred_element_type=F32)
    value_grad = jnp.einsum(
        "hqk,qhd->khd", weights.astype(BF), heads_grad, preferred_element_type=F32
    )
    return query_grad, key_grad, value_grad


def make_shards(ne, nh):
    def to_experts(blocks):
        return lax.all_to_all(blocks, "expert", split_axis=0, concat_axis=0, tiled=True)

    def reduce_quarters(rows):
        blocks = rows.reshape(nh, -1, rows.shape[-1])
        bit = 1
        while bit < nh:
            keep = [r for r in range(blocks.shape[0]) if r % 2 == 0]
            send = [r for r in range(blocks.shape[0]) if r % 2 == 1]
            got = swap(jnp.concatenate([blocks[r] for r in send], 0), "hidden", bit)
            blocks = (
                jnp.stack([blocks[r] for r in keep]).astype(F32)
                + got.reshape(len(keep), -1, rows.shape[-1]).astype(F32)
            ).astype(BF)
            bit *= 2
        return blocks[0]

    def gather_quarters(rows):
        bit = nh // 2
        while bit >= 1:
            rows = jnp.concatenate([rows, swap(rows, "hidden", bit)], 0)
            bit //= 2
        return rows

    def quarter_order():
        order = [0]
        bit = nh // 2
        while bit >= 1:
            order = order + [r ^ bit for r in order]
            bit //= 2
        return order

    def sum_hidden(rows):
        h = lax.axis_index("hidden")
        count = rows.shape[0] // 2
        flag = h % 2
        kept = lax.dynamic_slice_in_dim(rows, flag * count, count, 0)
        sent = lax.dynamic_slice_in_dim(rows, (1 - flag) * count, count, 0)
        kept = (kept.astype(F32) + swap(sent, "hidden", 1).astype(F32)).astype(BF)
        bit = 2
        while bit < nh:
            kept = (kept.astype(F32) + swap(kept, "hidden", bit).astype(F32)).astype(BF)
            bit *= 2
        return ordered(flag, kept, swap(kept, "hidden", 1))

    def shards(
        tokens,
        doc_ids,
        pad_mask,
        norm1_gain,
        norm1_bias,
        qkv_weight,
        out_weight,
        norm2_gain,
        norm2_bias,
        router,
        routes,
        up_weight,
        down_weight,
        cotangent,
    ):
        micro_count, row_count, width = tokens.shape
        expert_count = router.shape[1]
        top_count = routes.shape[2]
        pack_cap = 2 * row_count * top_count // expert_count
        quarter = row_count // nh
        cap = round_up((pack_cap + (nh - 1) * (expert_count - 1)) // nh, 8)
        local_heads = qkv_weight.shape[2] // HEAD_DIM
        e_idx = lax.axis_index("expert")
        h_idx = lax.axis_index("hidden")
        micros = range(micro_count)

        ups, downs = [up_weight[0]], [down_weight[0]]
        bit = nh // 2
        while bit >= 1:
            pair = jnp.stack(ups + downs)
            got = swap(pair, "hidden", bit)
            ups = ups + [got[i] for i in range(len(ups))]
            downs = downs + [got[len(downs) + i] for i in range(len(downs))]
            bit //= 2
        slice_order = quarter_order()
        ups = [ups[slice_order.index(r)] for r in range(nh)]
        downs = [downs[slice_order.index(r)] for r in range(nh)]
        up_all = jnp.concatenate(ups, 1)
        down_all = jnp.concatenate(downs, 1)

        perms, places, tables = [], [], []
        for m in micros:
            low = jnp.min(routes[m], -1)
            high = jnp.max(routes[m], -1)
            key = (low * expert_count + high) * row_count + jnp.arange(row_count, dtype=jnp.int32)
            rank = jnp.sum((key[:, None] < key[None, :]).astype(jnp.int32), 0)
            targets = jnp.concatenate(
                [jnp.arange(quarter, dtype=jnp.int32) * nh + (h_idx ^ r) for r in range(nh)]
            )
            perm = (targets[:, None] == rank[None, :]).astype(BF)
            perms.append(perm)
            mine = jnp.dot(perm[:quarter], routes[m].astype(BF), preferred_element_type=F32)
            first, second = mine[:, 0], mine[:, 1]
            names = jnp.arange(expert_count, dtype=F32)[:, None]
            member = (first[None, :] == names) | (second[None, :] == names)
            before = (
                jnp.arange(quarter)[:, None] < jnp.arange(quarter)[None, :]
            ).astype(BF)
            place = jnp.dot(member.astype(BF), before, preferred_element_type=F32)
            slot = jnp.arange(cap, dtype=F32)[None, :, None]
            table = (slot == place[:, None, :]) & member[:, None, :]
            tables.append(table.astype(BF))
            others = (first + second)[None, :] - names
            places.append((member, others))

        def dispatch(m, rows):
            return jnp.einsum("ejt,td->ejd", tables[m], rows, preferred_element_type=F32).astype(BF)

        upstream_mine, upstream_slots, other_slots = [], [], []
        for m in micros:
            up_rows = jnp.dot(perms[m][:quarter], cotangent[m], preferred_element_type=F32)
            upstream_mine.append(up_rows)
            other = jnp.sum(tables[m].astype(F32) * places[m][1][:, None, :], -1)
            other_row = jnp.pad(
                other[:, None, :], ((0, 0), (0, EXTRA - 1), (0, width - cap))
            ).astype(BF)
            sent = jnp.concatenate([dispatch(m, up_rows.astype(BF)), other_row], 1)
            got = to_experts(sent)
            upstream_slots.append(got[:, :cap].reshape(-1, width))
            other_slots.append(got[:, cap, :cap].astype(F32).reshape(-1, 1))

        state = []
        for m in micros:
            inputs = tokens[m].astype(F32)
            allowed = visible(doc_ids[m, 0], pad_mask[m])
            normed1, scale1 = normalize(inputs)
            attn_in = (normed1 * norm1_gain + norm1_bias).astype(BF)
            projected = jnp.einsum(
                "rd,cdf->crf", attn_in, qkv_weight, preferred_element_type=F32
            ).astype(BF)
            heads = projected.reshape(3, row_count, local_heads, HEAD_DIM)
            heads_out, log_total = attend_forward(heads[0], heads[1], heads[2], allowed)
            heads_low = heads_out.reshape(row_count, -1).astype(BF)
            heads_sorted = jnp.dot(perms[m], heads_low, preferred_element_type=F32).astype(BF)
            term = jnp.dot(heads_sorted, out_weight, preferred_element_type=F32).astype(BF)
            attention = reduce_quarters(term).astype(F32)
            inputs_mine = jnp.dot(perms[m][:quarter], tokens[m], preferred_element_type=F32)
            residual = inputs_mine + attention
            normed2, scale2 = normalize(residual)
            moe_in = (normed2 * norm2_gain + norm2_bias).astype(BF)
            logits = jnp.dot(moe_in, router, preferred_element_type=F32).T
            member = places[m][0]
            masked = jnp.where(member, logits, MASKED)
            raised = jnp.where(member, jnp.exp(masked - jnp.max(masked, 0, keepdims=True)), 0.0)
            gates = raised / jnp.sum(raised, 0, keepdims=True)
            received = to_experts(dispatch(m, moe_in)).reshape(-1, width)
            state.append(
                dict(
                    inputs=inputs,
                    allowed=allowed,
                    normed1=normed1,
                    scale1=scale1,
                    attn_in=attn_in,
                    heads=heads,
                    log_total=log_total,
                    heads_sorted=heads_sorted,
                    attention=attention,
                    normed2=normed2,
                    scale2=scale2,
                    moe_in=moe_in,
                    gates=gates,
                    received=received,
                )
            )

        ordinals = jnp.arange(expert_count, dtype=F32)[None, :]
        for m in micros:
            s = state[m]
            rows = s["received"]
            logits = jnp.dot(rows, router, preferred_element_type=F32)
            picks = (ordinals == e_idx.astype(F32)).astype(F32) - (
                ordinals == other_slots[m]
            ).astype(F32)
            gate = jax.nn.sigmoid(jnp.sum(logits * picks, -1, keepdims=True))
            grad_rows = (gate * upstream_slots[m].astype(F32)).astype(BF)
            hidden_pre = jnp.dot(rows, up_all, preferred_element_type=F32)
            act, slope = gelu_pair(hidden_pre)
            hidden_act = act.astype(BF)
            expert_out = jnp.einsum(
                "rf,df->rd", hidden_act, down_all, preferred_element_type=F32
            ).astype(BF)
            act_grad = jnp.dot(grad_rows, down_all, preferred_element_type=F32)
            pre_grad = (act_grad * slope).astype(BF)
            copies = jnp.einsum("rf,df->rd", pre_grad, up_all, preferred_element_type=F32).astype(BF)
            gate_grad = jnp.sum(upstream_slots[m].astype(F32) * expert_out.astype(F32), -1)
            gate_grad = gate_grad.reshape(expert_count, 1, cap)
            coarse = gate_grad.astype(BF)
            fine = (gate_grad - coarse.astype(F32)).astype(BF)
            extra = jnp.pad(
                jnp.concatenate([coarse, fine], 1), ((0, 0), (0, EXTRA - 2), (0, width - cap))
            )
            sent = jnp.concatenate([copies.reshape(expert_count, cap, width), extra], 1)
            s["copies_back"] = to_experts(sent)
            s["out_back"] = to_experts(expert_out.reshape(expert_count, cap, width))
            s["grad_rows"] = grad_rows
            s["hidden_act"] = hidden_act
            s["pre_grad"] = pre_grad

        grad_up = sum(
            jnp.einsum("rd,rf->df", s["received"], s["pre_grad"], preferred_element_type=F32)
            for s in state
        )
        grad_down = sum(
            jnp.einsum("rd,rf->df", s["grad_rows"], s["hidden_act"], preferred_element_type=F32)
            for s in state
        )
        part = jnp.concatenate([grad_up, grad_down], 0).astype(BF)
        part = part.reshape(2 * width, nh, -1).transpose(1, 0, 2).reshape(nh * 2 * width, -1)
        own = reduce_quarters(part)
        own = own.reshape(2, ne, width // ne, -1).transpose(1, 0, 2, 3)
        parts = to_experts(own)[ne // 2 :].astype(F32)

        grad_router = 0.0
        gain2_total, bias2_total = 0.0, 0.0
        for m in micros:
            s = state[m]
            back = s["copies_back"]
            table = tables[m]
            copies_sum = jnp.einsum("ejt,ejd->td", table, back[:, :cap], preferred_element_type=F32)
            slot_grad = back[:, cap, :cap].astype(F32) + back[:, cap + 1, :cap].astype(F32)
            gate_grad = jnp.sum(table.astype(F32) * slot_grad[:, :, None], 1)
            gates = s["gates"]
            logit_grad = gates * (gate_grad - jnp.sum(gates * gate_grad, 0, keepdims=True))
            normed2_grad = copies_sum + jnp.einsum(
                "et,de->td", logit_grad, router.astype(F32), precision=PRECISE
            )
            grad_router = grad_router + jnp.einsum(
                "et,td->ed", logit_grad, s["moe_in"].astype(F32), precision=PRECISE
            )
            gain2_total = gain2_total + jnp.sum(normed2_grad * s["normed2"], 0)
            bias2_total = bias2_total + jnp.sum(normed2_grad, 0)
            resid_grad = upstream_mine[m] + normalize_pull(
                s["normed2"], s["scale2"], norm2_gain, normed2_grad
            )
            s["resid_all"] = gather_quarters(resid_grad.astype(BF))
            weighted = (table.astype(F32) * gates[:, None, :]).astype(BF)
            mixture = jnp.einsum("ejt,ejd->td", weighted, s["out_back"], preferred_element_type=F32)
            s["delta_all"] = gather_quarters((s["attention"] + mixture).astype(BF))

        small = jnp.concatenate([gain2_total[None], bias2_total[None], grad_router], 0)
        small_rows = round_up(small.shape[0], 16)
        small = jnp.pad(small, ((0, small_rows - small.shape[0]), (0, 0))).astype(BF)

        order = quarter_order()
        grad_qkv, grad_proj = 0.0, 0.0
        gain1_total, bias1_total = 0.0, 0.0
        outputs, input_grads = [], []
        for m in micros:
            s = state[m]
            perm = perms[m].reshape(nh, quarter, row_count)
            perm_all = jnp.concatenate([perm[r] for r in order], 0)
            heads_sorted = s["heads_sorted"].reshape(nh, quarter, -1)
            heads_sorted = jnp.concatenate([heads_sorted[r] for r in order], 0)
            resid_all = s["resid_all"]
            grad_proj = grad_proj + jnp.einsum(
                "rf,rd->fd", heads_sorted, resid_all, preferred_element_type=F32
            )
            heads_grad = jnp.einsum(
                "rd,fd->rf", resid_all, out_weight, preferred_element_type=F32
            ).astype(BF)
            heads_grad = jnp.einsum(
                "rt,rf->tf", perm_all, heads_grad, preferred_element_type=F32
            ).astype(BF)
            heads = s["heads"]
            grads = attend_backward(
                heads[0],
                heads[1],
                heads[2],
                s["allowed"],
                s["log_total"],
                heads_grad.reshape(row_count, local_heads, HEAD_DIM),
            )
            qkv_grad = jnp.stack(grads).reshape(3, row_count, -1).astype(BF)
            grad_qkv = grad_qkv + jnp.einsum(
                "rd,crf->cdf", s["attn_in"], qkv_grad, preferred_element_type=F32
            )
            term = jnp.einsum(
                "crf,cdf->rd", qkv_grad, qkv_weight, preferred_element_type=F32
            ).astype(BF)
            if m == micro_count - 1:
                total = sum_hidden(jnp.concatenate([term, small], 0))
                small_sum = total[row_count:]
                normed1_grad = total[:row_count].astype(F32)
            else:
                normed1_grad = sum_hidden(term).astype(F32)
            gain1_total = gain1_total + jnp.sum(normed1_grad * s["normed1"], 0)
            bias1_total = bias1_total + jnp.sum(normed1_grad, 0)
            resid_grad = jnp.einsum("rt,rd->td", perm_all, resid_all, preferred_element_type=F32)
            input_grads.append(
                resid_grad + normalize_pull(s["normed1"], s["scale1"], norm1_gain, normed1_grad)
            )
            delta = jnp.einsum("rt,rd->td", perm_all, s["delta_all"], preferred_element_type=F32)
            outputs.append(s["inputs"] + delta)

        flat = jnp.concatenate([grad_qkv.reshape(-1), grad_proj.reshape(-1)]).astype(BF)
        flat = flat.reshape(ne, -1, width)
        share = jnp.sum(to_experts(flat).astype(F32), 0).astype(BF)
        share_rows = share.shape[0]
        extra = jnp.concatenate([gain1_total[None], bias1_total[None]], 0).astype(BF)
        extra = jnp.concatenate([extra, small_sum], 0)
        extra = jnp.pad(extra, ((0, round_up(extra.shape[0], 16) - extra.shape[0]), (0, 0)))
        gathered = jnp.concatenate([share, extra], 0)[None]
        bit = ne // 2
        while bit >= 1:
            gathered = jnp.concatenate([gathered, swap(gathered, "expert", bit)], 0)
            bit //= 2
        bits = []
        bit = ne // 2
        found = [0]
        while bit >= 1:
            found = found + [r ^ bit for r in found]
            bit //= 2
        sums = jnp.sum(gathered[:, share_rows:].astype(F32), 0)
        where = jnp.zeros((ne,), jnp.int32)
        slots = jnp.array([found.index(r) for r in range(ne)], jnp.int32)
        where = slots[jnp.arange(ne, dtype=jnp.int32) ^ e_idx]
        flat = gathered[:, :share_rows][where].astype(F32).reshape(-1)
        split = grad_qkv.size
        return (
            jnp.stack(outputs),
            jnp.stack(input_grads),
            sums[0],
            sums[1],
            flat[:split].reshape(grad_qkv.shape),
            flat[split:].reshape(grad_proj.shape),
            sums[2],
            sums[3],
            sums[4 : 4 + expert_count].T,
            parts[:, 0],
            parts[:, 1],
        )

    return shards


def solution(mesh):
    placed = (
        P(None, "expert", None),
        P(None, "expert", None),
        P(None, "expert"),
        P(),
        P(),
        P(None, None, "hidden"),
        P("hidden", None),
        P(),
        P(),
        P(),
        P(None, "expert", None),
        P("expert", None, "hidden"),
        P("expert", None, "hidden"),
        P(None, "expert", None),
    )
    return jax.shard_map(
        make_shards(mesh.shape["expert"], mesh.shape["hidden"]),
        mesh=mesh,
        in_specs=placed,
        out_specs=(
            P(None, "expert", None),
            P(None, "expert", None),
            P(),
            P(),
            P(None, None, "hidden"),
            P("hidden", None),
            P(),
            P(),
            P(),
            P(None, "expert", "hidden"),
            P(None, "expert", "hidden"),
        ),
        check_vma=False,
    )
```

time: 1670 us -> 757 us (0.45)
  waiting for transfers between devices: 693 us -> 267 us
  blocking collectives: 397 us -> 0 us
  local copies, waits for them, and re-layouts: 221 us -> 81.3 us
  matrix products: 120 us -> 227 us
  other arithmetic: 160 us -> 97.6 us
    all_to_all x4 -> x0, blocking collectives: 358 us -> none  [the longest x2 215 us: shards(): lax.all_to_all(in_summed.reshape(expert_count, capacity, feat_width), 'ex...]
    psum x5 -> x0, waiting for transfers between devices: 313 us -> none  [the longest x1 209 us: shards(): summed = lax.psum(slice_out.astype(jnp.bfloat16), 'hidden')]
    all_to_all x6 -> x10, waiting for transfers between devices: 380 us -> 108 us  [to_experts(): lax.all_to_all(blocks, 'expert', split_axis=0, concat_axis=0, tiled=True)]
    ppermute x0 -> x25, waiting for transfers between devices: none -> 159 us  [swap(): return lax.ppermute(values, axis, [(i, i ^ bit) for i in range(size)])]
    dot_general x34 -> x62, matrix products: 109 us -> 209 us  [the longest x2 27.7 us: shards(): act_grad = jnp.dot(grad_rows, down_all, preferred_element_type=F32)]
    gather x8 -> x2, local copies, waits for them, and re-layouts: 96.8 us -> 2.02 us  [the longest x1 1.27 us: shards(): where = slots[jnp.arange(ne, dtype=jnp.int32) ^ e_idx]]
    reduce_sum x22 -> x18, other arithmetic: 68.7 us -> 18.9 us  [the longest x2 3.33 us: shards(): gate_grad = jnp.sum(table.astype(F32) * slot_grad[:, :, None], 1)]
    psum x1 -> x0, blocking collectives: 38.8 us -> none  [shards(): lax.psum(gain1_total.astype(jnp.bfloat16), 'expert').astype(jnp.float32)]
  transfers between devices with their start and end apart: 11 -> 35, of which waited for: 11 -> 16; matrix products, arithmetic and copies ran while one was open for 15% -> 31% of each run, Pallas kernels for 0% -> 0%
where the time goes in v1:
time: 757 us; the launch traced here: 751 us
  waiting for transfers between devices  267 us (35%)
  matrix products  227 us (30%)
  other arithmetic  97.6 us (13%)
  local copies, waits for them, and re-layouts  81.3 us (11%)
  starting transfers between devices  73.7 us (10%)
    ppermute x25, waiting for transfers between devices, swap(): return lax.ppermute(values, axis, [(i, i ^ bit) for i in range(size)])  159 us
    all_to_all x10, waiting for transfers between devices, to_experts(): lax.all_to_all(blocks, 'expert', split_axis=0, concat_axis=0, tiled=True)  108 us
    all_to_all x10, starting transfers between devices, to_experts(): lax.all_to_all(blocks, 'expert', split_axis=0, concat_axis=0, tiled=True)  53.3 us
    dot_general x2, matrix products, shards(): act_grad = jnp.dot(grad_rows, down_all, preferred_element_type=F32)  27.7 us
    unnamed x475, local copies, waits for them, and re-layouts  25.5 us
    dot_general x2, matrix products, shards(): jnp.einsum('rf,df->rd', hidden_act, down_all, preferred_element_type=F32)  23.1 us
    dot_general x2, matrix products, shards(): jnp.einsum('rd,rf->df', s['grad_rows'], s['hidden_act'], preferred_elemen...  22.3 us
    ppermute x25, starting transfers between devices, swap(): return lax.ppermute(values, axis, [(i, i ^ bit) for i in range(size)])  20.4 us
  transfers between devices with their start and end apart: 35, of which 16 were waited for; matrix products, arithmetic and copies ran while one was open for 31% of the time, Pallas kernels for 0%

profile of v1, /device:TPU:0, one launch (start us, length us, event | category | flops | bytes accessed | tf_op | source)
XLA Modules:
  0.0 750.6 jit_solution(14671671766929429689)
XLA Ops:
  37.1 21.5 %collective-permute-done.2 = bf16[2,768,768]{2,1,0:T(8,128)(2,1)} collective-permute-done((bf16[2,768,768]{2,1,0:T(8,128)(2,1)}, bf16[2,768,768]{2,1,0:T(8,128)(2,1)}, u32[]{:S(2)}, u32[]{:S(2)}) %collective-permute-start.2) | collective-permute-done | bytes 2359328 | tf_op jit(solution)/shard_map/ppermute | solution.py:21
  66.4 7.7 %collective-permute-done.1 = bf16[192,768]{1,0:T(8,128)(2,1)S(1)} collective-permute-done((bf16[192,768]{1,0:T(8,128)(2,1)S(1)}, bf16[192,768]{1,0:T(8,128)(2,1)S(1)}, u32[]{:S(2)}, u32[]{:S(2)}) %collective-permute-start.1) | collective-permute-done | bytes 294944 | tf_op jit(solution)/shard_map/ppermute | solution.py:21
  91.9 24.9 %all-to-all-done = bf16[8,104,768]{2,1,0:T(8,128)(2,1)} async-done(((bf16[8,104,768]{2,1,0:T(8,128)(2,1)}), bf16[8,104,768]{2,1,0:T(8,128)(2,1)}, u32[]{:S(2)}, u32[]{:S(2)}) %all-to-all-start) | async-done | bytes 1277984 | tf_op jit(solution)/shard_map/all_to_all | solution.py:96
  122.2 9.4 %fusion.287 = f32[832,3072]{1,0:T(8,128)} fusion(bf16[832,768]{1,0:T(8,128)(2,1)} %bitcast.22, bf16[768,768]{1,0:T(8,128)(2,1)S(1)} %get-tuple-element.85, bf16[768,768]{1,0:T(8,128)(2,1)S(1)} %copy-done.70, bf16[768,768]{1,0:T(8,128)(2,1)S(1)} %get-tuple-element.86, bf16[768,768]{1,0:T(8,128)(2,1)S(1)} %bitcast.335), kind=kOutput, calls=%fused_computation.502 | convolution fusion | flops 3944742912 | bytes 16220160 | tf_op jit(solution)/shard_map/dot_general | solution.py:276
  131.6 11.5 %fusion.47 = (f32[832]{0:T(1024)}, bf16[832,768]{1,0:T(8,128)(2,1)}) fusion(bf16[832,768]{1,0:T(8,128)(2,1)S(1)} %bitcast.350, bf16[768,768]{1,0:T(8,128)(2,1)S(1)} %get-tuple-element.84, bf16[768,768]{1,0:T(8,128)(2,1)S(1)} %copy-done.73, bf16[768,768]{1,0:T(8,128)(2,1)S(1)} %get-tuple-element.83, bf16[768,768]{1,0:T(8,128)(2,1)S(1)} %bitcast.331, ...), kind=kOutput, calls=%fused_computation.95 | convolution fusion | flops 3970940160 | bytes 17501440 | tf_op jit(solution)/shard_map/rf,df->rd/dot_general | solution.py:279
  145.3 14.5 %fusion.9 = bf16[832,3072]{1,0:T(8,128)(2,1)S(1)} fusion(f32[832,3072]{1,0:T(8,128)} %fusion.287, bf16[832,768]{1,0:T(8,128)(2,1)} %bitcast.349, f32[832]{0:T(1024)} %add_divide_fusion.1, bf16[768,768]{1,0:T(8,128)(2,1)} %copy-done.65, bf16[768,768]{1,0:T(8,128)(2,1)} %get-tuple-element.89, bf16[768,768]{1,0:T(8,128)(2,1)} %copy-done.63, ...), kind=kOutput, calls=%fused_computation.15 | convolution fusion | flops 3995222016 | bytes 21335296 | tf_op jit(solution)/shard_map/dot_general | solution.py:282
  174.7 27.5 %all-to-all-done.5 = bf16[8,112,768]{2,1,0:T(8,128)(2,1)} async-done(((bf16[8,112,768]{2,1,0:T(8,128)(2,1)}), bf16[8,112,768]{2,1,0:T(8,128)(2,1)}, u32[]{:S(2)}, u32[]{:S(2)}) %all-to-all-start.5) | async-done | bytes 1376288 | tf_op jit(solution)/shard_map/all_to_all | solution.py:96
  229.9 7.4 multiply_reduce_fusion.1
  288.2 10.2 %all-to-all-done.6 = bf16[8,112,768]{2,1,0:T(8,128)(2,1)} async-done(((bf16[8,112,768]{2,1,0:T(8,128)(2,1)}), bf16[8,112,768]{2,1,0:T(8,128)(2,1)}, u32[]{:S(2)}, u32[]{:S(2)}) %all-to-all-start.6) | async-done | bytes 1376288 | tf_op jit(solution)/shard_map/all_to_all | solution.py:96
  316.7 16.3 %all-to-all-done.1 = bf16[8,104,768]{2,1,0:T(8,128)(2,1)} async-done(((bf16[8,104,768]{2,1,0:T(8,128)(2,1)}), bf16[8,104,768]{2,1,0:T(8,128)(2,1)}, u32[]{:S(2)}, u32[]{:S(2)}) %all-to-all-start.1) | async-done | bytes 1277984 | tf_op jit(solution)/shard_map/all_to_all | solution.py:96
  339.6 10.5 %fusion.170 = f32[768,3072]{1,0:T(8,128)} fusion(bf16[832,768]{1,0:T(8,128)(2,1)S(1)} %bitcast.351, f32[832]{0:T(1024)S(1)} %copy-done.219, f32[832,3072]{1,0:T(8,128)} %fusion.287), kind=kOutput, calls=%fused_computation.309 | convolution fusion | flops 3950788608 | bytes 20942080 | tf_op jit(solution)/shard_map/rd,rf->df/dot_general | solution.py:304
  361.2 9.8 %fusion.307 = f32[768,3072]{1,0:T(8,128)} fusion(bf16[832,768]{1,0:T(8,128)(2,1)} %bitcast.22, bf16[832,3072]{1,0:T(8,128)(2,1)} %copy-done.14), kind=kOutput, calls=%fused_computation.520 | convolution fusion | flops 3925868544 | bytes 15826944 | tf_op jit(solution)/shard_map/rd,rf->df/dot_general | solution.py:300
  380.9 11.8 %all-to-all-done.2 = bf16[8,104,768]{2,1,0:T(8,128)(2,1)} async-done(((bf16[8,104,768]{2,1,0:T(8,128)(2,1)}), bf16[8,104,768]{2,1,0:T(8,128)(2,1)}, u32[]{:S(2)}, u32[]{:S(2)}) %all-to-all-start.2) | async-done | bytes 1277984 | tf_op jit(solution)/shard_map/all_to_all | solution.py:96
  392.8 10.9 %fusion.286 = f32[832,3072]{1,0:T(8,128)} fusion(bf16[832,768]{1,0:T(8,128)(2,1)} %bitcast.56, bf16[768,768]{1,0:T(8,128)(2,1)} %copy-done.57, bf16[768,768]{1,0:T(8,128)(2,1)} %get-tuple-element.90, bf16[768,768]{1,0:T(8,128)(2,1)} %copy-done.60, bf16[768,768]{1,0:T(8,128)(2,1)} %bitcast.334), kind=kOutput, calls=%fused_computation.501 | convolution fusion | flops 3944742912 | bytes 16220160 | tf_op jit(solution)/shard_map/dot_general | solution.py:276
  405.5 11.6 %fusion.49 = (f32[832]{0:T(1024)}, bf16[832,768]{1,0:T(8,128)(2,1)}) fusion(bf16[832,768]{1,0:T(8,128)(2,1)S(1)} %bitcast.354, bf16[768,768]{1,0:T(8,128)(2,1)S(1)} %copy-done.66, bf16[768,768]{1,0:T(8,128)(2,1)S(1)} %copy-done.74, bf16[768,768]{1,0:T(8,128)(2,1)S(1)} %copy-done.64, bf16[768,768]{1,0:T(8,128)(2,1)S(1)} %bitcast.332, f32[832,3072]{1,0:T(8,128)} %fusion.286), kind=kOutput, calls=%fused_computation.97 | convolution fusion | flops 3970940160 | bytes 17501440 | tf_op jit(solution)/shard_map/rf,df->rd/dot_general | solution.py:279
  417.1 13.3 %fusion.15 = bf16[832,3072]{1,0:T(8,128)(2,1)S(1)} fusion(f32[832,3072]{1,0:T(8,128)} %fusion.286, bf16[832,768]{1,0:T(8,128)(2,1)S(1)} %bitcast.355, f32[832]{0:T(1024)S(1)} %add_divide_fusion, bf16[768,768]{1,0:T(8,128)(2,1)S(1)} %copy-done.66, bf16[768,768]{1,0:T(8,128)(2,1)S(1)} %copy-done.74, bf16[768,768]{1,0:T(8,128)(2,1)S(1)} %copy-done.64, ...), kind=kOutput, calls=%fused_computation.21 | convolution fusion | flops 3995222016 | bytes 21335296 | tf_op jit(solution)/shard_map/dot_general | solution.py:282
  430.3 11.8 %add_convert_fusion = bf16[768,3072]{1,0:T(8,128)(2,1)S(1)} fusion(f32[768,3072]{1,0:T(8,128)} %fusion.170, bf16[832,768]{1,0:T(8,128)(2,1)S(1)} %bitcast.356, f32[832]{0:T(1024)S(1)} %add_divide_fusion, f32[832,3072]{1,0:T(8,128)} %fusion.286), kind=kOutput, calls=%fused_computation.27 | convolution fusion | flops 3955507200 | bytes 25660672 | tf_op jit(solution)/shard_map/rd,rf->df/dot_general | solution.py:304
  460.3 8.8 %add_convert_fusion.1 = bf16[768,3072]{1,0:T(8,128)(2,1)S(1)} fusion(f32[768,3072]{1,0:T(8,128)} %fusion.307, bf16[832,768]{1,0:T(8,128)(2,1)} %bitcast.56, bf16[832,3072]{1,0:T(8,128)(2,1)} %copy-done.15), kind=kOutput, calls=%fused_computation.28 | convolution fusion | flops 3930587136 | bytes 20545536 | tf_op jit(solution)/shard_map/rd,rf->df/dot_general | solution.py:300
  475.9 17.3 %all-to-all-done.7 = bf16[8,112,768]{2,1,0:T(8,128)(2,1)} async-done(((bf16[8,112,768]{2,1,0:T(8,128)(2,1)}), bf16[8,112,768]{2,1,0:T(8,128)(2,1)}, u32[]{:S(2)}, u32[]{:S(2)}) %all-to-all-start.7) | async-done | bytes 1376288 | tf_op jit(solution)/shard_map/all_to_all | solution.py:96
  525.2 7.6 %multiply_reduce_fusion = (f32[3,768]{1,0:T(4,128)S(1)}, f32[3,768,768]{1,2,0:T(8,128)}) fusion(f32[3,768,768]{1,2,0:T(8,128)} %copy-done.2, f32[3,768]{1,0:T(4,128)S(1)} %copy-done.126, bf16[768,3,64]{0,2,1:T(8,128)(2,1)} %bitcast.359, bf16[768,3,64]{0,2,1:T(8,128)(2,1)} %bitcast.364), kind=kOutput, calls=%fused_computation.30 | convolution fusion | flops 231798528 | bytes 14764032 | tf_op jit(solution)/shard_map/qhd,khd->hqk/dot_general | solution.py:83
  579.7 53.8 %collective-permute-done.8 = bf16[192,768]{1,0:T(8,128)(2,1)S(1)} collective-permute-done((bf16[192,768]{1,0:T(8,128)(2,1)S(1)}, bf16[192,768]{1,0:T(8,128)(2,1)S(1)}, u32[]{:S(2)}, u32[]{:S(2)}) %collective-permute-start.8) | collective-permute-done | bytes 294944 | tf_op jit(solution)/shard_map/ppermute | solution.py:21
  671.5 37.8 %collective-permute-done.20 = bf16[1,128,768]{2,1,0:T(8,128)(2,1)S(1)} collective-permute-done((bf16[1,128,768]{2,1,0:T(8,128)(2,1)S(1)}, bf16[1,128,768]{2,1,0:T(8,128)(2,1)S(1)}, u32[]{:S(2)}, u32[]{:S(2)}) %collective-permute-start.20) | collective-permute-done | bytes 196640 | tf_op jit(solution)/shard_map/ppermute | solution.py:21
  709.4 9.9 %collective-permute-done.21 = bf16[2,128,768]{2,1,0:T(8,128)(2,1)S(1)} collective-permute-done((bf16[2,128,768]{2,1,0:T(8,128)(2,1)S(1)}, bf16[2,128,768]{2,1,0:T(8,128)(2,1)S(1)}, u32[]{:S(2)}, u32[]{:S(2)}) %collective-permute-start.21) | collective-permute-done | bytes 393248 | tf_op jit(solution)/shard_map/ppermute | solution.py:21
  725.3 11.8 %collective-permute-done.22 = bf16[4,128,768]{2,1,0:T(8,128)(2,1)S(1)} collective-permute-done((bf16[4,128,768]{2,1,0:T(8,128)(2,1)S(1)}, bf16[4,128,768]{2,1,0:T(8,128)(2,1)S(1)}, u32[]{:S(2)}, u32[]{:S(2)}) %collective-permute-start.22) | collective-permute-done | bytes 786464 | tf_op jit(solution)/shard_map/ppermute | solution.py:21
  (749 shorter events, 369.2 us)
Async XLA Ops:
  4.0 54.5 %collective-permute-start.2 = (bf16[2,768,768]{2,1,0:T(8,128)(2,1)}, bf16[2,768,768]{2,1,0:T(8,128)(2,1)}, u32[]{:S(2)}, u32[]{:S(2)}) collective-permute-start(bf16[2,768,768]{2,1,0:T(8,128)(2,1)} %pad_maximum_fusion.6), channel_id=1, source_target_pairs={{0,2},{1,3},{2,0},{3,1},{4,6},{5,7},{6,4},{7,5},{8,10},{9,11},{10,... | collective-permute-start | bytes 7077896 | tf_op jit(solution)/shard_map/ppermute | solution.py:21
  17.2 62.2 %all-to-all-start.4 = ((bf16[8,112,768]{2,1,0:T(8,128)(2,1)}), bf16[8,112,768]{2,1,0:T(8,128)(2,1)}, u32[]{:S(2)}, u32[]{:S(2)}) async-start(bf16[8,112,768]{2,1,0:T(8,128)(2,1)} %fusion.76), calls=%async_computation.4 | async-start | bytes 2752512 | tf_op jit(solution)/shard_map/all_to_all | solution.py:96
  37.0 27.4 %collective-permute-start = (bf16[384,768]{1,0:T(8,128)(2,1)S(1)}, bf16[384,768]{1,0:T(8,128)(2,1)S(1)}, u32[]{:S(2)}, u32[]{:S(2)}) collective-permute-start(bf16[384,768]{1,0:T(8,128)(2,1)S(1)} %pad_maximum_fusion.20), channel_id=1, source_target_pairs={{0,1},{1,0},{2,3},{3,2},{4,5},{5,4},{6,7},{7,6},{8,9},{9,8},{10,11... | collective-permute-start | bytes 1769480 | tf_op jit(solution)/shard_map/ppermute | solution.py:21
  64.4 54.8 %collective-permute-start.3 = (bf16[4,768,768]{2,1,0:T(8,128)(2,1)}, bf16[4,768,768]{2,1,0:T(8,128)(2,1)}, u32[]{:S(2)}, u32[]{:S(2)}) collective-permute-start(bf16[4,768,768]{2,1,0:T(8,128)(2,1)} %pad_maximum_fusion), channel_id=1, source_target_pairs={{0,1},{1,0},{2,3},{3,2},{4,5},{5,4},{6,7},{7,6},{8,9},{9,8},{10,11... | collective-permute-start | bytes 14155784 | tf_op jit(solution)/shard_map/ppermute | solution.py:21
  79.4 37.3 %all-to-all-start = ((bf16[8,104,768]{2,1,0:T(8,128)(2,1)}), bf16[8,104,768]{2,1,0:T(8,128)(2,1)}, u32[]{:S(2)}, u32[]{:S(2)}) async-start(bf16[8,104,768]{2,1,0:T(8,128)(2,1)} %convolution_convert_fusion.7), calls=%async_computation | async-start | bytes 2555904 | tf_op jit(solution)/shard_map/all_to_all | solution.py:96
  165.2 37.0 %all-to-all-start.5 = ((bf16[8,112,768]{2,1,0:T(8,128)(2,1)}), bf16[8,112,768]{2,1,0:T(8,128)(2,1)}, u32[]{:S(2)}, u32[]{:S(2)}) async-start(bf16[8,112,768]{2,1,0:T(8,128)(2,1)} %pad_maximum_fusion.7), calls=%async_computation.5 | async-start | bytes 2752512 | tf_op jit(solution)/shard_map/all_to_all | solution.py:96
  259.9 38.5 %all-to-all-start.6 = ((bf16[8,112,768]{2,1,0:T(8,128)(2,1)}), bf16[8,112,768]{2,1,0:T(8,128)(2,1)}, u32[]{:S(2)}, u32[]{:S(2)}) async-start(bf16[8,112,768]{2,1,0:T(8,128)(2,1)} %fusion.77), calls=%async_computation.6 | async-start | bytes 2752512 | tf_op jit(solution)/shard_map/all_to_all | solution.py:96
  298.4 34.6 %all-to-all-start.1 = ((bf16[8,104,768]{2,1,0:T(8,128)(2,1)}), bf16[8,104,768]{2,1,0:T(8,128)(2,1)}, u32[]{:S(2)}, u32[]{:S(2)}) async-start(bf16[8,104,768]{2,1,0:T(8,128)(2,1)} %bitcast.352), calls=%async_computation.1 | async-start | bytes 2555904 | tf_op jit(solution)/shard_map/all_to_all | solution.py:96
  310.8 26.0 %collective-permute-start.6 = (bf16[384,768]{1,0:T(8,128)(2,1)}, bf16[384,768]{1,0:T(8,128)(2,1)}, u32[]{:S(2)}, u32[]{:S(2)}) collective-permute-start(bf16[384,768]{1,0:T(8,128)(2,1)} %pad_maximum_fusion.22), channel_id=1, source_target_pairs={{0,1},{1,0},{2,3},{3,2},{4,5},{5,4},{6,7},{7,6},{8,9},{9,8},{10,11... | collective-permute-start | bytes 1769480 | tf_op jit(solution)/shard_map/ppermute | solution.py:21
  351.0 23.3 %collective-permute-start.5 = (bf16[384,768]{1,0:T(8,128)(2,1)}, bf16[384,768]{1,0:T(8,128)(2,1)}, u32[]{:S(2)}, u32[]{:S(2)}) collective-permute-start(bf16[384,768]{1,0:T(8,128)(2,1)} %pad_maximum_fusion.21), channel_id=1, source_target_pairs={{0,1},{1,0},{2,3},{3,2},{4,5},{5,4},{6,7},{7,6},{8,9},{9,8},{10,11... | collective-permute-start | bytes 1769480 | tf_op jit(solution)/shard_map/ppermute | solution.py:21
  356.8 35.9 %all-to-all-start.2 = ((bf16[8,104,768]{2,1,0:T(8,128)(2,1)}), bf16[8,104,768]{2,1,0:T(8,128)(2,1)}, u32[]{:S(2)}, u32[]{:S(2)}) async-start(bf16[8,104,768]{2,1,0:T(8,128)(2,1)} %convolution_convert_fusion.5), calls=%async_computation.2 | async-start | bytes 2555904 | tf_op jit(solution)/shard_map/all_to_all | solution.py:96
  456.1 37.2 %all-to-all-start.7 = ((bf16[8,112,768]{2,1,0:T(8,128)(2,1)}), bf16[8,112,768]{2,1,0:T(8,128)(2,1)}, u32[]{:S(2)}, u32[]{:S(2)}) async-start(bf16[8,112,768]{2,1,0:T(8,128)(2,1)} %pad_maximum_fusion.8), calls=%async_computation.7 | async-start | bytes 2752512 | tf_op jit(solution)/shard_map/all_to_all | solution.py:96
  493.2 73.3 %all-to-all-start.3 = ((bf16[8,104,768]{2,1,0:T(8,128)(2,1)}), bf16[8,104,768]{2,1,0:T(8,128)(2,1)}, u32[]{:S(2)}, u32[]{:S(2)}) async-start(bf16[8,104,768]{2,1,0:T(8,128)(2,1)} %bitcast.353), calls=%async_computation.3 | async-start | bytes 2555904 | tf_op jit(solution)/shard_map/all_to_all | solution.py:96
  507.9 45.1 %collective-permute-start.23 = (bf16[3072,768]{1,0:T(8,128)(2,1)}, bf16[3072,768]{1,0:T(8,128)(2,1)}, u32[]{:S(2)}, u32[]{:S(2)}) collective-permute-start(bf16[3072,768]{1,0:T(8,128)(2,1)} %pad_maximum_fusion.5), channel_id=1, source_target_pairs={{0,1},{1,0},{2,3},{3,2},{4,5},{5,4},{6,7},{7,6},{8,9},{9,8},{10,11... | collective-permute-start | bytes 14155784 | tf_op jit(solution)/shard_map/ppermute | solution.py:21
  552.9 19.8 %collective-permute-start.17 = (bf16[392,768]{1,0:T(8,128)(2,1)}, bf16[392,768]{1,0:T(8,128)(2,1)}, u32[]{:S(2)}, u32[]{:S(2)}) collective-permute-start(bf16[392,768]{1,0:T(8,128)(2,1)} %fusion.164), channel_id=1, source_target_pairs={{0,1},{1,0},{2,3},{3,2},{4,5},{5,4},{6,7},{7,6},{8,9},{9,8},{10,11... | collective-permute-start | bytes 1806344 | tf_op jit(solution)/shard_map/ppermute | solution.py:21
  560.6 75.4 %collective-permute-start.24 = (bf16[1536,768]{1,0:T(8,128)(2,1)}, bf16[1536,768]{1,0:T(8,128)(2,1)}, u32[]{:S(2)}, u32[]{:S(2)}) collective-permute-start(bf16[1536,768]{1,0:T(8,128)(2,1)} %slice_bitcast_fusion), channel_id=1, source_target_pairs={{0,2},{1,3},{2,0},{3,1},{4,6},{5,7},{6,4},{7,5},{8,10},{9,11},{10,... | collective-permute-start | bytes 7077896 | tf_op jit(solution)/shard_map/ppermute | solution.py:21
  566.5 74.0 %all-to-all-start.8 = ((bf16[8,96,768]{2,1,0:T(8,128)(2,1)}), bf16[8,96,768]{2,1,0:T(8,128)(2,1)}, u32[]{:S(2)}, u32[]{:S(2)}) async-start(bf16[8,96,768]{2,1,0:T(8,128)(2,1)} %convert_element_type.659), calls=%async_computation.8 | async-start | bytes 2359296 | tf_op jit(solution)/shard_map/all_to_all | solution.py:96
  574.4 60.0 %collective-permute-start.18 = (bf16[392,768]{1,0:T(8,128)(2,1)S(1)}, bf16[392,768]{1,0:T(8,128)(2,1)S(1)}, u32[]{:S(2)}, u32[]{:S(2)}) collective-permute-start(bf16[392,768]{1,0:T(8,128)(2,1)S(1)} %add_convert_fusion.4), channel_id=1, source_target_pairs={{0,2},{1,3},{2,0},{3,1},{4,6},{5,7},{6,4},{7,5},{8,10},{9,11},{10,... | collective-permute-start | bytes 1806344 | tf_op jit(solution)/shard_map/ppermute | solution.py:21
  577.5 56.0 %collective-permute-start.8 = (bf16[192,768]{1,0:T(8,128)(2,1)S(1)}, bf16[192,768]{1,0:T(8,128)(2,1)S(1)}, u32[]{:S(2)}, u32[]{:S(2)}) collective-permute-start(bf16[192,768]{1,0:T(8,128)(2,1)S(1)} %fusion.96), channel_id=1, source_target_pairs={{0,2},{1,3},{2,0},{3,1},{4,6},{5,7},{6,4},{7,5},{8,10},{9,11},{10,... | collective-permute-start | bytes 884744 | tf_op jit(solution)/shard_map/ppermute | solution.py:21
  634.4 18.1 %collective-permute-start.9 = (bf16[384,768]{1,0:T(8,128)(2,1)}, bf16[384,768]{1,0:T(8,128)(2,1)}, u32[]{:S(2)}, u32[]{:S(2)}) collective-permute-start(bf16[384,768]{1,0:T(8,128)(2,1)} %pad_maximum_fusion.23), channel_id=1, source_target_pairs={{0,1},{1,0},{2,3},{3,2},{4,5},{5,4},{6,7},{7,6},{8,9},{9,8},{10,11... | collective-permute-start | bytes 1769480 | tf_op jit(solution)/shard_map/ppermute | solution.py:21
  635.4 20.8 %collective-permute-start.19 = (bf16[392,768]{1,0:T(8,128)(2,1)}, bf16[392,768]{1,0:T(8,128)(2,1)}, u32[]{:S(2)}, u32[]{:S(2)}) collective-permute-start(bf16[392,768]{1,0:T(8,128)(2,1)} %add_convert_fusion.3), channel_id=1, source_target_pairs={{0,1},{1,0},{2,3},{3,2},{4,5},{5,4},{6,7},{7,6},{8,9},{9,8},{10,11... | collective-permute-start | bytes 1806344 | tf_op jit(solution)/shard_map/ppermute | solution.py:21
  640.5 106.8 %all-to-all-start.9 = ((bf16[8,2,96,768]{3,2,1,0:T(8,128)(2,1)}), bf16[8,2,96,768]{3,2,1,0:T(8,128)(2,1)}, u32[]{:S(2)}, u32[]{:S(2)}) async-start(bf16[8,2,96,768]{3,2,1,0:T(8,128)(2,1)} %bitcast.329), calls=%async_computation.9 | async-start | bytes 4718592 | tf_op jit(solution)/shard_map/all_to_all | solution.py:96
  663.5 45.8 %collective-permute-start.20 = (bf16[1,128,768]{2,1,0:T(8,128)(2,1)S(1)}, bf16[1,128,768]{2,1,0:T(8,128)(2,1)S(1)}, u32[]{:S(2)}, u32[]{:S(2)}) collective-permute-start(bf16[1,128,768]{2,1,0:T(8,128)(2,1)S(1)} %maximum_bitcast_fusion.1), channel_id=1, source_target_pairs={{0,16},{4,20},{8,24},{12,28},{16,0},{20,4},{24,8},{28,12},{1,17},{... | collective-permute-start | bytes 589832 | tf_op jit(solution)/shard_map/ppermute | solution.py:21
  719.4 17.7 %collective-permute-start.22 = (bf16[4,128,768]{2,1,0:T(8,128)(2,1)S(1)}, bf16[4,128,768]{2,1,0:T(8,128)(2,1)S(1)}, u32[]{:S(2)}, u32[]{:S(2)}) collective-permute-start(bf16[4,128,768]{2,1,0:T(8,128)(2,1)S(1)} %pad_maximum_fusion.19), channel_id=1, source_target_pairs={{0,4},{4,0},{8,12},{12,8},{16,20},{20,16},{24,28},{28,24},{1,5},{5... | collective-permute-start | bytes 2359304 | tf_op jit(solution)/shard_map/ppermute | solution.py:21
  (248 other events, 2091.0 us)

commit v2 on v1

--- a/solution.py
+++ b/solution.py
@@ -1,13 +1,15 @@
 import jax
 import jax.numpy as jnp
 from jax import lax
+from jax.experimental import pallas as pl
+from jax.experimental.pallas import tpu as pltpu
 from jax.sharding import PartitionSpec as P
 
 HEAD_DIM = 64
 EPSILON = 1e-05
 PRECISE = lax.Precision.HIGHEST
 MASKED = -1e30
-EXTRA = 8
+TILE = 16
 BF = jnp.bfloat16
 F32 = jnp.float32
 
@@ -50,6 +52,161 @@
     act = 0.5 * v * (1.0 + t)
     slope = 0.5 * (1.0 + t) + 0.5 * v * (1.0 - t * t) * (c0 * (1.0 + 3 * 0.044715 * v * v))
     return act, slope
+
+
+def after(values, *others):
+    return lax.optimization_barrier((values, others))[0]
+
+
+def diagonal(count):
+    return lax.broadcasted_iota(jnp.int32, (count, count), 0) == lax.broadcasted_iota(
+        jnp.int32, (count, count), 1
+    )
+
+
+def expert_body(slices, packs, cap, width, aliased):
+    rows_n = packs * cap
+
+    def body(own_ref, rows_ref, cot_ref, router_ref, *refs):
+        ups, downs = refs[:slices], refs[slices : 2 * slices]
+        refs = refs[2 * slices + (4 if aliased else 0) :]
+        (out_ref, copies_ref, rows_all, grads_all, act_all, pre_all) = refs[:6]
+        up_v, down_v, grad_rows, acc_out, acc_copies, sems = refs[6:]
+        i, s = pl.program_id(0), pl.program_id(1)
+
+        def fetch(r):
+            return (
+                pltpu.make_async_copy(ups[r], up_v.at[r], sems.at[0, r]),
+                pltpu.make_async_copy(downs[r], down_v.at[r], sems.at[1, r]),
+            )
+
+        @pl.when((i == 0) & (s == 0))
+        def _():
+            for r in range(slices):
+                for copy in fetch(r):
+                    copy.start()
+
+        for r in range(slices):
+
+            @pl.when((i == 0) & (s == r))
+            def _():
+                for copy in fetch(r):
+                    copy.wait()
+
+        @pl.when(s == 0)
+        def _():
+            rows = rows_ref[...].reshape(rows_n, width)
+            rows_all[...] = rows
+            logits = jnp.dot(rows, router_ref[...], preferred_element_type=F32)
+            ordinals = lax.broadcasted_iota(jnp.int32, logits.shape, 1).astype(F32)
+            eye = diagonal(cap)
+            other = []
+            for p in range(packs):
+                line = cot_ref[p, cap - TILE :, :][TILE - 1 :, :cap].astype(F32)
+                other.append(jnp.sum(jnp.where(eye, line, 0.0), 1, keepdims=True))
+            other = jnp.concatenate(other, 0)
+            own = own_ref[0].astype(F32)
+            picks = jnp.where(ordinals == own, 1.0, 0.0) - jnp.where(ordinals == other, 1.0, 0.0)
+            gate = jax.nn.sigmoid(jnp.sum(logits * picks, -1, keepdims=True))
+            cot = cot_ref[...].reshape(rows_n, width).astype(F32)
+            low = (gate * cot).astype(BF)
+            grad_rows[...] = low
+            grads_all[...] = low
+
+        up, down = up_v[s], down_v[s]
+        pre = jnp.dot(rows_ref[...].reshape(rows_n, width), up, preferred_element_type=F32)
+        act_grad = jnp.dot(grad_rows[...], down, preferred_element_type=F32)
+        act, slope = gelu_pair(pre)
+        act = act.astype(BF)
+        act_all[...] = act
+        pre_grad = (act_grad * slope).astype(BF)
+        pre_all[...] = pre_grad
+        along = (((1,), (1,)), ((), ()))
+        out = lax.dot_general(act, down, along, preferred_element_type=F32)
+        copies = lax.dot_general(pre_grad, up, along, preferred_element_type=F32)
+
+        @pl.when(s == 0)
+        def _():
+            acc_out[...] = out
+            acc_copies[...] = copies
+
+        @pl.when(s > 0)
+        def _():
+            acc_out[...] += out
+            acc_copies[...] += copies
+
+        @pl.when(s == slices - 1)
+        def _():
+            low = acc_out[...].astype(BF)
+            out_ref[...] = low.reshape(packs, cap, width)
+            copies_ref[...] = acc_copies[...].astype(BF).reshape(packs, cap, width)
+            cot = cot_ref[...].reshape(rows_n, width).astype(F32)
+            gate_grad = jnp.sum(cot * low.astype(F32), -1, keepdims=True)
+            eye = diagonal(cap)
+            index = lax.broadcasted_iota(jnp.int32, (TILE, width), 0)
+            for p in range(packs):
+                column = gate_grad[p * cap : (p + 1) * cap]
+                line = jnp.sum(jnp.where(eye, column, 0.0), 0, keepdims=True)
+                line = jnp.concatenate([line, jnp.zeros((1, width - cap), F32)], 1)
+                coarse = line.astype(BF).astype(F32)
+                tail = copies_ref[p, cap - TILE :, :].astype(F32)
+                tail = jnp.where(index == TILE - 1, coarse, tail)
+                tail = jnp.where(index == TILE - 2, line - coarse, tail)
+                copies_ref[p, cap - TILE :, :] = tail.astype(BF)
+
+    return body
+
+
+def run_expert(own, rows, cot, router, ups, downs, held, m, micro_count):
+    blocks, cap, width = rows.shape
+    slices = len(ups)
+    hidden = ups[0].shape[1]
+    packs = max(p for p in range(1, blocks + 1) if blocks % p == 0 and p * cap <= 448)
+    steps = blocks // packs
+    total = micro_count * blocks * cap
+    aliased = held is not None
+    rows_n = packs * cap
+    block = pl.BlockSpec((packs, cap, width), lambda i, s: (i, 0, 0))
+    any_spec = pl.BlockSpec(memory_space=pl.ANY)
+    whole_rows = pl.BlockSpec((rows_n, width), lambda i, s: (m * steps + i, 0))
+    whole_hidden = pl.BlockSpec((rows_n, hidden), lambda i, s: (m * steps + i, s))
+    inputs = [own, rows, cot, router, *ups, *downs]
+    in_specs = [
+        pl.BlockSpec(memory_space=pltpu.SMEM),
+        block,
+        block,
+        pl.BlockSpec(router.shape, lambda i, s: (0, 0)),
+    ] + [any_spec] * (2 * slices)
+    aliases = {}
+    if aliased:
+        aliases = {len(inputs) + k: 2 + k for k in range(4)}
+        inputs += list(held)
+        in_specs += [any_spec] * 4
+    return pl.pallas_call(
+        expert_body(slices, packs, cap, width, aliased),
+        grid=(steps, slices),
+        in_specs=in_specs,
+        out_specs=[block, block, whole_rows, whole_rows, whole_hidden, whole_hidden],
+        out_shape=[
+            jax.ShapeDtypeStruct((blocks, cap, width), BF),
+            jax.ShapeDtypeStruct((blocks, cap, width), BF),
+            jax.ShapeDtypeStruct((total, width), BF),
+            jax.ShapeDtypeStruct((total, width), BF),
+            jax.ShapeDtypeStruct((total, slices * hidden), BF),
+            jax.ShapeDtypeStruct((total, slices * hidden), BF),
+        ],
+        scratch_shapes=[
+            pltpu.VMEM((slices,) + ups[0].shape, BF),
+            pltpu.VMEM((slices,) + downs[0].shape, BF),
+            pltpu.VMEM((rows_n, width), BF),
+            pltpu.VMEM((rows_n, width), F32),
+            pltpu.VMEM((rows_n, width), F32),
+            pltpu.SemaphoreType.DMA((2, slices)),
+        ],
+        input_output_aliases=aliases,
+        compiler_params=pltpu.CompilerParams(vmem_limit_bytes=48 * 1024 * 1024),
+        name="expert",
+    )(*inputs)
 
 
 def visible(doc_row, pad_row):
@@ -158,25 +315,22 @@
         top_count = routes.shape[2]
         pack_cap = 2 * row_count * top_count // expert_count
         quarter = row_count // nh
-        cap = round_up((pack_cap + (nh - 1) * (expert_count - 1)) // nh, 8)
+        cap = round_up((pack_cap + (nh - 1) * (expert_count - 1)) // nh + 2, TILE)
         local_heads = qkv_weight.shape[2] // HEAD_DIM
         e_idx = lax.axis_index("expert")
         h_idx = lax.axis_index("hidden")
         micros = range(micro_count)
 
+        slice_order = quarter_order()
         ups, downs = [up_weight[0]], [down_weight[0]]
         bit = nh // 2
         while bit >= 1:
-            pair = jnp.stack(ups + downs)
-            got = swap(pair, "hidden", bit)
-            ups = ups + [got[i] for i in range(len(ups))]
-            downs = downs + [got[len(downs) + i] for i in range(len(downs))]
+            got_up = [swap(x, "hidden", bit) for x in ups]
+            got_down = [swap(x, "hidden", bit) for x in downs]
+            ups, downs = ups + got_up, downs + got_down
             bit //= 2
-        slice_order = quarter_order()
         ups = [ups[slice_order.index(r)] for r in range(nh)]
         downs = [downs[slice_order.index(r)] for r in range(nh)]
-        up_all = jnp.concatenate(ups, 1)
-        down_all = jnp.concatenate(downs, 1)
 
         perms, places, tables = [], [], []
         for m in micros:
@@ -206,18 +360,17 @@
         def dispatch(m, rows):
             return jnp.einsum("ejt,td->ejd", tables[m], rows, preferred_element_type=F32).astype(BF)
 
-        upstream_mine, upstream_slots, other_slots = [], [], []
+        upstream_mine, upstream_slots = [], []
         for m in micros:
             up_rows = jnp.dot(perms[m][:quarter], cotangent[m], preferred_element_type=F32)
             upstream_mine.append(up_rows)
             other = jnp.sum(tables[m].astype(F32) * places[m][1][:, None, :], -1)
-            other_row = jnp.pad(
-                other[:, None, :], ((0, 0), (0, EXTRA - 1), (0, width - cap))
-            ).astype(BF)
-            sent = jnp.concatenate([dispatch(m, up_rows.astype(BF)), other_row], 1)
-            got = to_experts(sent)
-            upstream_slots.append(got[:, :cap].reshape(-1, width))
-            other_slots.append(got[:, cap, :cap].astype(F32).reshape(-1, 1))
+            other = jnp.pad(other[:, None, :], ((0, 0), (0, 0), (0, width - cap)))
+            sent = jnp.einsum(
+                "ejt,td->ejd", tables[m], up_rows.astype(BF), preferred_element_type=F32
+            )
+            last = (jnp.arange(cap) == cap - 1)[None, :, None]
+            upstream_slots.append(to_experts(jnp.where(last, other, sent).astype(BF)))
 
         state = []
         for m in micros:
@@ -243,7 +396,7 @@
             masked = jnp.where(member, logits, MASKED)
             raised = jnp.where(member, jnp.exp(masked - jnp.max(masked, 0, keepdims=True)), 0.0)
             gates = raised / jnp.sum(raised, 0, keepdims=True)
-            received = to_experts(dispatch(m, moe_in)).reshape(-1, width)
+            received = to_experts(dispatch(m, moe_in))
             state.append(
                 dict(
                     inputs=inputs,
@@ -263,52 +416,47 @@
                 )
             )
 
-        ordinals = jnp.arange(expert_count, dtype=F32)[None, :]
+        own_expert = jnp.full((1,), e_idx, jnp.int32)
+        held = None
         for m in micros:
             s = state[m]
-            rows = s["received"]
-            logits = jnp.dot(rows, router, preferred_element_type=F32)
-            picks = (ordinals == e_idx.astype(F32)).astype(F32) - (
-                ordinals == other_slots[m]
-            ).astype(F32)
-            gate = jax.nn.sigmoid(jnp.sum(logits * picks, -1, keepdims=True))
-            grad_rows = (gate * upstream_slots[m].astype(F32)).astype(BF)
-            hidden_pre = jnp.dot(rows, up_all, preferred_element_type=F32)
-            act, slope = gelu_pair(hidden_pre)
-            hidden_act = act.astype(BF)
-            expert_out = jnp.einsum(
-                "rf,df->rd", hidden_act, down_all, preferred_element_type=F32
-            ).astype(BF)
-            act_grad = jnp.dot(grad_rows, down_all, preferred_element_type=F32)
-            pre_grad = (act_grad * slope).astype(BF)
-            copies = jnp.einsum("rf,df->rd", pre_grad, up_all, preferred_element_type=F32).astype(BF)
-            gate_grad = jnp.sum(upstream_slots[m].astype(F32) * expert_out.astype(F32), -1)
-            gate_grad = gate_grad.reshape(expert_count, 1, cap)
-            coarse = gate_grad.astype(BF)
-            fine = (gate_grad - coarse.astype(F32)).astype(BF)
-            extra = jnp.pad(
-                jnp.concatenate([coarse, fine], 1), ((0, 0), (0, EXTRA - 2), (0, width - cap))
-            )
-            sent = jnp.concatenate([copies.reshape(expert_count, cap, width), extra], 1)
-            s["copies_back"] = to_experts(sent)
-            s["out_back"] = to_experts(expert_out.reshape(expert_count, cap, width))
-            s["grad_rows"] = grad_rows
-            s["hidden_act"] = hidden_act
-            s["pre_grad"] = pre_grad
-
-        grad_up = sum(
-            jnp.einsum("rd,rf->df", s["received"], s["pre_grad"], preferred_element_type=F32)
-            for s in state
-        )
-        grad_down = sum(
-            jnp.einsum("rd,rf->df", s["grad_rows"], s["hidden_act"], preferred_element_type=F32)
-            for s in state
-        )
-        part = jnp.concatenate([grad_up, grad_down], 0).astype(BF)
-        part = part.reshape(2 * width, nh, -1).transpose(1, 0, 2).reshape(nh * 2 * width, -1)
-        own = reduce_quarters(part)
-        own = own.reshape(2, ne, width // ne, -1).transpose(1, 0, 2, 3)
-        parts = to_experts(own)[ne // 2 :].astype(F32)
+            out, copies, *held = run_expert(
+                own_expert,
+                s["received"],
+                upstream_slots[m],
+                router,
+                ups,
+                downs,
+                held,
+                m,
+                micro_count,
+            )
+            s["copies_back"] = to_experts(copies)
+            s["out_back"] = to_experts(out)
+
+        rows_all, grads_all, act_all, pre_all = held
+        parts = []
+        for left, right in ((rows_all, pre_all), (grads_all, act_all)):
+            hidden = right.shape[1] // nh
+            slabs = [
+                jnp.einsum(
+                    "rd,rf->df",
+                    left,
+                    right[:, r * hidden : (r + 1) * hidden],
+                    preferred_element_type=F32,
+                ).astype(BF)
+                for r in range(nh)
+            ]
+            bit = 1
+            while bit < nh:
+                got = [swap(slab, "hidden", bit) for slab in slabs[1::2]]
+                slabs = [
+                    (mine.astype(F32) + other.astype(F32)).astype(BF)
+                    for mine, other in zip(slabs[0::2], got)
+                ]
+                bit *= 2
+            rows = to_experts(slabs[0].reshape(ne, width // ne, -1))
+            parts.append(rows[ne // 2 :].astype(F32))
 
         grad_router = 0.0
         gain2_total, bias2_total = 0.0, 0.0
@@ -316,8 +464,8 @@
             s = state[m]
             back = s["copies_back"]
             table = tables[m]
-            copies_sum = jnp.einsum("ejt,ejd->td", table, back[:, :cap], preferred_element_type=F32)
-            slot_grad = back[:, cap, :cap].astype(F32) + back[:, cap + 1, :cap].astype(F32)
+            copies_sum = jnp.einsum("ejt,ejd->td", table, back, preferred_element_type=F32)
+            slot_grad = back[:, cap - 1, :cap].astype(F32) + back[:, cap - 2, :cap].astype(F32)
             gate_grad = jnp.sum(table.astype(F32) * slot_grad[:, :, None], 1)
             gates = s["gates"]
             logit_grad = gates * (gate_grad - jnp.sum(gates * gate_grad, 0, keepdims=True))
@@ -393,8 +541,16 @@
             outputs.append(s["inputs"] + delta)
 
         flat = jnp.concatenate([grad_qkv.reshape(-1), grad_proj.reshape(-1)]).astype(BF)
-        flat = flat.reshape(ne, -1, width)
-        share = jnp.sum(to_experts(flat).astype(F32), 0).astype(BF)
+        share = flat.reshape(ne, -1, width)
+        bit = 1
+        while bit < ne:
+            flag = (e_idx // bit) % 2
+            pairs = share.reshape(share.shape[0] // 2, 2, -1, width)
+            kept = lax.dynamic_index_in_dim(pairs, flag, 1, False)
+            sent = lax.dynamic_index_in_dim(pairs, 1 - flag, 1, False)
+            share = (kept.astype(F32) + swap(sent, "expert", bit).astype(F32)).astype(BF)
+            bit *= 2
+        share = share[0]
         share_rows = share.shape[0]
         extra = jnp.concatenate([gain1_total[None], bias1_total[None]], 0).astype(BF)
         extra = jnp.concatenate([extra, small_sum], 0)
@@ -426,8 +582,8 @@
             sums[2],
             sums[3],
             sums[4 : 4 + expert_count].T,
-            parts[:, 0],
-            parts[:, 1],
+            parts[0],
+            parts[1],
         )
 
     return shards

time: 757 us -> 669 us (0.88)
  matrix products: 227 us -> 134 us
  Pallas kernels: 0 us -> 55.1 us
  local copies, waits for them, and re-layouts: 81.3 us -> 44.2 us
  other arithmetic: 97.6 us -> 76.4 us
    dot_general x16 -> x12, matrix products: 130 us -> 46.4 us  [the longest x8 36.4 us: shards(): jnp.einsum('rd,rf->df', left, right[:, r * hidden:(r + 1) * hidden], pref...]
    pallas_call x0 -> x2, Pallas kernels: none -> 55.1 us  [run_expert(): pl.pallas_call(expert_body(slices, packs, cap, width, aliased), grid=(ste...]
    unnamed x475 -> x368, local copies, waits for them, and re-layouts: 25.5 us -> 15.1 us
    ppermute x25 -> x36, starting transfers between devices: 20.4 us -> 28.5 us  [swap(): return lax.ppermute(values, axis, [(i, i ^ bit) for i in range(size)])]
    ppermute x25 -> x36, waiting for transfers between devices: 159 us -> 154 us  [swap(): return lax.ppermute(values, axis, [(i, i ^ bit) for i in range(size)])]
  transfers between devices with their start and end apart: 35 -> 46, of which waited for: 16 -> 23; matrix products, arithmetic and copies ran while one was open for 31% -> 25% of each run, Pallas kernels for 0% -> 0%
where the time goes in v2:
time: 669 us; the launch traced here: 659 us
  waiting for transfers between devices  267 us (40%)
  matrix products  134 us (20%)
  starting transfers between devices  78 us (12%)
  other arithmetic  76.4 us (11%)
  Pallas kernels  55.1 us (8%)
  local copies, waits for them, and re-layouts  44.2 us (7%)
    ppermute x36, waiting for transfers between devices, swap(): return lax.ppermute(values, axis, [(i, i ^ bit) for i in range(size)])  154 us
    all_to_all x10, waiting for transfers between devices, to_experts(): lax.all_to_all(blocks, 'expert', split_axis=0, concat_axis=0, tiled=True)  113 us
    pallas_call x2, Pallas kernels, run_expert(): pl.pallas_call(expert_body(slices, packs, cap, width, aliased), grid=(ste...  55.1 us
    all_to_all x10, starting transfers between devices, to_experts(): lax.all_to_all(blocks, 'expert', split_axis=0, concat_axis=0, tiled=True)  49.5 us
    dot_general x8, matrix products, shards(): jnp.einsum('rd,rf->df', left, right[:, r * hidden:(r + 1) * hidden], pref...  36.4 us
    ppermute x36, starting transfers between devices, swap(): return lax.ppermute(values, axis, [(i, i ^ bit) for i in range(size)])  28.5 us
    unnamed x368, local copies, waits for them, and re-layouts  15.1 us
    dot_general x2, matrix products, attend_backward(): jnp.einsum('qhd,khd->hqk', heads_grad, value_rows, preferred_element_type...  14.9 us
  transfers between devices with their start and end apart: 46, of which 23 were waited for; matrix products, arithmetic and copies ran while one was open for 25% of the time, Pallas kernels for 0%

profile of v2, /device:TPU:0, one launch (start us, length us, event | category | flops | bytes accessed | tf_op | source)
XLA Modules:
  0.0 658.8 jit_solution(11993373685431272024)
XLA Ops:
  30.1 7.2 %all-to-all-start.1 = ((bf16[8,112,768]{2,1,0:T(8,128)(2,1)}), bf16[8,112,768]{2,1,0:T(8,128)(2,1)}, u32[]{:S(2)}, u32[]{:S(2)}) async-start(bf16[8,112,768]{2,1,0:T(8,128)(2,1)} %select_convert_fusion.1), calls=%async_computation.1 | async-start | bytes 2752512 | tf_op jit(solution)/shard_map/all_to_all | solution.py:253
  40.2 7.7 %collective-permute-done.1 = bf16[192,768]{1,0:T(8,128)(2,1)S(1)} collective-permute-done((bf16[192,768]{1,0:T(8,128)(2,1)S(1)}, bf16[192,768]{1,0:T(8,128)(2,1)S(1)}, u32[]{:S(2)}, u32[]{:S(2)}) %collective-permute-start.1) | collective-permute-done | bytes 294944 | tf_op jit(solution)/shard_map/ppermute | solution.py:23
  53.4 17.4 %all-to-all-done.1.cot_ref = bf16[8,112,768]{2,1,0:T(8,128)(2,1)} async-done(((bf16[8,112,768]{2,1,0:T(8,128)(2,1)}), bf16[8,112,768]{2,1,0:T(8,128)(2,1)}, u32[]{:S(2)}, u32[]{:S(2)}) %all-to-all-start.1) | async-done | bytes 1376288 | tf_op jit(solution)/shard_map/all_to_all | solution.py:253
  77.7 26.4 %collective-permute-done.3.refs_2_ = bf16[768,768]{1,0:T(8,128)(2,1)} collective-permute-done((bf16[768,768]{1,0:T(8,128)(2,1)S(1)}, bf16[768,768]{1,0:T(8,128)(2,1)}, u32[]{:S(2)}, u32[]{:S(2)}) %collective-permute-start.3) | collective-permute-done | bytes 1179680 | tf_op jit(solution)/shard_map/ppermute | solution.py:23
  104.1 23.7 %collective-permute-done.6.refs_6_ = bf16[768,768]{1,0:T(8,128)(2,1)} collective-permute-done((bf16[768,768]{1,0:T(8,128)(2,1)S(1)}, bf16[768,768]{1,0:T(8,128)(2,1)}, u32[]{:S(2)}, u32[]{:S(2)}) %collective-permute-start.6) | collective-permute-done | bytes 1179680 | tf_op jit(solution)/shard_map/ppermute | solution.py:23
  131.0 27.4 %expert.2 = (bf16[8,112,768]{2,1,0:T(8,128)(2,1)}, bf16[8,112,768]{2,1,0:T(8,128)(2,1)}, bf16[1792,768]{1,0:T(8,128)(2,1)}, bf16[1792,768]{1,0:T(8,128)(2,1)}, b...) custom-call(s32[1]{0:T(128)} %bitcast.21.own_ref, bf16[8,112,768]{2,1,0:T(8,128)(2,1)} %all-to-all-done.rows_ref, ...), custom_call_target="tpu_custom_call" | custom-call | tf_op jit(solution)/shard_map/expert/pallas_call | solution.py:185
  166.8 30.3 %all-to-all-done.6 = bf16[8,112,768]{2,1,0:T(8,128)(2,1)} async-done(((bf16[8,112,768]{2,1,0:T(8,128)(2,1)}), bf16[8,112,768]{2,1,0:T(8,128)(2,1)}, u32[]{:S(2)}, u32[]{:S(2)}) %all-to-all-start.6) | async-done | bytes 1376288 | tf_op jit(solution)/shard_map/all_to_all | solution.py:253
  204.7 6.4 collective-permute-done.14
  218.3 7.5 %multiply_reduce_fusion.1 = (f32[3,768]{1,0:T(4,128)S(1)}, f32[3,768,768]{1,2,0:T(8,128)}) fusion(f32[3,768,768]{1,2,0:T(8,128)} %copy-done.5, f32[3,768]{1,0:T(4,128)S(1)} %log_add_fusion.1, bf16[768,3,64]{0,2,1:T(8,128)(2,1)} %bitcast.313, bf16[768,3,64]{0,2,1:T(8,128)(2,1)} %bitcast.319), kind=kOutput, calls=%fused_computation.6 | convolution fusion | flops 231798528 | bytes 14764032 | tf_op jit(solution)/shard_map/qhd,khd->hqk/dot_general | solution.py:240
  240.4 12.5 %collective-permute-done.17 = bf16[384,768]{1,0:T(8,128)(2,1)S(1)} collective-permute-done((bf16[384,768]{1,0:T(8,128)(2,1)S(1)}, bf16[384,768]{1,0:T(8,128)(2,1)S(1)}, u32[]{:S(2)}, u32[]{:S(2)}) %collective-permute-start.17) | collective-permute-done | bytes 589856 | tf_op jit(solution)/shard_map/ppermute | solution.py:23
  285.0 12.4 %all-to-all-done.2 = bf16[8,112,768]{2,1,0:T(8,128)(2,1)} async-done(((bf16[8,112,768]{2,1,0:T(8,128)(2,1)}), bf16[8,112,768]{2,1,0:T(8,128)(2,1)}, u32[]{:S(2)}, u32[]{:S(2)}) %all-to-all-start.2) | async-done | bytes 1376288 | tf_op jit(solution)/shard_map/all_to_all | solution.py:253
  324.9 9.4 %all-to-all-done.4.cot_ref = bf16[8,112,768]{2,1,0:T(8,128)(2,1)} async-done(((bf16[8,112,768]{2,1,0:T(8,128)(2,1)}), bf16[8,112,768]{2,1,0:T(8,128)(2,1)}, u32[]{:S(2)}, u32[]{:S(2)}) %all-to-all-start.4) | async-done | bytes 1376288 | tf_op jit(solution)/shard_map/all_to_all | solution.py:253
  352.8 18.4 %all-to-all-done.3.rows_ref = bf16[8,112,768]{2,1,0:T(8,128)(2,1)} async-done(((bf16[8,112,768]{2,1,0:T(8,128)(2,1)}), bf16[8,112,768]{2,1,0:T(8,128)(2,1)}, u32[]{:S(2)}, u32[]{:S(2)}) %all-to-all-start.3) | async-done | bytes 1376288 | tf_op jit(solution)/shard_map/all_to_all | solution.py:253
  371.2 27.8 %expert.3 = (bf16[8,112,768]{2,1,0:T(8,128)(2,1)}, bf16[8,112,768]{2,1,0:T(8,128)(2,1)}, bf16[1792,768]{1,0:T(8,128)(2,1)}, bf16[1792,768]{1,0:T(8,128)(2,1)}, b...) custom-call(s32[1]{0:T(128)} %bitcast.21.own_ref, ...), custom_call_target="tpu_custom_call", output_to_operand_aliasing={{2}: (12, {}), {3}: (13, {}), {4}: (14, {}), {5}: (15, {})} | custom-call | tf_op jit(solution)/shard_map/expert/pallas_call | solution.py:185
  398.9 6.1 fusion.80
  405.1 6.2 fusion.83
  445.3 19.4 %collective-permute-done.35 = bf16[768,768]{1,0:T(8,128)(2,1)S(1)} collective-permute-done((bf16[768,768]{1,0:T(8,128)(2,1)S(1)}, bf16[768,768]{1,0:T(8,128)(2,1)S(1)}, u32[]{:S(2)}, u32[]{:S(2)}) %collective-permute-start.35) | collective-permute-done | bytes 1179680 | tf_op jit(solution)/shard_map/ppermute | solution.py:23
  479.0 16.7 %collective-permute-done.19 = bf16[192,768]{1,0:T(8,128)(2,1)S(1)} collective-permute-done((bf16[192,768]{1,0:T(8,128)(2,1)S(1)}, bf16[192,768]{1,0:T(8,128)(2,1)S(1)}, u32[]{:S(2)}, u32[]{:S(2)}) %collective-permute-start.19) | collective-permute-done | bytes 294944 | tf_op jit(solution)/shard_map/ppermute | solution.py:23
  495.8 8.2 %all-to-all-done.5 = bf16[8,112,768]{2,1,0:T(8,128)(2,1)} async-done(((bf16[8,112,768]{2,1,0:T(8,128)(2,1)}), bf16[8,112,768]{2,1,0:T(8,128)(2,1)}, u32[]{:S(2)}, u32[]{:S(2)}) %all-to-all-start.5) | async-done | bytes 1376288 | tf_op jit(solution)/shard_map/all_to_all | solution.py:253
  517.2 7.4 %multiply_reduce_fusion = (f32[3,768]{1,0:T(4,128)S(1)}, f32[3,768,768]{1,2,0:T(8,128)}) fusion(f32[3,768,768]{1,2,0:T(8,128)} %copy-done.4, f32[3,768]{1,0:T(4,128)S(1)} %log_add_fusion, bf16[768,3,64]{0,2,1:T(8,128)(2,1)S(1)} %bitcast.315, bf16[768,3,64]{0,2,1:T(8,128)(2,1)S(1)} %bitcast.318), kind=kOutput, calls=%fused_computation.3 | convolution fusion | flops 231798528 | bytes 14764032 | tf_op jit(solution)/shard_map/qhd,khd->hqk/dot_general | solution.py:240
  562.3 6.7 %collective-permute-done.24 = bf16[4,96,768]{2,1,0:T(8,128)(2,1)S(1)} collective-permute-done((bf16[4,96,768]{2,1,0:T(8,128)(2,1)S(1)}, bf16[4,96,768]{2,1,0:T(8,128)(2,1)S(1)}, u32[]{:S(2)}, u32[]{:S(2)}) %collective-permute-start.24) | collective-permute-done | bytes 589856 | tf_op jit(solution)/shard_map/ppermute | solution.py:23
  599.1 17.3 %all-to-all-done.8 = bf16[8,96,768]{2,1,0:T(8,128)(2,1)} async-done(((bf16[8,96,768]{2,1,0:T(8,128)(2,1)}), bf16[8,96,768]{2,1,0:T(8,128)(2,1)}, u32[]{:S(2)}, u32[]{:S(2)}) %all-to-all-start.8) | async-done | bytes 1179680 | tf_op jit(solution)/shard_map/all_to_all | solution.py:253
  620.1 9.2 %collective-permute-done.28 = bf16[2,128,768]{2,1,0:T(8,128)(2,1)S(1)} collective-permute-done((bf16[2,128,768]{2,1,0:T(8,128)(2,1)S(1)}, bf16[2,128,768]{2,1,0:T(8,128)(2,1)S(1)}, u32[]{:S(2)}, u32[]{:S(2)}) %collective-permute-start.28) | collective-permute-done | bytes 393248 | tf_op jit(solution)/shard_map/ppermute | solution.py:23
  637.2 10.2 %collective-permute-done.29 = bf16[4,128,768]{2,1,0:T(8,128)(2,1)S(1)} collective-permute-done((bf16[4,128,768]{2,1,0:T(8,128)(2,1)S(1)}, bf16[4,128,768]{2,1,0:T(8,128)(2,1)S(1)}, u32[]{:S(2)}, u32[]{:S(2)}) %collective-permute-start.29) | collective-permute-done | bytes 786464 | tf_op jit(solution)/shard_map/ppermute | solution.py:23
  (638 shorter events, 313.3 us)
Async XLA Ops:
  30.1 40.7 %all-to-all-start.1 = ((bf16[8,112,768]{2,1,0:T(8,128)(2,1)}), bf16[8,112,768]{2,1,0:T(8,128)(2,1)}, u32[]{:S(2)}, u32[]{:S(2)}) async-start(bf16[8,112,768]{2,1,0:T(8,128)(2,1)} %select_convert_fusion.1), calls=%async_computation.1 | async-start | bytes 2752512 | tf_op jit(solution)/shard_map/all_to_all | solution.py:253
  70.8 60.2 %all-to-all-start = ((bf16[8,112,768]{2,1,0:T(8,128)(2,1)}), bf16[8,112,768]{2,1,0:T(8,128)(2,1)}, u32[]{:S(2)}, u32[]{:S(2)}) async-start(bf16[8,112,768]{2,1,0:T(8,128)(2,1)} %convolution_convert_fusion.1), calls=%async_computation | async-start | bytes 2752512 | tf_op jit(solution)/shard_map/all_to_all | solution.py:253
  75.1 29.0 %collective-permute-start.3 = (bf16[768,768]{1,0:T(8,128)(2,1)S(1)}, bf16[768,768]{1,0:T(8,128)(2,1)}, u32[]{:S(2)}, u32[]{:S(2)}) collective-permute-start(bf16[768,768]{1,0:T(8,128)(2,1)S(1)} %bitcast.286), channel_id=1, source_target_pairs={{0,2},{1,3},{2,0},{3,1},{4,6},{5,7},{6,4},{7,5},{8,10},{9,11},{10,... | collective-permute-start | bytes 3538952 | tf_op jit(solution)/shard_map/ppermute | solution.py:23
  76.6 51.1 %collective-permute-start.6 = (bf16[768,768]{1,0:T(8,128)(2,1)S(1)}, bf16[768,768]{1,0:T(8,128)(2,1)}, u32[]{:S(2)}, u32[]{:S(2)}) collective-permute-start(bf16[768,768]{1,0:T(8,128)(2,1)S(1)} %bitcast.290), channel_id=1, source_target_pairs={{0,2},{1,3},{2,0},{3,1},{4,6},{5,7},{6,4},{7,5},{8,10},{9,11},{10,... | collective-permute-start | bytes 3538952 | tf_op jit(solution)/shard_map/ppermute | solution.py:23
  77.2 50.8 %collective-permute-start.2 = (bf16[768,768]{1,0:T(8,128)(2,1)S(1)}, bf16[768,768]{1,0:T(8,128)(2,1)}, u32[]{:S(2)}, u32[]{:S(2)}) collective-permute-start(bf16[768,768]{1,0:T(8,128)(2,1)S(1)} %bitcast.287), channel_id=1, source_target_pairs={{0,1},{1,0},{2,3},{3,2},{4,5},{5,4},{6,7},{7,6},{8,9},{9,8},{10,11... | collective-permute-start | bytes 3538952 | tf_op jit(solution)/shard_map/ppermute | solution.py:23
  77.2 50.8 %collective-permute-start.5 = (bf16[768,768]{1,0:T(8,128)(2,1)S(1)}, bf16[768,768]{1,0:T(8,128)(2,1)}, u32[]{:S(2)}, u32[]{:S(2)}) collective-permute-start(bf16[768,768]{1,0:T(8,128)(2,1)S(1)} %bitcast.291), channel_id=1, source_target_pairs={{0,1},{1,0},{2,3},{3,2},{4,5},{5,4},{6,7},{7,6},{8,9},{9,8},{10,11... | collective-permute-start | bytes 3538952 | tf_op jit(solution)/shard_map/ppermute | solution.py:23
  104.1 23.9 %collective-permute-start.4 = (bf16[768,768]{1,0:T(8,128)(2,1)}, bf16[768,768]{1,0:T(8,128)(2,1)}, u32[]{:S(2)}, u32[]{:S(2)}) collective-permute-start(bf16[768,768]{1,0:T(8,128)(2,1)} %collective-permute-done.3.refs_2_), channel_id=1, source_target_pairs={{0,1},{1,0},{2,3},{3,2},{4,5},{5,4},{6,7},{7,6},{8,9},{9,8},{10,11... | collective-permute-start | bytes 3538952 | tf_op jit(solution)/shard_map/ppermute | solution.py:23
  158.4 38.8 %all-to-all-start.6 = ((bf16[8,112,768]{2,1,0:T(8,128)(2,1)}), bf16[8,112,768]{2,1,0:T(8,128)(2,1)}, u32[]{:S(2)}, u32[]{:S(2)}) async-start(bf16[8,112,768]{2,1,0:T(8,128)(2,1)} %get-tuple-element.29), calls=%async_computation.6 | async-start | bytes 2752512 | tf_op jit(solution)/shard_map/all_to_all | solution.py:253
  259.0 38.3 %all-to-all-start.2 = ((bf16[8,112,768]{2,1,0:T(8,128)(2,1)}), bf16[8,112,768]{2,1,0:T(8,128)(2,1)}, u32[]{:S(2)}, u32[]{:S(2)}) async-start(bf16[8,112,768]{2,1,0:T(8,128)(2,1)} %get-tuple-element.23), calls=%async_computation.2 | async-start | bytes 2752512 | tf_op jit(solution)/shard_map/all_to_all | solution.py:253
  280.9 25.5 %collective-permute-start.10 = (bf16[384,768]{1,0:T(8,128)(2,1)}, bf16[384,768]{1,0:T(8,128)(2,1)}, u32[]{:S(2)}, u32[]{:S(2)}) collective-permute-start(bf16[384,768]{1,0:T(8,128)(2,1)} %pad_maximum_fusion.15), channel_id=1, source_target_pairs={{0,1},{1,0},{2,3},{3,2},{4,5},{5,4},{6,7},{7,6},{8,9},{9,8},{10,11... | collective-permute-start | bytes 1769480 | tf_op jit(solution)/shard_map/ppermute | solution.py:23
  297.4 36.9 %all-to-all-start.4 = ((bf16[8,112,768]{2,1,0:T(8,128)(2,1)}), bf16[8,112,768]{2,1,0:T(8,128)(2,1)}, u32[]{:S(2)}, u32[]{:S(2)}) async-start(bf16[8,112,768]{2,1,0:T(8,128)(2,1)} %select_convert_fusion), calls=%async_computation.4 | async-start | bytes 2752512 | tf_op jit(solution)/shard_map/all_to_all | solution.py:253
  315.7 27.2 %collective-permute-start.9 = (bf16[384,768]{1,0:T(8,128)(2,1)}, bf16[384,768]{1,0:T(8,128)(2,1)}, u32[]{:S(2)}, u32[]{:S(2)}) collective-permute-start(bf16[384,768]{1,0:T(8,128)(2,1)} %pad_maximum_fusion.14), channel_id=1, source_target_pairs={{0,1},{1,0},{2,3},{3,2},{4,5},{5,4},{6,7},{7,6},{8,9},{9,8},{10,11... | collective-permute-start | bytes 1769480 | tf_op jit(solution)/shard_map/ppermute | solution.py:23
  334.3 36.9 %all-to-all-start.3 = ((bf16[8,112,768]{2,1,0:T(8,128)(2,1)}), bf16[8,112,768]{2,1,0:T(8,128)(2,1)}, u32[]{:S(2)}, u32[]{:S(2)}) async-start(bf16[8,112,768]{2,1,0:T(8,128)(2,1)} %convolution_convert_fusion), calls=%async_computation.3 | async-start | bytes 2752512 | tf_op jit(solution)/shard_map/all_to_all | solution.py:253
  418.2 48.1 %all-to-all-start.7 = ((bf16[8,112,768]{2,1,0:T(8,128)(2,1)}), bf16[8,112,768]{2,1,0:T(8,128)(2,1)S(1)}, u32[]{:S(2)}, u32[]{:S(2)}) async-start(bf16[8,112,768]{2,1,0:T(8,128)(2,1)} %get-tuple-element.30), calls=%async_computation.7 | async-start | bytes 2752512 | tf_op jit(solution)/shard_map/all_to_all | solution.py:253
  435.8 28.9 %collective-permute-start.35 = (bf16[768,768]{1,0:T(8,128)(2,1)S(1)}, bf16[768,768]{1,0:T(8,128)(2,1)S(1)}, u32[]{:S(2)}, u32[]{:S(2)}) collective-permute-start(bf16[768,768]{1,0:T(8,128)(2,1)S(1)} %add_convert_fusion.1), channel_id=1, source_target_pairs={{0,2},{1,3},{2,0},{3,1},{4,6},{5,7},{6,4},{7,5},{8,10},{9,11},{10,... | collective-permute-start | bytes 3538952 | tf_op jit(solution)/shard_map/ppermute | solution.py:23
  440.8 116.7 %collective-permute-start.30 = (bf16[768,768]{1,0:T(8,128)(2,1)}, bf16[768,768]{1,0:T(8,128)(2,1)}, u32[]{:S(2)}, u32[]{:S(2)}) collective-permute-start(bf16[768,768]{1,0:T(8,128)(2,1)} %fusion.71), channel_id=1, source_target_pairs={{0,1},{1,0},{2,3},{3,2},{4,5},{5,4},{6,7},{7,6},{8,9},{9,8},{10,11... | collective-permute-start | bytes 3538952 | tf_op jit(solution)/shard_map/ppermute | solution.py:23
  444.7 112.8 %collective-permute-start.32 = (bf16[768,768]{1,0:T(8,128)(2,1)}, bf16[768,768]{1,0:T(8,128)(2,1)}, u32[]{:S(2)}, u32[]{:S(2)}) collective-permute-start(bf16[768,768]{1,0:T(8,128)(2,1)} %add_convert_fusion.4), channel_id=1, source_target_pairs={{0,2},{1,3},{2,0},{3,1},{4,6},{5,7},{6,4},{7,5},{8,10},{9,11},{10,... | collective-permute-start | bytes 3538952 | tf_op jit(solution)/shard_map/ppermute | solution.py:23
  466.2 37.8 %all-to-all-start.5 = ((bf16[8,112,768]{2,1,0:T(8,128)(2,1)}), bf16[8,112,768]{2,1,0:T(8,128)(2,1)}, u32[]{:S(2)}, u32[]{:S(2)}) async-start(bf16[8,112,768]{2,1,0:T(8,128)(2,1)} %get-tuple-element.28), calls=%async_computation.5 | async-start | bytes 2752512 | tf_op jit(solution)/shard_map/all_to_all | solution.py:253
  476.3 19.5 %collective-permute-start.19 = (bf16[192,768]{1,0:T(8,128)(2,1)S(1)}, bf16[192,768]{1,0:T(8,128)(2,1)S(1)}, u32[]{:S(2)}, u32[]{:S(2)}) collective-permute-start(bf16[192,768]{1,0:T(8,128)(2,1)S(1)} %add_convert_fusion.11), channel_id=1, source_target_pairs={{0,2},{1,3},{2,0},{3,1},{4,6},{5,7},{6,4},{7,5},{8,10},{9,11},{10,... | collective-permute-start | bytes 884744 | tf_op jit(solution)/shard_map/ppermute | solution.py:23
  495.8 19.1 %collective-permute-start.20 = (bf16[384,768]{1,0:T(8,128)(2,1)S(1)}, bf16[384,768]{1,0:T(8,128)(2,1)}, u32[]{:S(2)}, u32[]{:S(2)}) collective-permute-start(bf16[384,768]{1,0:T(8,128)(2,1)S(1)} %pad_maximum_fusion.18), channel_id=1, source_target_pairs={{0,1},{1,0},{2,3},{3,2},{4,5},{5,4},{6,7},{7,6},{8,9},{9,8},{10,11... | collective-permute-start | bytes 1769480 | tf_op jit(solution)/shard_map/ppermute | solution.py:23
  504.0 75.5 %all-to-all-start.9 = ((bf16[8,96,768]{2,1,0:T(8,128)(2,1)}), bf16[8,96,768]{2,1,0:T(8,128)(2,1)}, u32[]{:S(2)}, u32[]{:S(2)}) async-start(bf16[8,96,768]{2,1,0:T(8,128)(2,1)} %bitcast.97), calls=%async_computation.9 | async-start | bytes 2359296 | tf_op jit(solution)/shard_map/all_to_all | solution.py:253
  512.5 48.2 %collective-permute-start.12 = (bf16[192,768]{1,0:T(8,128)(2,1)}, bf16[192,768]{1,0:T(8,128)(2,1)}, u32[]{:S(2)}, u32[]{:S(2)}) collective-permute-start(bf16[192,768]{1,0:T(8,128)(2,1)} %fusion.102), channel_id=1, source_target_pairs={{0,2},{1,3},{2,0},{3,1},{4,6},{5,7},{6,4},{7,5},{8,10},{9,11},{10,... | collective-permute-start | bytes 884744 | tf_op jit(solution)/shard_map/ppermute | solution.py:23
  579.6 36.8 %all-to-all-start.8 = ((bf16[8,96,768]{2,1,0:T(8,128)(2,1)}), bf16[8,96,768]{2,1,0:T(8,128)(2,1)}, u32[]{:S(2)}, u32[]{:S(2)}) async-start(bf16[8,96,768]{2,1,0:T(8,128)(2,1)} %bitcast.300), calls=%async_computation.8 | async-start | bytes 2359296 | tf_op jit(solution)/shard_map/all_to_all | solution.py:253
  596.7 22.1 %collective-permute-start.27 = (bf16[1,128,768]{2,1,0:T(8,128)(2,1)S(1)}, bf16[1,128,768]{2,1,0:T(8,128)(2,1)}, u32[]{:S(2)}, u32[]{:S(2)}) collective-permute-start(bf16[1,128,768]{2,1,0:T(8,128)(2,1)S(1)} %maximum_bitcast_fusion), channel_id=1, source_target_pairs={{0,16},{4,20},{8,24},{12,28},{16,0},{20,4},{24,8},{28,12},{1,17},{... | collective-permute-start | bytes 589832 | tf_op jit(solution)/shard_map/ppermute | solution.py:23
  (205 other events, 2236.3 us)

commit v3 on v2

--- a/solution.py
+++ b/solution.py
@@ -322,18 +322,18 @@
         micros = range(micro_count)
 
         slice_order = quarter_order()
-        ups, downs = [up_weight[0]], [down_weight[0]]
-        bit = nh // 2
-        while bit >= 1:
-            got_up = [swap(x, "hidden", bit) for x in ups]
-            got_down = [swap(x, "hidden", bit) for x in downs]
-            ups, downs = ups + got_up, downs + got_down
-            bit //= 2
-        ups = [ups[slice_order.index(r)] for r in range(nh)]
-        downs = [downs[slice_order.index(r)] for r in range(nh)]
-
-        perms, places, tables = [], [], []
-        for m in micros:
+        far = nh // 2
+        up_far = swap(up_weight[0], "hidden", far)
+
+        def spread(mine, got):
+            parts = [mine, got]
+            bit = far // 2
+            while bit >= 1:
+                parts = parts + [swap(x, "hidden", bit) for x in parts]
+                bit //= 2
+            return [parts[slice_order.index(r)] for r in range(nh)]
+
+        def route(m):
             low = jnp.min(routes[m], -1)
             high = jnp.max(routes[m], -1)
             key = (low * expert_count + high) * row_count + jnp.arange(row_count, dtype=jnp.int32)
@@ -342,39 +342,43 @@
                 [jnp.arange(quarter, dtype=jnp.int32) * nh + (h_idx ^ r) for r in range(nh)]
             )
             perm = (targets[:, None] == rank[None, :]).astype(BF)
-            perms.append(perm)
             mine = jnp.dot(perm[:quarter], routes[m].astype(BF), preferred_element_type=F32)
             first, second = mine[:, 0], mine[:, 1]
             names = jnp.arange(expert_count, dtype=F32)[:, None]
             member = (first[None, :] == names) | (second[None, :] == names)
-            before = (
-                jnp.arange(quarter)[:, None] < jnp.arange(quarter)[None, :]
-            ).astype(BF)
+            before = (jnp.arange(quarter)[:, None] < jnp.arange(quarter)[None, :]).astype(BF)
             place = jnp.dot(member.astype(BF), before, preferred_element_type=F32)
             slot = jnp.arange(cap, dtype=F32)[None, :, None]
-            table = (slot == place[:, None, :]) & member[:, None, :]
-            tables.append(table.astype(BF))
+            table = ((slot == place[:, None, :]) & member[:, None, :]).astype(BF)
             others = (first + second)[None, :] - names
-            places.append((member, others))
-
-        def dispatch(m, rows):
-            return jnp.einsum("ejt,td->ejd", tables[m], rows, preferred_element_type=F32).astype(BF)
-
-        upstream_mine, upstream_slots = [], []
-        for m in micros:
-            up_rows = jnp.dot(perms[m][:quarter], cotangent[m], preferred_element_type=F32)
-            upstream_mine.append(up_rows)
-            other = jnp.sum(tables[m].astype(F32) * places[m][1][:, None, :], -1)
+            return perm, table, member, others
+
+        def dispatch(table, rows):
+            return jnp.einsum("ejt,td->ejd", table, rows, preferred_element_type=F32).astype(BF)
+
+        def dispatch_upstream(m, perm, table, others):
+            up_rows = jnp.dot(perm[:quarter], cotangent[m], preferred_element_type=F32)
+            other = jnp.sum(table.astype(F32) * others[:, None, :], -1)
             other = jnp.pad(other[:, None, :], ((0, 0), (0, 0), (0, width - cap)))
-            sent = jnp.einsum(
-                "ejt,td->ejd", tables[m], up_rows.astype(BF), preferred_element_type=F32
-            )
+            sent = jnp.einsum("ejt,td->ejd", table, up_rows.astype(BF), preferred_element_type=F32)
             last = (jnp.arange(cap) == cap - 1)[None, :, None]
-            upstream_slots.append(to_experts(jnp.where(last, other, sent).astype(BF)))
-
+            return up_rows, jnp.where(last, other, sent).astype(BF)
+
+        perms, tables, upstream_mine, upstream_slots = [], [], [], []
         state = []
         for m in micros:
-            inputs = tokens[m].astype(F32)
+            if m == 0:
+                perm, table, member, others = route(m)
+                up_rows, up_sent = dispatch_upstream(m, perm, table, others)
+                upstream_slots.append(to_experts(up_sent))
+                following = None
+            else:
+                perm, table, member, others, up_rows, up_sent = following
+            perms.append(perm)
+            tables.append(table)
+            upstream_mine.append(up_rows)
+            mine_tokens = after(tokens[m], up_sent)
+            inputs = mine_tokens.astype(F32)
             allowed = visible(doc_ids[m, 0], pad_mask[m])
             normed1, scale1 = normalize(inputs)
             attn_in = (normed1 * norm1_gain + norm1_bias).astype(BF)
@@ -386,17 +390,34 @@
             heads_low = heads_out.reshape(row_count, -1).astype(BF)
             heads_sorted = jnp.dot(perms[m], heads_low, preferred_element_type=F32).astype(BF)
             term = jnp.dot(heads_sorted, out_weight, preferred_element_type=F32).astype(BF)
+            if m == 0:
+                term, up_far = after((term, up_far), up_far)
+                down_mine = after(down_weight[0], term)
+                down_far = swap(down_mine, "hidden", far)
+                ups = spread(up_weight[0], up_far)
+            elif m == micro_count - 1:
+                term, down_far = after((term, down_far), down_far)
+                downs = spread(down_weight[0], down_far)
             attention = reduce_quarters(term).astype(F32)
-            inputs_mine = jnp.dot(perms[m][:quarter], tokens[m], preferred_element_type=F32)
+            inputs_mine = jnp.dot(perm[:quarter], mine_tokens, preferred_element_type=F32)
             residual = inputs_mine + attention
             normed2, scale2 = normalize(residual)
             moe_in = (normed2 * norm2_gain + norm2_bias).astype(BF)
             logits = jnp.dot(moe_in, router, preferred_element_type=F32).T
-            member = places[m][0]
             masked = jnp.where(member, logits, MASKED)
             raised = jnp.where(member, jnp.exp(masked - jnp.max(masked, 0, keepdims=True)), 0.0)
             gates = raised / jnp.sum(raised, 0, keepdims=True)
-            received = to_experts(dispatch(m, moe_in))
+            if m + 1 < micro_count:
+                following = route(m + 1)
+                moe_in, following = after((moe_in, following), following)
+            sent = dispatch(table, moe_in)
+            received = to_experts(sent)
+            if m + 1 < micro_count:
+                perm, table, member, others = after(following, sent)
+                up_rows, up_sent = dispatch_upstream(m + 1, perm, table, others)
+                upstream_slots.append(to_experts(up_sent))
+                following = (perm, table, member, others, up_rows, up_sent)
+            last_sent = sent
             state.append(
                 dict(
                     inputs=inputs,
@@ -420,9 +441,10 @@
         held = None
         for m in micros:
             s = state[m]
+            rows = after(s["received"], last_sent) if m == 0 else s["received"]
             out, copies, *held = run_expert(
                 own_expert,
-                s["received"],
+                rows,
                 upstream_slots[m],
                 router,
                 ups,
@@ -432,10 +454,13 @@
                 micro_count,
             )
             s["copies_back"] = to_experts(copies)
-            s["out_back"] = to_experts(out)
+            s["out"] = out
+        for m in micros:
+            state[m]["out_back"] = to_experts(after(state[m]["out"], copies))
 
         rows_all, grads_all, act_all, pre_all = held
         parts = []
+        made = []
         for left, right in ((rows_all, pre_all), (grads_all, act_all)):
             hidden = right.shape[1] // nh
             slabs = [
@@ -447,6 +472,7 @@
                 ).astype(BF)
                 for r in range(nh)
             ]
+            made += slabs
             bit = 1
             while bit < nh:
                 got = [swap(slab, "hidden", bit) for slab in slabs[1::2]]
@@ -462,7 +488,7 @@
         gain2_total, bias2_total = 0.0, 0.0
         for m in micros:
             s = state[m]
-            back = s["copies_back"]
+            back = after(s["copies_back"], made) if m == 0 else s["copies_back"]
             table = tables[m]
             copies_sum = jnp.einsum("ejt,ejd->td", table, back, preferred_element_type=F32)
             slot_grad = back[:, cap - 1, :cap].astype(F32) + back[:, cap - 2, :cap].astype(F32)

time: 669 us -> 568 us (0.85)
  waiting for transfers between devices: 267 us -> 172 us
    ppermute x36, waiting for transfers between devices: 154 us -> 102 us  [swap(): return lax.ppermute(values, axis, [(i, i ^ bit) for i in range(size)])]
    all_to_all x10, waiting for transfers between devices: 113 us -> 69.6 us  [to_experts(): lax.all_to_all(blocks, 'expert', split_axis=0, concat_axis=0, tiled=True)]
    unnamed x368 -> x366, local copies, waits for them, and re-layouts: 15.1 us -> 17.3 us
  transfers between devices with their start and end apart: 46 -> 46, of which waited for: 23 -> 16; matrix products, arithmetic and copies ran while one was open for 25% -> 40% of each run, Pallas kernels for 0% -> 10%
where the time goes in v3:
time: 568 us; the launch traced here: 562 us
  waiting for transfers between devices  172 us (30%)
  matrix products  129 us (23%)
  starting transfers between devices  78.4 us (14%)
  other arithmetic  76.1 us (13%)
  Pallas kernels  55.9 us (10%)
  local copies, waits for them, and re-layouts  46.5 us (8%)
    ppermute x36, waiting for transfers between devices, swap(): return lax.ppermute(values, axis, [(i, i ^ bit) for i in range(size)])  102 us
    all_to_all x10, waiting for transfers between devices, to_experts(): lax.all_to_all(blocks, 'expert', split_axis=0, concat_axis=0, tiled=True)  69.6 us
    pallas_call x2, Pallas kernels, run_expert(): pl.pallas_call(expert_body(slices, packs, cap, width, aliased), grid=(ste...  55.9 us
    all_to_all x10, starting transfers between devices, to_experts(): lax.all_to_all(blocks, 'expert', split_axis=0, concat_axis=0, tiled=True)  53.1 us
    dot_general x8, matrix products, shards(): jnp.einsum('rd,rf->df', left, right[:, r * hidden:(r + 1) * hidden], pref...  38.5 us
    ppermute x36, starting transfers between devices, swap(): return lax.ppermute(values, axis, [(i, i ^ bit) for i in range(size)])  25.4 us
    unnamed x366, local copies, waits for them, and re-layouts  17.3 us
    dot_general x2, matrix products, attend_backward(): jnp.einsum('qhd,khd->hqk', heads_grad, value_rows, preferred_element_type...  14.7 us
  transfers between devices with their start and end apart: 46, of which 16 were waited for; matrix products, arithmetic and copies ran while one was open for 40% of the time, Pallas kernels for 10%

profile of v3, /device:TPU:0, one launch (start us, length us, event | category | flops | bytes accessed | tf_op | source)
XLA Modules:
  0.0 562.3 jit_solution(16920874915695088199)
XLA Ops:
  12.4 6.1 %all-to-all-start.1 = ((bf16[8,112,768]{2,1,0:T(8,128)(2,1)}), bf16[8,112,768]{2,1,0:T(8,128)(2,1)}, u32[]{:S(2)}, u32[]{:S(2)}) async-start(bf16[8,112,768]{2,1,0:T(8,128)(2,1)} %select_convert_fusion.1), calls=%async_computation.1 | async-start | bytes 2752512 | tf_op jit(solution)/shard_map/all_to_all | solution.py:253
  37.4 7.1 %collective-permute-done.2 = bf16[192,768]{1,0:T(8,128)(2,1)S(1)} collective-permute-done((bf16[192,768]{1,0:T(8,128)(2,1)S(1)}, bf16[192,768]{1,0:T(8,128)(2,1)S(1)}, u32[]{:S(2)}, u32[]{:S(2)}) %collective-permute-start.2) | collective-permute-done | bytes 294944 | tf_op jit(solution)/shard_map/ppermute | solution.py:23
  59.5 6.0 %all-to-all-start = ((bf16[8,112,768]{2,1,0:T(8,128)(2,1)}), bf16[8,112,768]{2,1,0:T(8,128)(2,1)}, u32[]{:S(2)}, u32[]{:S(2)}) async-start(bf16[8,112,768]{2,1,0:T(8,128)(2,1)} %convolution_convert_fusion.1), calls=%async_computation | async-start | bytes 2752512 | tf_op jit(solution)/shard_map/all_to_all | solution.py:253
  76.3 21.0 %all-to-all-done.rows_ref = bf16[8,112,768]{2,1,0:T(8,128)(2,1)} async-done(((bf16[8,112,768]{2,1,0:T(8,128)(2,1)}), bf16[8,112,768]{2,1,0:T(8,128)(2,1)}, u32[]{:S(2)}, u32[]{:S(2)}) %all-to-all-start) | async-done | bytes 1376288 | tf_op jit(solution)/shard_map/all_to_all | solution.py:253
  105.6 6.1 %collective-permute-done.5 = bf16[192,768]{1,0:T(8,128)(2,1)} collective-permute-done((bf16[192,768]{1,0:T(8,128)(2,1)}, bf16[192,768]{1,0:T(8,128)(2,1)}, u32[]{:S(2)}, u32[]{:S(2)}) %collective-permute-start.5) | collective-permute-done | bytes 294944 | tf_op jit(solution)/shard_map/ppermute | solution.py:23
  117.1 16.7 %all-to-all-done.3.cot_ref = bf16[8,112,768]{2,1,0:T(8,128)(2,1)} async-done(((bf16[8,112,768]{2,1,0:T(8,128)(2,1)}), bf16[8,112,768]{2,1,0:T(8,128)(2,1)}, u32[]{:S(2)}, u32[]{:S(2)}) %all-to-all-start.3) | async-done | bytes 1376288 | tf_op jit(solution)/shard_map/all_to_all | solution.py:253
  149.6 27.8 %expert.2 = (bf16[8,112,768]{2,1,0:T(8,128)(2,1)}, bf16[8,112,768]{2,1,0:T(8,128)(2,1)}, bf16[1792,768]{1,0:T(8,128)(2,1)}, bf16[1792,768]{1,0:T(8,128)(2,1)}, b...) custom-call(s32[1]{0:T(128)} %bitcast.26.own_ref, bf16[8,112,768]{2,1,0:T(8,128)(2,1)} %all-to-all-done.rows_ref, ...), custom_call_target="tpu_custom_call" | custom-call | tf_op jit(solution)/shard_map/expert/pallas_call | solution.py:185
  178.5 6.0 %all-to-all-start.6 = ((bf16[8,112,768]{2,1,0:T(8,128)(2,1)}), bf16[8,112,768]{2,1,0:T(8,128)(2,1)}, u32[]{:S(2)}, u32[]{:S(2)}) async-start(bf16[8,112,768]{2,1,0:T(8,128)(2,1)} %get-tuple-element.69), calls=%async_computation.6 | async-start | bytes 2752512 | tf_op jit(solution)/shard_map/all_to_all | solution.py:253
  187.0 28.1 %expert.3 = (bf16[8,112,768]{2,1,0:T(8,128)(2,1)}, bf16[8,112,768]{2,1,0:T(8,128)(2,1)}, bf16[1792,768]{1,0:T(8,128)(2,1)}, bf16[1792,768]{1,0:T(8,128)(2,1)}, b...) custom-call(s32[1]{0:T(128)} %bitcast.26.own_ref, ...), custom_call_target="tpu_custom_call", output_to_operand_aliasing={{2}: (12, {}), {3}: (13, {}), {4}: (14, {}), {5}: (15, {})} | custom-call | tf_op jit(solution)/shard_map/expert/pallas_call | solution.py:185
  215.1 6.3 %fusion.89 = bf16[768,768]{1,0:T(8,128)(2,1)} fusion(bf16[1792,768]{1,0:T(8,128)(2,1)} %get-tuple-element.72, bf16[1792,3072]{1,0:T(8,128)(2,1)} %get-tuple-element.73), kind=kOutput, calls=%fused_computation.120 | convolution fusion | flops 2114519040 | bytes 6684672 | tf_op jit(solution)/shard_map/rd,rf->df/dot_general | solution.py:467
  221.3 6.1 %fusion.77 = bf16[768,768]{1,0:T(8,128)(2,1)} fusion(bf16[1792,768]{1,0:T(8,128)(2,1)} %get-tuple-element.70, bf16[1792,3072]{1,0:T(8,128)(2,1)} %get-tuple-element.71), kind=kOutput, calls=%fused_computation.116 | convolution fusion | flops 2114519040 | bytes 6684672 | tf_op jit(solution)/shard_map/rd,rf->df/dot_general | solution.py:467
  238.4 6.4 %all-to-all-start.7 = ((bf16[8,112,768]{2,1,0:T(8,128)(2,1)}), bf16[8,112,768]{2,1,0:T(8,128)(2,1)S(1)}, u32[]{:S(2)}, u32[]{:S(2)}) async-start(bf16[8,112,768]{2,1,0:T(8,128)(2,1)} %get-tuple-element.64), calls=%async_computation.7 | async-start | bytes 2752512 | tf_op jit(solution)/shard_map/all_to_all | solution.py:253
  255.7 5.4 fusion.68
  267.2 10.6 %all-to-all-done.7 = bf16[8,112,768]{2,1,0:T(8,128)(2,1)S(1)} async-done(((bf16[8,112,768]{2,1,0:T(8,128)(2,1)}), bf16[8,112,768]{2,1,0:T(8,128)(2,1)S(1)}, u32[]{:S(2)}, u32[]{:S(2)}) %all-to-all-start.7) | async-done | bytes 1376288 | tf_op jit(solution)/shard_map/all_to_all | solution.py:253
  287.1 5.9 %collective-permute-done.35 = bf16[768,768]{1,0:T(8,128)(2,1)} collective-permute-done((bf16[768,768]{1,0:T(8,128)(2,1)}, bf16[768,768]{1,0:T(8,128)(2,1)}, u32[]{:S(2)}, u32[]{:S(2)}) %collective-permute-start.35) | collective-permute-done | bytes 1179680 | tf_op jit(solution)/shard_map/ppermute | solution.py:23
  296.1 21.2 %collective-permute-done.32 = bf16[768,768]{1,0:T(8,128)(2,1)} collective-permute-done((bf16[768,768]{1,0:T(8,128)(2,1)}, bf16[768,768]{1,0:T(8,128)(2,1)}, u32[]{:S(2)}, u32[]{:S(2)}) %collective-permute-start.32) | collective-permute-done | bytes 1179680 | tf_op jit(solution)/shard_map/ppermute | solution.py:23
  321.7 6.0 %all-to-all-start.5 = ((bf16[8,112,768]{2,1,0:T(8,128)(2,1)}), bf16[8,112,768]{2,1,0:T(8,128)(2,1)}, u32[]{:S(2)}, u32[]{:S(2)}) async-start(bf16[8,112,768]{2,1,0:T(8,128)(2,1)} %get-tuple-element.68), calls=%async_computation.5 | async-start | bytes 2752512 | tf_op jit(solution)/shard_map/all_to_all | solution.py:253
  338.7 21.3 %all-to-all-done.5 = bf16[8,112,768]{2,1,0:T(8,128)(2,1)} async-done(((bf16[8,112,768]{2,1,0:T(8,128)(2,1)}), bf16[8,112,768]{2,1,0:T(8,128)(2,1)}, u32[]{:S(2)}, u32[]{:S(2)}) %all-to-all-start.5) | async-done | bytes 1376288 | tf_op jit(solution)/shard_map/all_to_all | solution.py:253
  381.5 7.3 %multiply_reduce_fusion.1 = (f32[3,768]{1,0:T(4,128)S(1)}, f32[3,768,768]{1,2,0:T(8,128)}) fusion(f32[3,768,768]{1,2,0:T(8,128)} %copy-done.9, f32[3,768]{1,0:T(4,128)S(1)} %copy-done.119, bf16[768,3,64]{0,2,1:T(8,128)(2,1)S(1)} %bitcast.287, bf16[768,3,64]{0,2,1:T(8,128)(2,1)S(1)} %bitcast.292), kind=kOutput, calls=%fused_computation.6 | convolution fusion | flops 231798528 | bytes 14764032 | tf_op jit(solution)/shard_map/qhd,khd->hqk/dot_general | solution.py:240
  400.9 7.3 %multiply_reduce_fusion = (f32[3,768]{1,0:T(4,128)S(1)}, f32[3,768,768]{1,2,0:T(8,128)}) fusion(f32[3,768,768]{1,2,0:T(8,128)} %get-tuple-element.208, f32[3,768]{1,0:T(4,128)S(1)} %copy-done.120, bf16[768,3,64]{0,2,1:T(8,128)(2,1)S(1)} %bitcast.289, bf16[768,3,64]{0,2,1:T(8,128)(2,1)S(1)} %bitcast.294), kind=kOutput, calls=%fused_computation.3 | convolution fusion | flops 231798528 | bytes 14764032 | tf_op jit(solution)/shard_map/qhd,khd->hqk/dot_general | solution.py:240
  475.5 21.9 %collective-permute-done.26 = bf16[1,96,768]{2,1,0:T(8,128)(2,1)S(1)} collective-permute-done((bf16[1,96,768]{2,1,0:T(8,128)(2,1)S(1)}, bf16[1,96,768]{2,1,0:T(8,128)(2,1)S(1)}, u32[]{:S(2)}, u32[]{:S(2)}) %collective-permute-start.26) | collective-permute-done | bytes 147488 | tf_op jit(solution)/shard_map/ppermute | solution.py:23
  515.6 7.1 %collective-permute-done.27 = bf16[1,128,768]{2,1,0:T(8,128)(2,1)S(1)} collective-permute-done((bf16[1,128,768]{2,1,0:T(8,128)(2,1)S(1)}, bf16[1,128,768]{2,1,0:T(8,128)(2,1)S(1)}, u32[]{:S(2)}, u32[]{:S(2)}) %collective-permute-start.27) | collective-permute-done | bytes 196640 | tf_op jit(solution)/shard_map/ppermute | solution.py:23
  522.8 11.0 %collective-permute-done.28 = bf16[2,128,768]{2,1,0:T(8,128)(2,1)S(1)} collective-permute-done((bf16[2,128,768]{2,1,0:T(8,128)(2,1)S(1)}, bf16[2,128,768]{2,1,0:T(8,128)(2,1)S(1)}, u32[]{:S(2)}, u32[]{:S(2)}) %collective-permute-start.28) | collective-permute-done | bytes 393248 | tf_op jit(solution)/shard_map/ppermute | solution.py:23
  540.7 11.9 %collective-permute-done.29 = bf16[4,128,768]{2,1,0:T(8,128)(2,1)S(1)} collective-permute-done((bf16[4,128,768]{2,1,0:T(8,128)(2,1)S(1)}, bf16[4,128,768]{2,1,0:T(8,128)(2,1)S(1)}, u32[]{:S(2)}, u32[]{:S(2)}) %collective-permute-start.29) | collective-permute-done | bytes 786464 | tf_op jit(solution)/shard_map/ppermute | solution.py:23
  (637 shorter events, 277.6 us)
Async XLA Ops:
  12.4 47.1 %all-to-all-start.1 = ((bf16[8,112,768]{2,1,0:T(8,128)(2,1)}), bf16[8,112,768]{2,1,0:T(8,128)(2,1)}, u32[]{:S(2)}, u32[]{:S(2)}) async-start(bf16[8,112,768]{2,1,0:T(8,128)(2,1)} %select_convert_fusion.1), calls=%async_computation.1 | async-start | bytes 2752512 | tf_op jit(solution)/shard_map/all_to_all | solution.py:253
  35.8 38.8 %collective-permute-start.3 = (bf16[768,768]{1,0:T(8,128)(2,1)S(1)}, bf16[768,768]{1,0:T(8,128)(2,1)}, u32[]{:S(2)}, u32[]{:S(2)}) collective-permute-start(bf16[768,768]{1,0:T(8,128)(2,1)S(1)} %bitcast.266), channel_id=1, source_target_pairs={{0,2},{1,3},{2,0},{3,1},{4,6},{5,7},{6,4},{7,5},{8,10},{9,11},{10,... | collective-permute-start | bytes 3538952 | tf_op jit(solution)/shard_map/ppermute | solution.py:23
  59.5 37.8 %all-to-all-start = ((bf16[8,112,768]{2,1,0:T(8,128)(2,1)}), bf16[8,112,768]{2,1,0:T(8,128)(2,1)}, u32[]{:S(2)}, u32[]{:S(2)}) async-start(bf16[8,112,768]{2,1,0:T(8,128)(2,1)} %convolution_convert_fusion.1), calls=%async_computation | async-start | bytes 2752512 | tf_op jit(solution)/shard_map/all_to_all | solution.py:253
  97.3 36.5 %all-to-all-start.3 = ((bf16[8,112,768]{2,1,0:T(8,128)(2,1)}), bf16[8,112,768]{2,1,0:T(8,128)(2,1)}, u32[]{:S(2)}, u32[]{:S(2)}) async-start(bf16[8,112,768]{2,1,0:T(8,128)(2,1)} %select_convert_fusion), calls=%async_computation.3 | async-start | bytes 2752512 | tf_op jit(solution)/shard_map/all_to_all | solution.py:253
  104.2 43.4 %collective-permute-start.6 = (bf16[768,768]{1,0:T(8,128)(2,1)S(1)}, bf16[768,768]{1,0:T(8,128)(2,1)}, u32[]{:S(2)}, u32[]{:S(2)}) collective-permute-start(bf16[768,768]{1,0:T(8,128)(2,1)S(1)} %bitcast.263), channel_id=1, source_target_pairs={{0,1},{1,0},{2,3},{3,2},{4,5},{5,4},{6,7},{7,6},{8,9},{9,8},{10,11... | collective-permute-start | bytes 3538952 | tf_op jit(solution)/shard_map/ppermute | solution.py:23
  104.2 43.4 %collective-permute-start.8 = (bf16[768,768]{1,0:T(8,128)(2,1)S(1)}, bf16[768,768]{1,0:T(8,128)(2,1)}, u32[]{:S(2)}, u32[]{:S(2)}) collective-permute-start(bf16[768,768]{1,0:T(8,128)(2,1)S(1)} %bitcast.267), channel_id=1, source_target_pairs={{0,1},{1,0},{2,3},{3,2},{4,5},{5,4},{6,7},{7,6},{8,9},{9,8},{10,11... | collective-permute-start | bytes 3538952 | tf_op jit(solution)/shard_map/ppermute | solution.py:23
  133.8 44.6 %all-to-all-start.2 = ((bf16[8,112,768]{2,1,0:T(8,128)(2,1)}), bf16[8,112,768]{2,1,0:T(8,128)(2,1)}, u32[]{:S(2)}, u32[]{:S(2)}) async-start(bf16[8,112,768]{2,1,0:T(8,128)(2,1)} %convolution_convert_fusion), calls=%async_computation.2 | async-start | bytes 2752512 | tf_op jit(solution)/shard_map/all_to_all | solution.py:253
  178.5 60.0 %all-to-all-start.6 = ((bf16[8,112,768]{2,1,0:T(8,128)(2,1)}), bf16[8,112,768]{2,1,0:T(8,128)(2,1)}, u32[]{:S(2)}, u32[]{:S(2)}) async-start(bf16[8,112,768]{2,1,0:T(8,128)(2,1)} %get-tuple-element.69), calls=%async_computation.6 | async-start | bytes 2752512 | tf_op jit(solution)/shard_map/all_to_all | solution.py:253
  221.3 39.8 %collective-permute-start.34 = (bf16[768,768]{1,0:T(8,128)(2,1)}, bf16[768,768]{1,0:T(8,128)(2,1)}, u32[]{:S(2)}, u32[]{:S(2)}) collective-permute-start(bf16[768,768]{1,0:T(8,128)(2,1)} %fusion.89), channel_id=1, source_target_pairs={{0,1},{1,0},{2,3},{3,2},{4,5},{5,4},{6,7},{7,6},{8,9},{9,8},{10,11... | collective-permute-start | bytes 3538952 | tf_op jit(solution)/shard_map/ppermute | solution.py:23
  227.5 36.9 %collective-permute-start.31 = (bf16[768,768]{1,0:T(8,128)(2,1)}, bf16[768,768]{1,0:T(8,128)(2,1)S(1)}, u32[]{:S(2)}, u32[]{:S(2)}) collective-permute-start(bf16[768,768]{1,0:T(8,128)(2,1)} %fusion.77), channel_id=1, source_target_pairs={{0,1},{1,0},{2,3},{3,2},{4,5},{5,4},{6,7},{7,6},{8,9},{9,8},{10,11... | collective-permute-start | bytes 3538952 | tf_op jit(solution)/shard_map/ppermute | solution.py:23
  238.4 39.3 %all-to-all-start.7 = ((bf16[8,112,768]{2,1,0:T(8,128)(2,1)}), bf16[8,112,768]{2,1,0:T(8,128)(2,1)S(1)}, u32[]{:S(2)}, u32[]{:S(2)}) async-start(bf16[8,112,768]{2,1,0:T(8,128)(2,1)} %get-tuple-element.64), calls=%async_computation.7 | async-start | bytes 2752512 | tf_op jit(solution)/shard_map/all_to_all | solution.py:253
  255.2 31.8 %collective-permute-start.33 = (bf16[768,768]{1,0:T(8,128)(2,1)}, bf16[768,768]{1,0:T(8,128)(2,1)}, u32[]{:S(2)}, u32[]{:S(2)}) collective-permute-start(bf16[768,768]{1,0:T(8,128)(2,1)} %fusion.83), channel_id=1, source_target_pairs={{0,1},{1,0},{2,3},{3,2},{4,5},{5,4},{6,7},{7,6},{8,9},{9,8},{10,11... | collective-permute-start | bytes 3538952 | tf_op jit(solution)/shard_map/ppermute | solution.py:23
  255.2 40.9 %collective-permute-start.30 = (bf16[768,768]{1,0:T(8,128)(2,1)}, bf16[768,768]{1,0:T(8,128)(2,1)}, u32[]{:S(2)}, u32[]{:S(2)}) collective-permute-start(bf16[768,768]{1,0:T(8,128)(2,1)} %fusion.71), channel_id=1, source_target_pairs={{0,1},{1,0},{2,3},{3,2},{4,5},{5,4},{6,7},{7,6},{8,9},{9,8},{10,11... | collective-permute-start | bytes 3538952 | tf_op jit(solution)/shard_map/ppermute | solution.py:23
  265.7 51.6 %collective-permute-start.32 = (bf16[768,768]{1,0:T(8,128)(2,1)}, bf16[768,768]{1,0:T(8,128)(2,1)}, u32[]{:S(2)}, u32[]{:S(2)}) collective-permute-start(bf16[768,768]{1,0:T(8,128)(2,1)} %add_convert_fusion.4), channel_id=1, source_target_pairs={{0,2},{1,3},{2,0},{3,1},{4,6},{5,7},{6,4},{7,5},{8,10},{9,11},{10,... | collective-permute-start | bytes 3538952 | tf_op jit(solution)/shard_map/ppermute | solution.py:23
  277.8 43.9 %all-to-all-start.4 = ((bf16[8,112,768]{2,1,0:T(8,128)(2,1)}), bf16[8,112,768]{2,1,0:T(8,128)(2,1)}, u32[]{:S(2)}, u32[]{:S(2)}) async-start(bf16[8,112,768]{2,1,0:T(8,128)(2,1)} %get-tuple-element.65), calls=%async_computation.4 | async-start | bytes 2752512 | tf_op jit(solution)/shard_map/all_to_all | solution.py:253
  321.7 38.3 %all-to-all-start.5 = ((bf16[8,112,768]{2,1,0:T(8,128)(2,1)}), bf16[8,112,768]{2,1,0:T(8,128)(2,1)}, u32[]{:S(2)}, u32[]{:S(2)}) async-start(bf16[8,112,768]{2,1,0:T(8,128)(2,1)} %get-tuple-element.68), calls=%async_computation.5 | async-start | bytes 2752512 | tf_op jit(solution)/shard_map/all_to_all | solution.py:253
  332.4 34.2 %collective-permute-start.14 = (bf16[192,768]{1,0:T(8,128)(2,1)}, bf16[192,768]{1,0:T(8,128)(2,1)S(1)}, u32[]{:S(2)}, u32[]{:S(2)}) collective-permute-start(bf16[192,768]{1,0:T(8,128)(2,1)} %get-tuple-element.195), channel_id=1, source_target_pairs={{0,2},{1,3},{2,0},{3,1},{4,6},{5,7},{6,4},{7,5},{8,10},{9,11},{10,... | collective-permute-start | bytes 884744 | tf_op jit(solution)/shard_map/ppermute | solution.py:23
  332.9 36.3 %collective-permute-start.19 = (bf16[192,768]{1,0:T(8,128)(2,1)S(1)}, bf16[192,768]{1,0:T(8,128)(2,1)}, u32[]{:S(2)}, u32[]{:S(2)}) collective-permute-start(bf16[192,768]{1,0:T(8,128)(2,1)S(1)} %get-tuple-element.196), channel_id=1, source_target_pairs={{0,2},{1,3},{2,0},{3,1},{4,6},{5,7},{6,4},{7,5},{8,10},{9,11},{10,... | collective-permute-start | bytes 884744 | tf_op jit(solution)/shard_map/ppermute | solution.py:23
  338.0 32.5 %collective-permute-start.10 = (bf16[192,768]{1,0:T(8,128)(2,1)}, bf16[192,768]{1,0:T(8,128)(2,1)}, u32[]{:S(2)}, u32[]{:S(2)}) collective-permute-start(bf16[192,768]{1,0:T(8,128)(2,1)} %fusion.100), channel_id=1, source_target_pairs={{0,2},{1,3},{2,0},{3,1},{4,6},{5,7},{6,4},{7,5},{8,10},{9,11},{10,... | collective-permute-start | bytes 884744 | tf_op jit(solution)/shard_map/ppermute | solution.py:23
  360.0 98.2 %all-to-all-start.9 = ((bf16[8,96,768]{2,1,0:T(8,128)(2,1)}), bf16[8,96,768]{2,1,0:T(8,128)(2,1)}, u32[]{:S(2)}, u32[]{:S(2)}) async-start(bf16[8,96,768]{2,1,0:T(8,128)(2,1)} %bitcast.97), calls=%async_computation.9 | async-start | bytes 2359296 | tf_op jit(solution)/shard_map/all_to_all | solution.py:253
  372.4 72.3 %collective-permute-start.11 = (bf16[384,768]{1,0:T(8,128)(2,1)}, bf16[384,768]{1,0:T(8,128)(2,1)}, u32[]{:S(2)}, u32[]{:S(2)}) collective-permute-start(bf16[384,768]{1,0:T(8,128)(2,1)} %pad_maximum_fusion.15), channel_id=1, source_target_pairs={{0,1},{1,0},{2,3},{3,2},{4,5},{5,4},{6,7},{7,6},{8,9},{9,8},{10,11... | collective-permute-start | bytes 1769480 | tf_op jit(solution)/shard_map/ppermute | solution.py:23
  378.4 70.2 %collective-permute-start.13 = (bf16[384,768]{1,0:T(8,128)(2,1)}, bf16[384,768]{1,0:T(8,128)(2,1)}, u32[]{:S(2)}, u32[]{:S(2)}) collective-permute-start(bf16[384,768]{1,0:T(8,128)(2,1)} %pad_maximum_fusion.16), channel_id=1, source_target_pairs={{0,1},{1,0},{2,3},{3,2},{4,5},{5,4},{6,7},{7,6},{8,9},{9,8},{10,11... | collective-permute-start | bytes 1769480 | tf_op jit(solution)/shard_map/ppermute | solution.py:23
  458.2 44.6 %all-to-all-start.8 = ((bf16[8,96,768]{2,1,0:T(8,128)(2,1)}), bf16[8,96,768]{2,1,0:T(8,128)(2,1)}, u32[]{:S(2)}, u32[]{:S(2)}) async-start(bf16[8,96,768]{2,1,0:T(8,128)(2,1)} %bitcast.274), calls=%async_computation.8 | async-start | bytes 2359296 | tf_op jit(solution)/shard_map/all_to_all | solution.py:253
  464.7 34.5 %collective-permute-start.17 = (bf16[384,768]{1,0:T(8,128)(2,1)S(1)}, bf16[384,768]{1,0:T(8,128)(2,1)S(1)}, u32[]{:S(2)}, u32[]{:S(2)}) collective-permute-start(bf16[384,768]{1,0:T(8,128)(2,1)S(1)} %add_convert_fusion.10), channel_id=1, source_target_pairs={{0,2},{1,3},{2,0},{3,1},{4,6},{5,7},{6,4},{7,5},{8,10},{9,11},{10,... | collective-permute-start | bytes 1769480 | tf_op jit(solution)/shard_map/ppermute | solution.py:23
  (204 other events, 2156.2 us)

commit v4 on v3

--- a/solution.py
+++ b/solution.py
@@ -69,7 +69,7 @@
 
     def body(own_ref, rows_ref, cot_ref, router_ref, *refs):
         ups, downs = refs[:slices], refs[slices : 2 * slices]
-        refs = refs[2 * slices + (4 if aliased else 0) :]
+        refs = refs[2 * slices + (1 if aliased else 0) :]
         (out_ref, copies_ref, rows_all, grads_all, act_all, pre_all) = refs[:6]
         up_v, down_v, grad_rows, acc_out, acc_copies, sems = refs[6:]
         i, s = pl.program_id(0), pl.program_id(1)
@@ -157,38 +157,42 @@
     return body
 
 
-def run_expert(own, rows, cot, router, ups, downs, held, m, micro_count):
-    blocks, cap, width = rows.shape
+def run_expert(own, rows, row_part, cots, cot_part, router, ups, downs, held, m, micro_count):
+    blocks, width = rows.shape[0], rows.shape[2]
+    cap = cots.shape[1] // (cot_part + 1)
     slices = len(ups)
     hidden = ups[0].shape[1]
     packs = max(p for p in range(1, blocks + 1) if blocks % p == 0 and p * cap <= 448)
     steps = blocks // packs
-    total = micro_count * blocks * cap
+    total = blocks * cap
     aliased = held is not None
     rows_n = packs * cap
-    block = pl.BlockSpec((packs, cap, width), lambda i, s: (i, 0, 0))
+
+    def block(part):
+        return pl.BlockSpec((packs, cap, width), lambda i, s: (i, part, 0))
+
     any_spec = pl.BlockSpec(memory_space=pl.ANY)
-    whole_rows = pl.BlockSpec((rows_n, width), lambda i, s: (m * steps + i, 0))
-    whole_hidden = pl.BlockSpec((rows_n, hidden), lambda i, s: (m * steps + i, s))
-    inputs = [own, rows, cot, router, *ups, *downs]
+    whole_rows = pl.BlockSpec((rows_n, width), lambda i, s: (i, 0))
+    whole_hidden = pl.BlockSpec((rows_n, hidden), lambda i, s: (i, s))
+    inputs = [own, rows, cots, router, *ups, *downs]
     in_specs = [
         pl.BlockSpec(memory_space=pltpu.SMEM),
-        block,
-        block,
+        block(row_part),
+        block(cot_part),
         pl.BlockSpec(router.shape, lambda i, s: (0, 0)),
     ] + [any_spec] * (2 * slices)
     aliases = {}
     if aliased:
-        aliases = {len(inputs) + k: 2 + k for k in range(4)}
-        inputs += list(held)
-        in_specs += [any_spec] * 4
+        aliases = {len(inputs): 0}
+        inputs.append(held)
+        in_specs.append(any_spec)
     return pl.pallas_call(
         expert_body(slices, packs, cap, width, aliased),
         grid=(steps, slices),
         in_specs=in_specs,
-        out_specs=[block, block, whole_rows, whole_rows, whole_hidden, whole_hidden],
+        out_specs=[block(m), block(0), whole_rows, whole_rows, whole_hidden, whole_hidden],
         out_shape=[
-            jax.ShapeDtypeStruct((blocks, cap, width), BF),
+            jax.ShapeDtypeStruct((blocks, micro_count * cap, width), BF),
             jax.ShapeDtypeStruct((blocks, cap, width), BF),
             jax.ShapeDtypeStruct((total, width), BF),
             jax.ShapeDtypeStruct((total, width), BF),
@@ -364,20 +368,22 @@
             last = (jnp.arange(cap) == cap - 1)[None, :, None]
             return up_rows, jnp.where(last, other, sent).astype(BF)
 
-        perms, tables, upstream_mine, upstream_slots = [], [], [], []
+        perms, tables, upstream_mine = [], [], []
         state = []
         for m in micros:
             if m == 0:
                 perm, table, member, others = route(m)
                 up_rows, up_sent = dispatch_upstream(m, perm, table, others)
-                upstream_slots.append(to_experts(up_sent))
-                following = None
+                upstream_slots = to_experts(up_sent)
+                earlier = up_sent
             else:
-                perm, table, member, others, up_rows, up_sent = following
+                perm, table, member, others = following
+                up_rows, up_sent = dispatch_upstream(m, perm, table, others)
+                earlier = last_sent
             perms.append(perm)
             tables.append(table)
             upstream_mine.append(up_rows)
-            mine_tokens = after(tokens[m], up_sent)
+            mine_tokens = after(tokens[m], earlier)
             inputs = mine_tokens.astype(F32)
             allowed = visible(doc_ids[m, 0], pad_mask[m])
             normed1, scale1 = normalize(inputs)
@@ -410,14 +416,12 @@
             if m + 1 < micro_count:
                 following = route(m + 1)
                 moe_in, following = after((moe_in, following), following)
-            sent = dispatch(table, moe_in)
-            received = to_experts(sent)
-            if m + 1 < micro_count:
-                perm, table, member, others = after(following, sent)
-                up_rows, up_sent = dispatch_upstream(m + 1, perm, table, others)
-                upstream_slots.append(to_experts(up_sent))
-                following = (perm, table, member, others, up_rows, up_sent)
-            last_sent = sent
+            last_sent = dispatch(table, moe_in)
+            if m == 0:
+                received = (to_experts(last_sent), 0, upstream_slots, 0)
+            else:
+                both = to_experts(jnp.concatenate([last_sent, up_sent], 1))
+                received = (both, 0, both, 1)
             state.append(
                 dict(
                     inputs=inputs,
@@ -438,14 +442,21 @@
             )
 
         own_expert = jnp.full((1,), e_idx, jnp.int32)
-        held = None
+        held, slabs = None, None
         for m in micros:
             s = state[m]
-            rows = after(s["received"], last_sent) if m == 0 else s["received"]
-            out, copies, *held = run_expert(
+            rows, row_part, cots, cot_part = s["received"]
+            if m == 0:
+                rows = after(rows, last_sent)
+            else:
+                rows = after(rows, slabs)
+                cots = rows
+            held, copies, rows_all, grads_all, act_all, pre_all = run_expert(
                 own_expert,
                 rows,
-                upstream_slots[m],
+                row_part,
+                cots,
+                cot_part,
                 router,
                 ups,
                 downs,
@@ -454,41 +465,41 @@
                 micro_count,
             )
             s["copies_back"] = to_experts(copies)
-            s["out"] = out
-        for m in micros:
-            state[m]["out_back"] = to_experts(after(state[m]["out"], copies))
-
-        rows_all, grads_all, act_all, pre_all = held
-        parts = []
-        made = []
-        for left, right in ((rows_all, pre_all), (grads_all, act_all)):
-            hidden = right.shape[1] // nh
-            slabs = [
-                jnp.einsum(
-                    "rd,rf->df",
-                    left,
-                    right[:, r * hidden : (r + 1) * hidden],
-                    preferred_element_type=F32,
-                ).astype(BF)
-                for r in range(nh)
-            ]
-            made += slabs
+            made = []
+            for left, right in ((rows_all, pre_all), (grads_all, act_all)):
+                hidden = right.shape[1] // nh
+                for r in range(nh):
+                    slab = jnp.einsum(
+                        "rd,rf->df",
+                        left,
+                        right[:, r * hidden : (r + 1) * hidden],
+                        preferred_element_type=F32,
+                    )
+                    if slabs is not None:
+                        slab = slab + slabs[len(made)].astype(F32)
+                    made.append(slab.astype(BF))
+            slabs = made
+
+        owned = []
+        for part in (slabs[:nh], slabs[nh:]):
             bit = 1
             while bit < nh:
-                got = [swap(slab, "hidden", bit) for slab in slabs[1::2]]
-                slabs = [
+                got = [swap(slab, "hidden", bit) for slab in part[1::2]]
+                part = [
                     (mine.astype(F32) + other.astype(F32)).astype(BF)
-                    for mine, other in zip(slabs[0::2], got)
+                    for mine, other in zip(part[0::2], got)
                 ]
                 bit *= 2
-            rows = to_experts(slabs[0].reshape(ne, width // ne, -1))
-            parts.append(rows[ne // 2 :].astype(F32))
-
+            owned.append(part[0].reshape(ne, width // ne, -1))
+        owned = jnp.concatenate(owned, 1)
+
+        order = quarter_order()
         grad_router = 0.0
         gain2_total, bias2_total = 0.0, 0.0
+        previous = slabs
         for m in micros:
             s = state[m]
-            back = after(s["copies_back"], made) if m == 0 else s["copies_back"]
+            back = s["copies_back"] = after(s["copies_back"], previous)
             table = tables[m]
             copies_sum = jnp.einsum("ejt,ejd->td", table, back, preferred_element_type=F32)
             slot_grad = back[:, cap - 1, :cap].astype(F32) + back[:, cap - 2, :cap].astype(F32)
@@ -507,34 +518,32 @@
                 s["normed2"], s["scale2"], norm2_gain, normed2_grad
             )
             s["resid_all"] = gather_quarters(resid_grad.astype(BF))
-            weighted = (table.astype(F32) * gates[:, None, :]).astype(BF)
-            mixture = jnp.einsum("ejt,ejd->td", weighted, s["out_back"], preferred_element_type=F32)
-            s["delta_all"] = gather_quarters((s["attention"] + mixture).astype(BF))
+            perm = perms[m].reshape(nh, quarter, row_count)
+            s["perm_all"] = jnp.concatenate([perm[r] for r in order], 0)
+            heads_grad = jnp.einsum(
+                "rd,fd->rf", s["resid_all"], out_weight, preferred_element_type=F32
+            ).astype(BF)
+            s["heads_grad"] = jnp.einsum(
+                "rt,rf->tf", s["perm_all"], heads_grad, preferred_element_type=F32
+            ).astype(BF)
+            previous = s["heads_grad"]
 
         small = jnp.concatenate([gain2_total[None], bias2_total[None], grad_router], 0)
         small_rows = round_up(small.shape[0], 16)
         small = jnp.pad(small, ((0, small_rows - small.shape[0]), (0, 0))).astype(BF)
 
-        order = quarter_order()
         grad_qkv, grad_proj = 0.0, 0.0
         gain1_total, bias1_total = 0.0, 0.0
-        outputs, input_grads = [], []
+        input_grads = []
+        out_back = to_experts(after(held, state[-1]["copies_back"]))
         for m in micros:
             s = state[m]
-            perm = perms[m].reshape(nh, quarter, row_count)
-            perm_all = jnp.concatenate([perm[r] for r in order], 0)
+            perm_all, resid_all, heads_grad = s["perm_all"], s["resid_all"], s["heads_grad"]
             heads_sorted = s["heads_sorted"].reshape(nh, quarter, -1)
             heads_sorted = jnp.concatenate([heads_sorted[r] for r in order], 0)
-            resid_all = s["resid_all"]
             grad_proj = grad_proj + jnp.einsum(
                 "rf,rd->fd", heads_sorted, resid_all, preferred_element_type=F32
             )
-            heads_grad = jnp.einsum(
-                "rd,fd->rf", resid_all, out_weight, preferred_element_type=F32
-            ).astype(BF)
-            heads_grad = jnp.einsum(
-                "rt,rf->tf", perm_all, heads_grad, preferred_element_type=F32
-            ).astype(BF)
             heads = s["heads"]
             grads = attend_backward(
                 heads[0],
@@ -563,8 +572,10 @@
             input_grads.append(
                 resid_grad + normalize_pull(s["normed1"], s["scale1"], norm1_gain, normed1_grad)
             )
-            delta = jnp.einsum("rt,rd->td", perm_all, s["delta_all"], preferred_element_type=F32)
-            outputs.append(s["inputs"] + delta)
+            if m == micro_count - 1:
+                out_back, _ = after((out_back, term), term)
+
+        parts = to_experts(after(owned, out_back))[ne // 2 :].astype(F32)
 
         flat = jnp.concatenate([grad_qkv.reshape(-1), grad_proj.reshape(-1)]).astype(BF)
         share = flat.reshape(ne, -1, width)
@@ -592,6 +603,19 @@
         while bit >= 1:
             found = found + [r ^ bit for r in found]
             bit //= 2
+        outputs = []
+        for m in micros:
+            s = state[m]
+            weighted = (tables[m].astype(F32) * s["gates"][:, None, :]).astype(BF)
+            mixture = jnp.einsum(
+                "ejt,ejd->td",
+                weighted,
+                out_back[:, m * cap : (m + 1) * cap],
+                preferred_element_type=F32,
+            )
+            delta_all = gather_quarters((s["attention"] + mixture).astype(BF))
+            delta = jnp.einsum("rt,rd->td", s["perm_all"], delta_all, preferred_element_type=F32)
+            outputs.append(s["inputs"] + delta)
         sums = jnp.sum(gathered[:, share_rows:].astype(F32), 0)
         where = jnp.zeros((ne,), jnp.int32)
         slots = jnp.array([found.index(r) for r in range(ne)], jnp.int32)
@@ -608,8 +632,8 @@
             sums[2],
             sums[3],
             sums[4 : 4 + expert_count].T,
-            parts[0],
-            parts[1],
+            parts[:, : width // ne],
+            parts[:, width // ne :],
         )
 
     return shards

time: 568 us -> 544 us (0.958)
  waiting for transfers between devices: 172 us -> 154 us
  starting transfers between devices: 78.4 us -> 68.1 us
  local copies, waits for them, and re-layouts: 46.5 us -> 52.6 us
    all_to_all x10 -> x7, waiting for transfers between devices: 69.6 us -> 25.3 us  [to_experts(): lax.all_to_all(blocks, 'expert', split_axis=0, concat_axis=0, tiled=True)]
    ppermute x36, waiting for transfers between devices: 102 us -> 129 us  [swap(): return lax.ppermute(values, axis, [(i, i ^ bit) for i in range(size)])]
    all_to_all x10 -> x7, starting transfers between devices: 53.1 us -> 38.1 us  [to_experts(): lax.all_to_all(blocks, 'expert', split_axis=0, concat_axis=0, tiled=True)]
    dot_general x8 -> x16, matrix products: 38.5 us -> 43.9 us  [shards(): jnp.einsum('rd,rf->df', left, right[:, r * hidden:(r + 1) * hidden], pref...]
    unnamed x366 -> x412, local copies, waits for them, and re-layouts: 17.3 us -> 17.9 us
  transfers between devices with their start and end apart: 46 -> 43, of which waited for: 16 -> 17; matrix products, arithmetic and copies ran while one was open for 40% -> 43% of each run, Pallas kernels for 10% -> 11%
where the time goes in v4:
time: 544 us; the launch traced here: 538 us
  waiting for transfers between devices  154 us (28%)
  matrix products  130 us (24%)
  other arithmetic  72.6 us (13%)
  starting transfers between devices  68.1 us (13%)
  Pallas kernels  56.5 us (10%)
  local copies, waits for them, and re-layouts  52.6 us (10%)
    ppermute x36, waiting for transfers between devices, swap(): return lax.ppermute(values, axis, [(i, i ^ bit) for i in range(size)])  129 us
    pallas_call x2, Pallas kernels, run_expert(): pl.pallas_call(expert_body(slices, packs, cap, width, aliased), grid=(ste...  56.5 us
    dot_general x16, matrix products, shards(): jnp.einsum('rd,rf->df', left, right[:, r * hidden:(r + 1) * hidden], pref...  43.9 us
    all_to_all x7, starting transfers between devices, to_experts(): lax.all_to_all(blocks, 'expert', split_axis=0, concat_axis=0, tiled=True)  38.1 us
    ppermute x36, starting transfers between devices, swap(): return lax.ppermute(values, axis, [(i, i ^ bit) for i in range(size)])  30 us
    all_to_all x7, waiting for transfers between devices, to_experts(): lax.all_to_all(blocks, 'expert', split_axis=0, concat_axis=0, tiled=True)  25.3 us
    unnamed x412, local copies, waits for them, and re-layouts  17.9 us
    dot_general x2, matrix products, attend_backward(): jnp.einsum('qhd,khd->hqk', heads_grad, value_rows, preferred_element_type...  14.7 us
  transfers between devices with their start and end apart: 43, of which 17 were waited for; matrix products, arithmetic and copies ran while one was open for 43% of the time, Pallas kernels for 11%

profile of v4, /device:TPU:0, one launch (start us, length us, event | category | flops | bytes accessed | tf_op | source)
XLA Modules:
  0.0 537.8 jit_solution(14013582194670996377)
XLA Ops:
  12.6 6.1 %all-to-all-start.2 = ((bf16[8,112,768]{2,1,0:T(8,128)(2,1)}), bf16[8,112,768]{2,1,0:T(8,128)(2,1)}, u32[]{:S(2)}, u32[]{:S(2)}) async-start(bf16[8,112,768]{2,1,0:T(8,128)(2,1)} %select_convert_fusion.1), calls=%async_computation.2 | async-start | bytes 2752512 | tf_op jit(solution)/shard_map/all_to_all | solution.py:257
  40.2 7.1 %collective-permute-done.2 = bf16[192,768]{1,0:T(8,128)(2,1)S(1)} collective-permute-done((bf16[192,768]{1,0:T(8,128)(2,1)S(1)}, bf16[192,768]{1,0:T(8,128)(2,1)S(1)}, u32[]{:S(2)}, u32[]{:S(2)}) %collective-permute-start.2) | collective-permute-done | bytes 294944 | tf_op jit(solution)/shard_map/ppermute | solution.py:23
  60.7 11.1 %collective-permute-done.3.refs_6_ = bf16[768,768]{1,0:T(8,128)(2,1)S(1)} collective-permute-done((bf16[768,768]{1,0:T(8,128)(2,1)S(1)}, bf16[768,768]{1,0:T(8,128)(2,1)S(1)}, u32[]{:S(2)}, u32[]{:S(2)}) %collective-permute-start.3) | collective-permute-done | bytes 1179680 | tf_op jit(solution)/shard_map/ppermute | solution.py:23
  75.1 6.0 %all-to-all-start.1 = ((bf16[8,112,768]{2,1,0:T(8,128)(2,1)}), bf16[8,112,768]{2,1,0:T(8,128)(2,1)}, u32[]{:S(2)}, u32[]{:S(2)}) async-start(bf16[8,112,768]{2,1,0:T(8,128)(2,1)} %convolution_convert_fusion.1), calls=%async_computation.1 | async-start | bytes 2752512 | tf_op jit(solution)/shard_map/all_to_all | solution.py:257
  83.7 8.0 %collective-permute-done.5 = bf16[192,768]{1,0:T(8,128)(2,1)S(1)} collective-permute-done((bf16[192,768]{1,0:T(8,128)(2,1)S(1)}, bf16[192,768]{1,0:T(8,128)(2,1)S(1)}, u32[]{:S(2)}, u32[]{:S(2)}) %collective-permute-start.5) | collective-permute-done | bytes 294944 | tf_op jit(solution)/shard_map/ppermute | solution.py:23
  97.3 17.3 %all-to-all-done.1.rows_ref = bf16[8,112,768]{2,1,0:T(8,128)(2,1)} async-done(((bf16[8,112,768]{2,1,0:T(8,128)(2,1)}), bf16[8,112,768]{2,1,0:T(8,128)(2,1)}, u32[]{:S(2)}, u32[]{:S(2)}) %all-to-all-start.1) | async-done | bytes 1376288 | tf_op jit(solution)/shard_map/all_to_all | solution.py:257
  114.6 4.4 all-to-all-start
  128.3 28.4 %expert.2 = (bf16[8,224,768]{2,1,0:T(8,128)(2,1)}, bf16[8,112,768]{2,1,0:T(8,128)(2,1)}, bf16[896,768]{1,0:T(8,128)(2,1)}, bf16[896,768]{1,0:T(8,128)(2,1)}, bf1...) custom-call(s32[1]{0:T(128)} %bitcast.26.own_ref, bf16[8,112,768]{2,1,0:T(8,128)(2,1)} %all-to-all-done.1.rows_ref, ...), custom_call_target="tpu_custom_call" | custom-call | tf_op jit(solution)/shard_map/expert/pallas_call | solution.py:189
  181.2 4.5 all-to-all-start.4
  188.2 28.1 %expert.3 = (bf16[8,224,768]{2,1,0:T(8,128)(2,1)}, bf16[8,112,768]{2,1,0:T(8,128)(2,1)}, bf16[896,768]{1,0:T(8,128)(2,1)}, bf16[896,768]{1,0:T(8,128)(2,1)}, bf1...) custom-call(s32[1]{0:T(128)} %bitcast.26.own_ref, ...), custom_call_target="tpu_custom_call", output_to_operand_aliasing={{0}: (12, {})} | custom-call | tf_op jit(solution)/shard_map/expert/pallas_call | solution.py:189
  247.3 5.6 %collective-permute-done.10 = bf16[192,768]{1,0:T(8,128)(2,1)S(1)} collective-permute-done((bf16[192,768]{1,0:T(8,128)(2,1)S(1)}, bf16[192,768]{1,0:T(8,128)(2,1)S(1)}, u32[]{:S(2)}, u32[]{:S(2)}) %collective-permute-start.10) | collective-permute-done | bytes 294944 | tf_op jit(solution)/shard_map/ppermute | solution.py:23
  256.1 5.7 %all-to-all-start.3 = ((bf16[8,112,768]{2,1,0:T(8,128)(2,1)}), bf16[8,112,768]{2,1,0:T(8,128)(2,1)}, u32[]{:S(2)}, u32[]{:S(2)}) async-start(bf16[8,112,768]{2,1,0:T(8,128)(2,1)} %get-tuple-element.61), calls=%async_computation.3 | async-start | bytes 2752512 | tf_op jit(solution)/shard_map/all_to_all | solution.py:257
  265.1 7.4 %multiply_reduce_fusion = (f32[3,768]{1,0:T(4,128)S(1)}, f32[3,768,768]{1,2,0:T(8,128)}) fusion(f32[3,768,768]{1,2,0:T(8,128)} %copy-done.10, f32[3,768]{1,0:T(4,128)S(1)} %copy-done.96, bf16[768,3,64]{0,2,1:T(8,128)(2,1)S(1)} %bitcast.292, bf16[768,3,64]{0,2,1:T(8,128)(2,1)S(1)} %bitcast.299), kind=kOutput, calls=%fused_computation.3 | convolution fusion | flops 231798528 | bytes 14764032 | tf_op jit(solution)/shard_map/qhd,khd->hqk/dot_general | solution.py:244
  289.6 5.3 all-to-all-done.3
  304.9 23.5 %collective-permute-done.19 = bf16[384,768]{1,0:T(8,128)(2,1)} collective-permute-done((bf16[384,768]{1,0:T(8,128)(2,1)}, bf16[384,768]{1,0:T(8,128)(2,1)}, u32[]{:S(2)}, u32[]{:S(2)}) %collective-permute-start.19) | collective-permute-done | bytes 589856 | tf_op jit(solution)/shard_map/ppermute | solution.py:23
  331.2 6.4 %all-to-all-start.5 = ((bf16[8,224,768]{2,1,0:T(8,128)(2,1)}), bf16[8,224,768]{2,1,0:T(8,128)(2,1)}, u32[]{:S(2)}, u32[]{:S(2)}) async-start(bf16[8,224,768]{2,1,0:T(8,128)(2,1)} %get-tuple-element.69), calls=%async_computation.5 | async-start | bytes 5505024 | tf_op jit(solution)/shard_map/all_to_all | solution.py:257
  345.1 7.3 %multiply_reduce_fusion.1 = (f32[3,768]{1,0:T(4,128)S(1)}, f32[3,768,768]{1,2,0:T(8,128)}) fusion(f32[3,768,768]{1,2,0:T(8,128)} %copy-done.9, f32[3,768]{1,0:T(4,128)S(1)} %copy-done.97, bf16[768,3,64]{0,2,1:T(8,128)(2,1)S(1)} %bitcast.294, bf16[768,3,64]{0,2,1:T(8,128)(2,1)S(1)} %bitcast.297), kind=kOutput, calls=%fused_computation.6 | convolution fusion | flops 231798528 | bytes 14764032 | tf_op jit(solution)/shard_map/qhd,khd->hqk/dot_general | solution.py:244
  391.9 11.0 %collective-permute-done.24 = bf16[4,96,768]{2,1,0:T(8,128)(2,1)S(1)} collective-permute-done((bf16[4,96,768]{2,1,0:T(8,128)(2,1)S(1)}, bf16[4,96,768]{2,1,0:T(8,128)(2,1)S(1)}, u32[]{:S(2)}, u32[]{:S(2)}) %collective-permute-start.24) | collective-permute-done | bytes 589856 | tf_op jit(solution)/shard_map/ppermute | solution.py:23
  408.1 4.9 collective-permute-done.25
  416.4 6.0 %collective-permute-done.26 = bf16[1,96,768]{2,1,0:T(8,128)(2,1)S(1)} collective-permute-done((bf16[1,96,768]{2,1,0:T(8,128)(2,1)S(1)}, bf16[1,96,768]{2,1,0:T(8,128)(2,1)S(1)}, u32[]{:S(2)}, u32[]{:S(2)}) %collective-permute-start.26) | collective-permute-done | bytes 147488 | tf_op jit(solution)/shard_map/ppermute | solution.py:23
  426.7 5.1 all-to-all-start.6
  437.5 6.2 %collective-permute-start.28 = (bf16[2,128,768]{2,1,0:T(8,128)(2,1)S(1)}, bf16[2,128,768]{2,1,0:T(8,128)(2,1)S(1)}, u32[]{:S(2)}, u32[]{:S(2)}) collective-permute-start(bf16[2,128,768]{2,1,0:T(8,128)(2,1)S(1)} %pad_maximum_fusion.21), channel_id=1, source_target_pairs={{0,8},{4,12},{8,0},{12,4},{16,24},{20,28},{24,16},{28,20},{1,9},{5... | collective-permute-start | bytes 1179656 | tf_op jit(solution)/shard_map/ppermute | solution.py:23
  443.6 36.6 %collective-permute-done.28 = bf16[2,128,768]{2,1,0:T(8,128)(2,1)S(1)} collective-permute-done((bf16[2,128,768]{2,1,0:T(8,128)(2,1)S(1)}, bf16[2,128,768]{2,1,0:T(8,128)(2,1)S(1)}, u32[]{:S(2)}, u32[]{:S(2)}) %collective-permute-start.28) | collective-permute-done | bytes 393248 | tf_op jit(solution)/shard_map/ppermute | solution.py:23
  490.8 8.9 %collective-permute-done.29 = bf16[4,128,768]{2,1,0:T(8,128)(2,1)S(1)} collective-permute-done((bf16[4,128,768]{2,1,0:T(8,128)(2,1)S(1)}, bf16[4,128,768]{2,1,0:T(8,128)(2,1)S(1)}, u32[]{:S(2)}, u32[]{:S(2)}) %collective-permute-start.29) | collective-permute-done | bytes 786464 | tf_op jit(solution)/shard_map/ppermute | solution.py:23
  (690 shorter events, 273.0 us)
Async XLA Ops:
  0.7 33.3 %collective-permute-start = (bf16[768,768]{1,0:T(8,128)(2,1)}, bf16[768,768]{1,0:T(8,128)(2,1)S(1)}, u32[]{:S(2)}, u32[]{:S(2)}) collective-permute-start(bf16[768,768]{1,0:T(8,128)(2,1)} %bitcast.266), channel_id=1, source_target_pairs={{0,2},{1,3},{2,0},{3,1},{4,6},{5,7},{6,4},{7,5},{8,10},{9,11},{10,... | collective-permute-start | bytes 3538952 | tf_op jit(solution)/shard_map/ppermute | solution.py:23
  12.6 62.5 %all-to-all-start.2 = ((bf16[8,112,768]{2,1,0:T(8,128)(2,1)}), bf16[8,112,768]{2,1,0:T(8,128)(2,1)}, u32[]{:S(2)}, u32[]{:S(2)}) async-start(bf16[8,112,768]{2,1,0:T(8,128)(2,1)} %select_convert_fusion.1), calls=%async_computation.2 | async-start | bytes 2752512 | tf_op jit(solution)/shard_map/all_to_all | solution.py:257
  38.6 33.1 %collective-permute-start.3 = (bf16[768,768]{1,0:T(8,128)(2,1)S(1)}, bf16[768,768]{1,0:T(8,128)(2,1)S(1)}, u32[]{:S(2)}, u32[]{:S(2)}) collective-permute-start(bf16[768,768]{1,0:T(8,128)(2,1)S(1)} %bitcast.270), channel_id=1, source_target_pairs={{0,2},{1,3},{2,0},{3,1},{4,6},{5,7},{6,4},{7,5},{8,10},{9,11},{10,... | collective-permute-start | bytes 3538952 | tf_op jit(solution)/shard_map/ppermute | solution.py:23
  75.1 39.6 %all-to-all-start.1 = ((bf16[8,112,768]{2,1,0:T(8,128)(2,1)}), bf16[8,112,768]{2,1,0:T(8,128)(2,1)}, u32[]{:S(2)}, u32[]{:S(2)}) async-start(bf16[8,112,768]{2,1,0:T(8,128)(2,1)} %convolution_convert_fusion.1), calls=%async_computation.1 | async-start | bytes 2752512 | tf_op jit(solution)/shard_map/all_to_all | solution.py:257
  114.6 66.5 %all-to-all-start = ((bf16[8,224,768]{2,1,0:T(8,128)(2,1)}), bf16[8,224,768]{2,1,0:T(8,128)(2,1)}, u32[]{:S(2)}, u32[]{:S(2)}) async-start(bf16[8,224,768]{2,1,0:T(8,128)(2,1)} %pad_maximum_fusion.2), calls=%async_computation | async-start | bytes 5505024 | tf_op jit(solution)/shard_map/all_to_all | solution.py:257
  181.2 57.4 %all-to-all-start.4 = ((bf16[8,112,768]{2,1,0:T(8,128)(2,1)}), bf16[8,112,768]{2,1,0:T(8,128)(2,1)}, u32[]{:S(2)}, u32[]{:S(2)}) async-start(bf16[8,112,768]{2,1,0:T(8,128)(2,1)} %get-tuple-element.62), calls=%async_computation.4 | async-start | bytes 2752512 | tf_op jit(solution)/shard_map/all_to_all | solution.py:257
  255.1 28.9 %collective-permute-start.31 = (bf16[768,768]{1,0:T(8,128)(2,1)}, bf16[768,768]{1,0:T(8,128)(2,1)}, u32[]{:S(2)}, u32[]{:S(2)}) collective-permute-start(bf16[768,768]{1,0:T(8,128)(2,1)} %add_convert_fusion.10), channel_id=1, source_target_pairs={{0,1},{1,0},{2,3},{3,2},{4,5},{5,4},{6,7},{7,6},{8,9},{9,8},{10,11... | collective-permute-start | bytes 3538952 | tf_op jit(solution)/shard_map/ppermute | solution.py:23
  255.1 129.0 %collective-permute-start.30 = (bf16[768,768]{1,0:T(8,128)(2,1)}, bf16[768,768]{1,0:T(8,128)(2,1)}, u32[]{:S(2)}, u32[]{:S(2)}) collective-permute-start(bf16[768,768]{1,0:T(8,128)(2,1)} %add_convert_fusion.12), channel_id=1, source_target_pairs={{0,1},{1,0},{2,3},{3,2},{4,5},{5,4},{6,7},{7,6},{8,9},{9,8},{10,11... | collective-permute-start | bytes 3538952 | tf_op jit(solution)/shard_map/ppermute | solution.py:23
  255.6 46.2 %collective-permute-start.34 = (bf16[768,768]{1,0:T(8,128)(2,1)}, bf16[768,768]{1,0:T(8,128)(2,1)}, u32[]{:S(2)}, u32[]{:S(2)}) collective-permute-start(bf16[768,768]{1,0:T(8,128)(2,1)} %add_convert_fusion.6), channel_id=1, source_target_pairs={{0,1},{1,0},{2,3},{3,2},{4,5},{5,4},{6,7},{7,6},{8,9},{9,8},{10,11... | collective-permute-start | bytes 3538952 | tf_op jit(solution)/shard_map/ppermute | solution.py:23
  255.6 150.2 %collective-permute-start.33 = (bf16[768,768]{1,0:T(8,128)(2,1)}, bf16[768,768]{1,0:T(8,128)(2,1)}, u32[]{:S(2)}, u32[]{:S(2)}) collective-permute-start(bf16[768,768]{1,0:T(8,128)(2,1)} %add_convert_fusion.8), channel_id=1, source_target_pairs={{0,1},{1,0},{2,3},{3,2},{4,5},{5,4},{6,7},{7,6},{8,9},{9,8},{10,11... | collective-permute-start | bytes 3538952 | tf_op jit(solution)/shard_map/ppermute | solution.py:23
  256.1 38.8 %all-to-all-start.3 = ((bf16[8,112,768]{2,1,0:T(8,128)(2,1)}), bf16[8,112,768]{2,1,0:T(8,128)(2,1)}, u32[]{:S(2)}, u32[]{:S(2)}) async-start(bf16[8,112,768]{2,1,0:T(8,128)(2,1)} %get-tuple-element.61), calls=%async_computation.3 | async-start | bytes 2752512 | tf_op jit(solution)/shard_map/all_to_all | solution.py:257
  286.6 97.5 %collective-permute-start.32 = (bf16[768,768]{1,0:T(8,128)(2,1)}, bf16[768,768]{1,0:T(8,128)(2,1)}, u32[]{:S(2)}, u32[]{:S(2)}) collective-permute-start(bf16[768,768]{1,0:T(8,128)(2,1)} %add_convert_fusion.4), channel_id=1, source_target_pairs={{0,2},{1,3},{2,0},{3,1},{4,6},{5,7},{6,4},{7,5},{8,10},{9,11},{10,... | collective-permute-start | bytes 3538952 | tf_op jit(solution)/shard_map/ppermute | solution.py:23
  288.1 40.3 %collective-permute-start.19 = (bf16[384,768]{1,0:T(8,128)(2,1)}, bf16[384,768]{1,0:T(8,128)(2,1)}, u32[]{:S(2)}, u32[]{:S(2)}) collective-permute-start(bf16[384,768]{1,0:T(8,128)(2,1)} %add_convert_fusion.18), channel_id=1, source_target_pairs={{0,2},{1,3},{2,0},{3,1},{4,6},{5,7},{6,4},{7,5},{8,10},{9,11},{10,... | collective-permute-start | bytes 1769480 | tf_op jit(solution)/shard_map/ppermute | solution.py:23
  301.8 35.7 %collective-permute-start.12 = (bf16[192,768]{1,0:T(8,128)(2,1)}, bf16[192,768]{1,0:T(8,128)(2,1)}, u32[]{:S(2)}, u32[]{:S(2)}) collective-permute-start(bf16[192,768]{1,0:T(8,128)(2,1)} %add_convert_fusion.19), channel_id=1, source_target_pairs={{0,2},{1,3},{2,0},{3,1},{4,6},{5,7},{6,4},{7,5},{8,10},{9,11},{10,... | collective-permute-start | bytes 884744 | tf_op jit(solution)/shard_map/ppermute | solution.py:23
  328.4 77.3 %collective-permute-start.35 = (bf16[768,768]{1,0:T(8,128)(2,1)}, bf16[768,768]{1,0:T(8,128)(2,1)}, u32[]{:S(2)}, u32[]{:S(2)}) collective-permute-start(bf16[768,768]{1,0:T(8,128)(2,1)} %add_convert_fusion.1), channel_id=1, source_target_pairs={{0,2},{1,3},{2,0},{3,1},{4,6},{5,7},{6,4},{7,5},{8,10},{9,11},{10,... | collective-permute-start | bytes 3538952 | tf_op jit(solution)/shard_map/ppermute | solution.py:23
  331.2 95.6 %all-to-all-start.5 = ((bf16[8,224,768]{2,1,0:T(8,128)(2,1)}), bf16[8,224,768]{2,1,0:T(8,128)(2,1)}, u32[]{:S(2)}, u32[]{:S(2)}) async-start(bf16[8,224,768]{2,1,0:T(8,128)(2,1)} %get-tuple-element.69), calls=%async_computation.5 | async-start | bytes 5505024 | tf_op jit(solution)/shard_map/all_to_all | solution.py:257
  384.1 38.9 %collective-permute-start.20 = (bf16[384,768]{1,0:T(8,128)(2,1)}, bf16[384,768]{1,0:T(8,128)(2,1)S(1)}, u32[]{:S(2)}, u32[]{:S(2)}) collective-permute-start(bf16[384,768]{1,0:T(8,128)(2,1)} %add_convert_fusion.17), channel_id=1, source_target_pairs={{0,1},{1,0},{2,3},{3,2},{4,5},{5,4},{6,7},{7,6},{8,9},{9,8},{10,11... | collective-permute-start | bytes 1769480 | tf_op jit(solution)/shard_map/ppermute | solution.py:23
  384.2 18.8 %collective-permute-start.24 = (bf16[4,96,768]{2,1,0:T(8,128)(2,1)S(1)}, bf16[4,96,768]{2,1,0:T(8,128)(2,1)S(1)}, u32[]{:S(2)}, u32[]{:S(2)}) collective-permute-start(bf16[4,96,768]{2,1,0:T(8,128)(2,1)S(1)} %dynamic-slice_bitcast_fusion), channel_id=1, source_target_pairs={{0,4},{4,0},{8,12},{12,8},{16,20},{20,16},{24,28},{28,24},{1,5},{5... | collective-permute-start | bytes 1769480 | tf_op jit(solution)/shard_map/ppermute | solution.py:23
  390.4 17.4 %collective-permute-start.22 = (bf16[392,768]{1,0:T(8,128)(2,1)S(1)}, bf16[392,768]{1,0:T(8,128)(2,1)S(1)}, u32[]{:S(2)}, u32[]{:S(2)}) collective-permute-start(bf16[392,768]{1,0:T(8,128)(2,1)S(1)} %add_convert_fusion.16), channel_id=1, source_target_pairs={{0,2},{1,3},{2,0},{3,1},{4,6},{5,7},{6,4},{7,5},{8,10},{9,11},{10,... | collective-permute-start | bytes 1806344 | tf_op jit(solution)/shard_map/ppermute | solution.py:23
  426.7 107.8 %all-to-all-start.6 = ((bf16[8,192,768]{2,1,0:T(8,128)(2,1)}), bf16[8,192,768]{2,1,0:T(8,128)(2,1)}, u32[]{:S(2)}, u32[]{:S(2)}) async-start(bf16[8,192,768]{2,1,0:T(8,128)(2,1)} %pad_maximum_fusion.3), calls=%async_computation.6 | async-start | bytes 4718592 | tf_op jit(solution)/shard_map/all_to_all | solution.py:257
  437.5 42.8 %collective-permute-start.28 = (bf16[2,128,768]{2,1,0:T(8,128)(2,1)S(1)}, bf16[2,128,768]{2,1,0:T(8,128)(2,1)S(1)}, u32[]{:S(2)}, u32[]{:S(2)}) collective-permute-start(bf16[2,128,768]{2,1,0:T(8,128)(2,1)S(1)} %pad_maximum_fusion.21), channel_id=1, source_target_pairs={{0,8},{4,12},{8,0},{12,4},{16,24},{20,28},{24,16},{28,20},{1,9},{5... | collective-permute-start | bytes 1179656 | tf_op jit(solution)/shard_map/ppermute | solution.py:23
  481.3 18.4 %collective-permute-start.29 = (bf16[4,128,768]{2,1,0:T(8,128)(2,1)S(1)}, bf16[4,128,768]{2,1,0:T(8,128)(2,1)S(1)}, u32[]{:S(2)}, u32[]{:S(2)}) collective-permute-start(bf16[4,128,768]{2,1,0:T(8,128)(2,1)S(1)} %pad_maximum_fusion.14), channel_id=1, source_target_pairs={{0,4},{4,0},{8,12},{12,8},{16,20},{20,16},{24,28},{28,24},{1,5},{5... | collective-permute-start | bytes 2359304 | tf_op jit(solution)/shard_map/ppermute | solution.py:23
  505.3 21.7 %collective-permute-start.15 = (bf16[384,768]{1,0:T(8,128)(2,1)}, bf16[384,768]{1,0:T(8,128)(2,1)}, u32[]{:S(2)}, u32[]{:S(2)}) collective-permute-start(bf16[384,768]{1,0:T(8,128)(2,1)} %pad_maximum_fusion.19), channel_id=1, source_target_pairs={{0,1},{1,0},{2,3},{3,2},{4,5},{5,4},{6,7},{7,6},{8,9},{9,8},{10,11... | collective-permute-start | bytes 1769480 | tf_op jit(solution)/shard_map/ppermute | solution.py:23
  510.7 19.0 %collective-permute-start.17 = (bf16[384,768]{1,0:T(8,128)(2,1)}, bf16[384,768]{1,0:T(8,128)(2,1)}, u32[]{:S(2)}, u32[]{:S(2)}) collective-permute-start(bf16[384,768]{1,0:T(8,128)(2,1)} %pad_maximum_fusion.20), channel_id=1, source_target_pairs={{0,1},{1,0},{2,3},{3,2},{4,5},{5,4},{6,7},{7,6},{8,9},{9,8},{10,11... | collective-permute-start | bytes 1769480 | tf_op jit(solution)/shard_map/ppermute | solution.py:23
  (224 other events, 1812.0 us)

commit v5 on v4

--- a/solution.py
+++ b/solution.py
@@ -10,6 +10,8 @@
 PRECISE = lax.Precision.HIGHEST
 MASKED = -1e30
 TILE = 16
+LONGEST = 384
+BLOCK = 256
 BF = jnp.bfloat16
 F32 = jnp.float32
 
@@ -209,47 +211,164 @@
         ],
         input_output_aliases=aliases,
         compiler_params=pltpu.CompilerParams(vmem_limit_bytes=48 * 1024 * 1024),
+        cost_estimate=CHEAP,
         name="expert",
     )(*inputs)
 
 
-def visible(doc_row, pad_row):
-    total_rows = doc_row.shape[0]
-    query_pos = jnp.arange(total_rows)[:, None]
-    key_pos = jnp.arange(total_rows)[None, :]
-    same_doc = doc_row[:, None] == doc_row[None, :]
-    is_real = (pad_row[None, :] == 1) | (query_pos == key_pos)
+CHEAP = pl.CostEstimate(flops=1, bytes_accessed=1, transcendentals=0)
+ALONG = (((1,), (1,)), ((), ()))
+DOWN = (((0,), (0,)), ((), ()))
+
+
+def mm(left, right, dims=None):
+    if dims is None:
+        return jnp.dot(left, right, preferred_element_type=F32)
+    return lax.dot_general(left, right, dims, preferred_element_type=F32)
+
+
+def windows(total_rows):
+    for q0 in range(0, total_rows, BLOCK):
+        q1 = min(q0 + BLOCK, total_rows)
+        yield q0, q1, max(0, (q0 - LONGEST + 1) // 128 * 128)
+
+
+def visible(info, info_t, q0, q1, k0):
+    shape = (q1 - k0, q1 - q0)
+    key_pos = lax.broadcasted_iota(jnp.int32, shape, 0) + k0
+    query_pos = lax.broadcasted_iota(jnp.int32, shape, 1) + q0
+    same_doc = info_t[k0:q1, 0:1] == info[0:1, q0:q1]
+    is_real = (info_t[k0:q1, 1:2] == 1.0) | (query_pos == key_pos)
     return (key_pos <= query_pos) & same_doc & is_real
 
 
-def masked_scores(queries, key_rows, allowed):
-    scores = jnp.einsum("qhd,khd->hqk", queries, key_rows, preferred_element_type=F32)
-    return jnp.where(allowed[None], scores * HEAD_DIM**-0.5, MASKED)
-
-
-def attend_forward(queries, key_rows, value_rows, allowed):
-    scores = masked_scores(queries, key_rows, allowed)
-    row_peak = jnp.max(scores, -1, keepdims=True)
-    exponent = jnp.exp(scores - row_peak)
-    row_total = jnp.sum(exponent, -1, keepdims=True)
-    weights = (exponent / row_total).astype(BF)
-    output = jnp.einsum("hqk,khd->qhd", weights, value_rows, preferred_element_type=F32)
-    return output, row_peak + jnp.log(row_total)
-
-
-def attend_backward(queries, key_rows, value_rows, allowed, log_total, heads_grad):
-    scale = HEAD_DIM**-0.5
-    scores = masked_scores(queries, key_rows, allowed)
-    weights = jnp.exp(scores - log_total)
-    weight_grad = jnp.einsum("qhd,khd->hqk", heads_grad, value_rows, preferred_element_type=F32)
-    row_delta = jnp.sum(weights * weight_grad, -1, keepdims=True)
-    score_grad = (weights * (weight_grad - row_delta)).astype(BF)
-    query_grad = scale * jnp.einsum("hqk,khd->qhd", score_grad, key_rows, preferred_element_type=F32)
-    key_grad = scale * jnp.einsum("hqk,qhd->khd", score_grad, queries, preferred_element_type=F32)
-    value_grad = jnp.einsum(
-        "hqk,qhd->khd", weights.astype(BF), heads_grad, preferred_element_type=F32
-    )
-    return query_grad, key_grad, value_grad
+def attend_forward_body(
+    tokens_ref, info_ref, gain_ref, bias_ref, qkv_w_ref, out_w_ref,
+    term_ref, attn_in_ref, qkv_ref, heads_ref, log_ref,
+):
+    total_rows = tokens_ref.shape[0]
+    local = qkv_w_ref.shape[2]
+    info = info_ref[...]
+    info_t = info.T
+    normed, _ = normalize(tokens_ref[...].astype(F32))
+    attn_in = (normed * gain_ref[...] + bias_ref[...]).astype(BF)
+    attn_in_ref[...] = attn_in
+    for c in range(3):
+        qkv_ref[c] = mm(attn_in, qkv_w_ref[c]).astype(BF)
+    for q0, q1, k0 in windows(total_rows):
+        allowed = visible(info, info_t, q0, q1, k0)
+        for h in range(local // HEAD_DIM):
+            part = slice(h * HEAD_DIM, (h + 1) * HEAD_DIM)
+            scores = mm(qkv_ref[1, k0:q1, part], qkv_ref[0, q0:q1, part], ALONG)
+            scores = jnp.where(allowed, scores * HEAD_DIM**-0.5, MASKED)
+            peak = jnp.max(scores, 0, keepdims=True)
+            exponent = jnp.exp(scores - peak)
+            total = jnp.sum(exponent, 0, keepdims=True)
+            weights = (exponent * (1.0 / total)).astype(BF)
+            output = mm(qkv_ref[2, k0:q1, part], weights, DOWN)
+            heads_ref[q0:q1, part] = output.T.astype(BF)
+            log_ref[h : h + 1, q0:q1] = peak + jnp.log(total)
+    perm = jnp.where(info_t[:, 3:4] == info[2:3, :], 1.0, 0.0).astype(BF)
+    arranged = mm(perm, heads_ref[...]).astype(BF)
+    term_ref[...] = mm(arranged, out_w_ref[...]).astype(BF)
+
+
+def attend_forward(tokens, info, gain, bias, qkv_weight, out_weight):
+    total_rows, width = tokens.shape
+    local = out_weight.shape[0]
+    shape = jax.ShapeDtypeStruct
+    return pl.pallas_call(
+        attend_forward_body,
+        out_shape=[
+            shape((total_rows, width), BF),
+            shape((total_rows, width), BF),
+            shape((3, total_rows, local), BF),
+            shape((total_rows, local), BF),
+            shape((8, total_rows), F32),
+        ],
+        compiler_params=pltpu.CompilerParams(vmem_limit_bytes=40 * 1024 * 1024),
+        cost_estimate=CHEAP,
+        name="attend_forward",
+    )(tokens, info, gain[None], bias[None], qkv_weight, out_weight)
+
+
+def attend_backward_body(adds):
+    def body(resid_ref, info_ref, attn_in_ref, qkv_ref, heads_ref, log_ref, qkv_w_ref, out_w_ref, *refs):
+        if adds:
+            earlier_ref, refs = refs[0], refs[1:]
+        term_ref, resid_out, sums_ref, grads, key_sum, value_sum = refs
+        total_rows = resid_ref.shape[0]
+        local = out_w_ref.shape[0]
+        scale = HEAD_DIM**-0.5
+        info = info_ref[...]
+        info_t = info.T
+        unperm = jnp.where(info_t[:, 2:3] == info[4:5, :], 1.0, 0.0).astype(BF)
+        resid = mm(unperm, resid_ref[...]).astype(BF)
+        resid_out[...] = resid
+        heads_grad = mm(resid, out_w_ref[...], ALONG).astype(BF)
+        key_sum[...] = jnp.zeros(key_sum.shape, F32)
+        value_sum[...] = jnp.zeros(value_sum.shape, F32)
+        for q0, q1, k0 in windows(total_rows):
+            allowed = visible(info, info_t, q0, q1, k0)
+            for h in range(local // HEAD_DIM):
+                part = slice(h * HEAD_DIM, (h + 1) * HEAD_DIM)
+                query, key = qkv_ref[0, q0:q1, part], qkv_ref[1, k0:q1, part]
+                value, out_grad = qkv_ref[2, k0:q1, part], heads_grad[q0:q1, part]
+                scores = mm(key, query, ALONG) * scale
+                scores = jnp.where(allowed, scores, MASKED)
+                weights = jnp.exp(scores - log_ref[h : h + 1, q0:q1])
+                weight_grad = mm(value, out_grad, ALONG)
+                delta = jnp.sum(weights * weight_grad, 0, keepdims=True)
+                score_grad = (weights * (weight_grad - delta)).astype(BF)
+                grads[0, q0:q1, part] = (scale * mm(key, score_grad, DOWN)).T.astype(BF)
+                key_sum[h, k0:q1] += mm(score_grad, query)
+                value_sum[h, k0:q1] += mm(weights.astype(BF), out_grad)
+        for h in range(local // HEAD_DIM):
+            part = slice(h * HEAD_DIM, (h + 1) * HEAD_DIM)
+            grads[1, :, part] = (scale * key_sum[h]).astype(BF)
+            grads[2, :, part] = value_sum[h].astype(BF)
+        term = mm(grads[0], qkv_w_ref[0], ALONG)
+        for c in (1, 2):
+            term = term + mm(grads[c], qkv_w_ref[c], ALONG)
+        term_ref[...] = term.astype(BF)
+        attn_in = attn_in_ref[...]
+        for c in range(4):
+            rows = slice(c * local, (c + 1) * local)
+            if c < 3:
+                found = mm(grads[c], attn_in, DOWN)
+            else:
+                found = mm(heads_ref[...], resid, DOWN)
+            if adds:
+                found = found + earlier_ref[rows, :]
+            sums_ref[rows, :] = found.astype(sums_ref.dtype)
+
+    return body
+
+
+def attend_backward(resid, info, saved, qkv_weight, out_weight, earlier, last):
+    attn_in, qkv, heads, log_total = saved
+    total_rows, width = resid.shape
+    local = out_weight.shape[0]
+    shape = jax.ShapeDtypeStruct
+    inputs = [resid, info, attn_in, qkv, heads, log_total, qkv_weight, out_weight]
+    if earlier is not None:
+        inputs.append(earlier)
+    return pl.pallas_call(
+        attend_backward_body(earlier is not None),
+        out_shape=[
+            shape((total_rows, width), BF),
+            shape((total_rows, width), BF),
+            shape((4 * local, width), BF if last else F32),
+        ],
+        scratch_shapes=[
+            pltpu.VMEM((3, total_rows, local), BF),
+            pltpu.VMEM((local // HEAD_DIM, total_rows, HEAD_DIM), F32),
+            pltpu.VMEM((local // HEAD_DIM, total_rows, HEAD_DIM), F32),
+        ],
+        compiler_params=pltpu.CompilerParams(vmem_limit_bytes=48 * 1024 * 1024),
+        cost_estimate=CHEAP,
+        name="attend_backward",
+    )(*inputs)
 
 
 def make_shards(ne, nh):
@@ -320,7 +439,7 @@
         pack_cap = 2 * row_count * top_count // expert_count
         quarter = row_count // nh
         cap = round_up((pack_cap + (nh - 1) * (expert_count - 1)) // nh + 2, TILE)
-        local_heads = qkv_weight.shape[2] // HEAD_DIM
+        order = quarter_order()
         e_idx = lax.axis_index("expert")
         h_idx = lax.axis_index("hidden")
         micros = range(micro_count)
@@ -355,7 +474,12 @@
             slot = jnp.arange(cap, dtype=F32)[None, :, None]
             table = ((slot == place[:, None, :]) & member[:, None, :]).astype(BF)
             others = (first + second)[None, :] - names
-            return perm, table, member, others
+            deal = jnp.concatenate(
+                [jnp.arange(quarter, dtype=jnp.int32) * nh + (h_idx ^ r) for r in order]
+            )
+            blank = jnp.zeros((row_count,), jnp.int32)
+            info = [doc_ids[m, 0], pad_mask[m], rank, targets, deal, blank, blank, blank]
+            return perm, table, member, others, jnp.stack(info).astype(F32)
 
         def dispatch(table, rows):
             return jnp.einsum("ejt,td->ejd", table, rows, preferred_element_type=F32).astype(BF)
@@ -372,30 +496,21 @@
         state = []
         for m in micros:
             if m == 0:
-                perm, table, member, others = route(m)
+                perm, table, member, others, info = route(m)
                 up_rows, up_sent = dispatch_upstream(m, perm, table, others)
                 upstream_slots = to_experts(up_sent)
                 earlier = up_sent
             else:
-                perm, table, member, others = following
+                perm, table, member, others, info = following
                 up_rows, up_sent = dispatch_upstream(m, perm, table, others)
                 earlier = last_sent
             perms.append(perm)
             tables.append(table)
             upstream_mine.append(up_rows)
             mine_tokens = after(tokens[m], earlier)
-            inputs = mine_tokens.astype(F32)
-            allowed = visible(doc_ids[m, 0], pad_mask[m])
-            normed1, scale1 = normalize(inputs)
-            attn_in = (normed1 * norm1_gain + norm1_bias).astype(BF)
-            projected = jnp.einsum(
-                "rd,cdf->crf", attn_in, qkv_weight, preferred_element_type=F32
-            ).astype(BF)
-            heads = projected.reshape(3, row_count, local_heads, HEAD_DIM)
-            heads_out, log_total = attend_forward(heads[0], heads[1], heads[2], allowed)
-            heads_low = heads_out.reshape(row_count, -1).astype(BF)
-            heads_sorted = jnp.dot(perms[m], heads_low, preferred_element_type=F32).astype(BF)
-            term = jnp.dot(heads_sorted, out_weight, preferred_element_type=F32).astype(BF)
+            term, *saved = attend_forward(
+                mine_tokens, info, norm1_gain, norm1_bias, qkv_weight, out_weight
+            )
             if m == 0:
                 term, up_far = after((term, up_far), up_far)
                 down_mine = after(down_weight[0], term)
@@ -424,14 +539,8 @@
                 received = (both, 0, both, 1)
             state.append(
                 dict(
-                    inputs=inputs,
-                    allowed=allowed,
-                    normed1=normed1,
-                    scale1=scale1,
-                    attn_in=attn_in,
-                    heads=heads,
-                    log_total=log_total,
-                    heads_sorted=heads_sorted,
+                    saved=saved,
+                    info=info,
                     attention=attention,
                     normed2=normed2,
                     scale2=scale2,
@@ -518,67 +627,45 @@
                 s["normed2"], s["scale2"], norm2_gain, normed2_grad
             )
             s["resid_all"] = gather_quarters(resid_grad.astype(BF))
-            perm = perms[m].reshape(nh, quarter, row_count)
-            s["perm_all"] = jnp.concatenate([perm[r] for r in order], 0)
-            heads_grad = jnp.einsum(
-                "rd,fd->rf", s["resid_all"], out_weight, preferred_element_type=F32
-            ).astype(BF)
-            s["heads_grad"] = jnp.einsum(
-                "rt,rf->tf", s["perm_all"], heads_grad, preferred_element_type=F32
-            ).astype(BF)
-            previous = s["heads_grad"]
+            previous = s["resid_all"]
 
         small = jnp.concatenate([gain2_total[None], bias2_total[None], grad_router], 0)
         small_rows = round_up(small.shape[0], 16)
         small = jnp.pad(small, ((0, small_rows - small.shape[0]), (0, 0))).astype(BF)
 
-        grad_qkv, grad_proj = 0.0, 0.0
+        pack_sums = None
         gain1_total, bias1_total = 0.0, 0.0
         input_grads = []
         out_back = to_experts(after(held, state[-1]["copies_back"]))
         for m in micros:
             s = state[m]
-            perm_all, resid_all, heads_grad = s["perm_all"], s["resid_all"], s["heads_grad"]
-            heads_sorted = s["heads_sorted"].reshape(nh, quarter, -1)
-            heads_sorted = jnp.concatenate([heads_sorted[r] for r in order], 0)
-            grad_proj = grad_proj + jnp.einsum(
-                "rf,rd->fd", heads_sorted, resid_all, preferred_element_type=F32
-            )
-            heads = s["heads"]
-            grads = attend_backward(
-                heads[0],
-                heads[1],
-                heads[2],
-                s["allowed"],
-                s["log_total"],
-                heads_grad.reshape(row_count, local_heads, HEAD_DIM),
-            )
-            qkv_grad = jnp.stack(grads).reshape(3, row_count, -1).astype(BF)
-            grad_qkv = grad_qkv + jnp.einsum(
-                "rd,crf->cdf", s["attn_in"], qkv_grad, preferred_element_type=F32
-            )
-            term = jnp.einsum(
-                "crf,cdf->rd", qkv_grad, qkv_weight, preferred_element_type=F32
-            ).astype(BF)
+            term, resid, pack_sums = attend_backward(
+                s["resid_all"],
+                s["info"],
+                s["saved"],
+                qkv_weight,
+                out_weight,
+                pack_sums,
+                m == micro_count - 1,
+            )
             if m == micro_count - 1:
                 total = sum_hidden(jnp.concatenate([term, small], 0))
                 small_sum = total[row_count:]
                 normed1_grad = total[:row_count].astype(F32)
             else:
                 normed1_grad = sum_hidden(term).astype(F32)
-            gain1_total = gain1_total + jnp.sum(normed1_grad * s["normed1"], 0)
+            normed1, scale1 = normalize(tokens[m].astype(F32))
+            gain1_total = gain1_total + jnp.sum(normed1_grad * normed1, 0)
             bias1_total = bias1_total + jnp.sum(normed1_grad, 0)
-            resid_grad = jnp.einsum("rt,rd->td", perm_all, resid_all, preferred_element_type=F32)
             input_grads.append(
-                resid_grad + normalize_pull(s["normed1"], s["scale1"], norm1_gain, normed1_grad)
+                resid.astype(F32) + normalize_pull(normed1, scale1, norm1_gain, normed1_grad)
             )
             if m == micro_count - 1:
                 out_back, _ = after((out_back, term), term)
 
         parts = to_experts(after(owned, out_back))[ne // 2 :].astype(F32)
 
-        flat = jnp.concatenate([grad_qkv.reshape(-1), grad_proj.reshape(-1)]).astype(BF)
-        share = flat.reshape(ne, -1, width)
+        share = pack_sums.reshape(ne, -1, width)
         bit = 1
         while bit < ne:
             flag = (e_idx // bit) % 2
@@ -614,21 +701,22 @@
                 preferred_element_type=F32,
             )
             delta_all = gather_quarters((s["attention"] + mixture).astype(BF))
-            delta = jnp.einsum("rt,rd->td", s["perm_all"], delta_all, preferred_element_type=F32)
-            outputs.append(s["inputs"] + delta)
+            perm = perms[m].reshape(nh, quarter, row_count)
+            perm = jnp.concatenate([perm[r] for r in order], 0)
+            delta = jnp.einsum("rt,rd->td", perm, delta_all, preferred_element_type=F32)
+            outputs.append(tokens[m].astype(F32) + delta)
         sums = jnp.sum(gathered[:, share_rows:].astype(F32), 0)
         where = jnp.zeros((ne,), jnp.int32)
         slots = jnp.array([found.index(r) for r in range(ne)], jnp.int32)
         where = slots[jnp.arange(ne, dtype=jnp.int32) ^ e_idx]
-        flat = gathered[:, :share_rows][where].astype(F32).reshape(-1)
-        split = grad_qkv.size
+        flat = gathered[:, :share_rows][where].astype(F32).reshape(4, -1, width)
         return (
             jnp.stack(outputs),
             jnp.stack(input_grads),
             sums[0],
             sums[1],
-            flat[:split].reshape(grad_qkv.shape),
-            flat[split:].reshape(grad_proj.shape),
+            flat[:3].transpose(0, 2, 1),
+            flat[3],
             sums[2],
             sums[3],
             sums[4 : 4 + expert_count].T,

time: 544 us -> 491 us (0.903)
  matrix products: 130 us -> 71 us
  Pallas kernels: 56.5 us -> 93.7 us
  local copies, waits for them, and re-layouts: 52.6 us -> 33 us
  other arithmetic: 72.6 us -> 62 us
    dot_general x28 -> x2, matrix products: 56.8 us -> 4.54 us  [shards(): delta = jnp.einsum('rt,rd->td', perm, delta_all, preferred_element_type=F32)]
    pallas_call x0 -> x4, Pallas kernels: none -> 37.2 us  [the longest x2 23.5 us: attend_backward(): pl.pallas_call(attend_backward_body(earlier is not None), out_shape=[shap...]
    reshape x3 -> x0, local copies, waits for them, and re-layouts: 7.72 us -> none  [the longest x1 3.33 us: shards(): grad_qkv.reshape(-1)]
    convert_element_type x4 -> x2, other arithmetic: 8.82 us -> 1.34 us  [route(): return (perm, table, member, others, jnp.stack(info).astype(F32))]
    unnamed x412 -> x304, local copies, waits for them, and re-layouts: 17.9 us -> 14.4 us
  transfers between devices with their start and end apart: 43 -> 43, of which waited for: 17 -> 18; matrix products, arithmetic and copies ran while one was open for 43% -> 30% of each run, Pallas kernels for 11% -> 19%
where the time goes in v5:
time: 491 us; the launch traced here: 485 us
  waiting for transfers between devices  155 us (32%)
  Pallas kernels  93.7 us (19%)
  matrix products  71 us (14%)
  starting transfers between devices  67.4 us (14%)
  other arithmetic  62 us (13%)
  local copies, waits for them, and re-layouts  33 us (7%)
    ppermute x36, waiting for transfers between devices, swap(): return lax.ppermute(values, axis, [(i, i ^ bit) for i in range(size)])  130 us
    pallas_call x2, Pallas kernels, run_expert(): pl.pallas_call(expert_body(slices, packs, cap, width, aliased), grid=(ste...  56.5 us
    dot_general x16, matrix products, shards(): jnp.einsum('rd,rf->df', left, right[:, r * hidden:(r + 1) * hidden], pref...  43.9 us
    all_to_all x7, starting transfers between devices, to_experts(): lax.all_to_all(blocks, 'expert', split_axis=0, concat_axis=0, tiled=True)  37.1 us
    ppermute x36, starting transfers between devices, swap(): return lax.ppermute(values, axis, [(i, i ^ bit) for i in range(size)])  30.3 us
    all_to_all x7, waiting for transfers between devices, to_experts(): lax.all_to_all(blocks, 'expert', split_axis=0, concat_axis=0, tiled=True)  24.3 us
    pallas_call x2, Pallas kernels, attend_backward(): pl.pallas_call(attend_backward_body(earlier is not None), out_shape=[shap...  23.5 us
    unnamed x304, local copies, waits for them, and re-layouts  14.4 us
  transfers between devices with their start and end apart: 43, of which 18 were waited for; matrix products, arithmetic and copies ran while one was open for 30% of the time, Pallas kernels for 19%

profile of v5, /device:TPU:0, one launch (start us, length us, event | category | flops | bytes accessed | tf_op | source)
XLA Modules:
  0.0 485.3 jit_solution(14102729830674976228)
XLA Ops:
  12.5 6.1 %all-to-all-start.2 = ((bf16[8,112,768]{2,1,0:T(8,128)(2,1)}), bf16[8,112,768]{2,1,0:T(8,128)(2,1)}, u32[]{:S(2)}, u32[]{:S(2)}) async-start(bf16[8,112,768]{2,1,0:T(8,128)(2,1)} %select_convert_fusion.1), calls=%async_computation.2 | async-start | bytes 2752512 | tf_op jit(solution)/shard_map/all_to_all | solution.py:376
  26.9 6.8 %attend_forward.2 = (bf16[768,768]{1,0:T(8,128)(2,1)S(1)}, bf16[768,768]{1,0:T(8,128)(2,1)S(1)}, bf16[3,768,192]{2,1,0:T(8,128)(2,1)S(1)}, bf16[768,192]{1,0:T(8,128)(2,1)S(1)}, f32[8,768]{1,0:T(8,128)S(1)}) custom-call(bf16[768,768]{1,0:T(8,128)(2,1)S(1)} %get-tuple-element.59.tokens_ref, f32[8,768]{1,0:T(8,128)S(1)} %copy-done.19, ...), custom_call_target="tpu_custom_call" | custom-call | flops 1 | bytes 1 | tf_op jit(solution)/shard_map/attend_forward/pallas_call | solution.py:280
  54.5 6.8 %attend_forward.3 = (bf16[768,768]{1,0:T(8,128)(2,1)S(1)}, bf16[768,768]{1,0:T(8,128)(2,1)S(1)}, bf16[3,768,192]{2,1,0:T(8,128)(2,1)S(1)}, bf16[768,192]{1,0:T(8,128)(2,1)S(1)}, f32[8,768]{1,0:T(8,128)S(1)}) custom-call(bf16[768,768]{1,0:T(8,128)(2,1)S(1)} %get-tuple-element.65.tokens_ref, f32[8,768]{1,0:T(8,128)S(1)} %convert_element_type.450.info_ref, ...), custom_call_target="tpu_custom_call" | custom-call | flops 1 | bytes 1 | tf_op jit(solution)/shard_map/attend_forward/pallas_call | solution.py:280
  61.4 12.3 %collective-permute-done.3.refs_6_ = bf16[768,768]{1,0:T(8,128)(2,1)S(1)} collective-permute-done((bf16[768,768]{1,0:T(8,128)(2,1)}, bf16[768,768]{1,0:T(8,128)(2,1)S(1)}, u32[]{:S(2)}, u32[]{:S(2)}) %collective-permute-start.3) | collective-permute-done | bytes 1179680 | tf_op jit(solution)/shard_map/ppermute | solution.py:25
  77.9 6.1 %all-to-all-start.1 = ((bf16[8,112,768]{2,1,0:T(8,128)(2,1)}), bf16[8,112,768]{2,1,0:T(8,128)(2,1)}, u32[]{:S(2)}, u32[]{:S(2)}) async-start(bf16[8,112,768]{2,1,0:T(8,128)(2,1)} %convolution_convert_fusion.1), calls=%async_computation.1 | async-start | bytes 2752512 | tf_op jit(solution)/shard_map/all_to_all | solution.py:376
  86.5 7.2 %collective-permute-done.5 = bf16[192,768]{1,0:T(8,128)(2,1)S(1)} collective-permute-done((bf16[192,768]{1,0:T(8,128)(2,1)S(1)}, bf16[192,768]{1,0:T(8,128)(2,1)S(1)}, u32[]{:S(2)}, u32[]{:S(2)}) %collective-permute-start.5) | collective-permute-done | bytes 294944 | tf_op jit(solution)/shard_map/ppermute | solution.py:25
  98.8 18.0 %all-to-all-done.1.rows_ref = bf16[8,112,768]{2,1,0:T(8,128)(2,1)} async-done(((bf16[8,112,768]{2,1,0:T(8,128)(2,1)}), bf16[8,112,768]{2,1,0:T(8,128)(2,1)}, u32[]{:S(2)}, u32[]{:S(2)}) %all-to-all-start.1) | async-done | bytes 1376288 | tf_op jit(solution)/shard_map/all_to_all | solution.py:376
  132.6 28.1 %expert.2 = (bf16[8,224,768]{2,1,0:T(8,128)(2,1)}, bf16[8,112,768]{2,1,0:T(8,128)(2,1)}, bf16[896,768]{1,0:T(8,128)(2,1)}, bf16[896,768]{1,0:T(8,128)(2,1)}, bf1...) custom-call(s32[1]{0:T(128)} %bitcast.18.own_ref, bf16[8,112,768]{2,1,0:T(8,128)(2,1)} %all-to-all-done.1.rows_ref, ...), custom_call_target="tpu_custom_call" | custom-call | flops 1 | bytes 1 | tf_op jit(solution)/shard_map/expert/pallas_call | solution.py:191
  182.9 5.4 %all-to-all-start.4 = ((bf16[8,112,768]{2,1,0:T(8,128)(2,1)}), bf16[8,112,768]{2,1,0:T(8,128)(2,1)}, u32[]{:S(2)}, u32[]{:S(2)}) async-start(bf16[8,112,768]{2,1,0:T(8,128)(2,1)} %get-tuple-element.82), calls=%async_computation.4 | async-start | bytes 2752512 | tf_op jit(solution)/shard_map/all_to_all | solution.py:376
  190.6 28.4 %expert.3 = (bf16[8,224,768]{2,1,0:T(8,128)(2,1)}, bf16[8,112,768]{2,1,0:T(8,128)(2,1)}, bf16[896,768]{1,0:T(8,128)(2,1)}, bf16[896,768]{1,0:T(8,128)(2,1)}, bf1...) custom-call(s32[1]{0:T(128)} %bitcast.18.own_ref, ...), custom_call_target="tpu_custom_call", output_to_operand_aliasing={{0}: (12, {})} | custom-call | flops 1 | bytes 1 | tf_op jit(solution)/shard_map/expert/pallas_call | solution.py:191
  246.5 6.1 %all-to-all-start.3 = ((bf16[8,112,768]{2,1,0:T(8,128)(2,1)}), bf16[8,112,768]{2,1,0:T(8,128)(2,1)}, u32[]{:S(2)}, u32[]{:S(2)}) async-start(bf16[8,112,768]{2,1,0:T(8,128)(2,1)} %get-tuple-element.81), calls=%async_computation.3 | async-start | bytes 2752512 | tf_op jit(solution)/shard_map/all_to_all | solution.py:376
  255.2 5.9 %collective-permute-done.10 = bf16[192,768]{1,0:T(8,128)(2,1)S(1)} collective-permute-done((bf16[192,768]{1,0:T(8,128)(2,1)S(1)}, bf16[192,768]{1,0:T(8,128)(2,1)S(1)}, u32[]{:S(2)}, u32[]{:S(2)}) %collective-permute-start.10) | collective-permute-done | bytes 294944 | tf_op jit(solution)/shard_map/ppermute | solution.py:25
  264.1 11.9 %attend_backward.2 = (bf16[768,768]{1,0:T(8,128)(2,1)S(1)}, bf16[768,768]{1,0:T(8,128)(2,1)S(1)}, f32[768,768]{1,0:T(8,128)}) custom-call(bf16[768,768]{1,0:T(8,128)(2,1)S(1)} %pad_maximum_fusion.7.resid_ref, f32[8,768]{1,0:T(8,128)S(1)} %copy-done.20, bf16[768,768]{1,0:T(8,128)(2,1)S(1)} %copy-done.11, bf16[3,768,192]{2,1,0:T(8,128)(2,1)} %copy-done.12, ...), custom_call_target="tpu_custom_call" | custom-call | flops 1 | bytes 1 | tf_op jit(solution)/shard_map/attend_backward/pallas_call | solution.py:356
  279.3 5.9 %all-to-all-done.3 = bf16[8,112,768]{2,1,0:T(8,128)(2,1)} async-done(((bf16[8,112,768]{2,1,0:T(8,128)(2,1)}), bf16[8,112,768]{2,1,0:T(8,128)(2,1)}, u32[]{:S(2)}, u32[]{:S(2)}) %all-to-all-start.3) | async-done | bytes 1376288 | tf_op jit(solution)/shard_map/all_to_all | solution.py:376
  301.6 12.7 %collective-permute-done.12 = bf16[192,768]{1,0:T(8,128)(2,1)} collective-permute-done((bf16[192,768]{1,0:T(8,128)(2,1)}, bf16[192,768]{1,0:T(8,128)(2,1)}, u32[]{:S(2)}, u32[]{:S(2)}) %collective-permute-start.12) | collective-permute-done | bytes 294944 | tf_op jit(solution)/shard_map/ppermute | solution.py:25
  319.1 11.6 %attend_backward.3 = (bf16[768,768]{1,0:T(8,128)(2,1)S(1)}, bf16[768,768]{1,0:T(8,128)(2,1)S(1)}, bf16[768,768]{1,0:T(8,128)(2,1)S(1)}) custom-call(bf16[768,768]{1,0:T(8,128)(2,1)S(1)} %pad_maximum_fusion.8.resid_ref, f32[8,768]{1,0:T(8,128)S(1)} %copy-done.22, bf16[768,768]{1,0:T(8,128)(2,1)} %copy-done.13, bf16[3,768,192]{2,1,0:T(8,128)(2,1)} %copy-done.14, ...), custom_call_target="tpu_custom_call" | custom-call | flops 1 | bytes 1 | tf_op jit(solution)/shard_map/attend_backward/pallas_call | solution.py:356
  339.1 15.2 %collective-permute-done.24 = bf16[4,96,768]{2,1,0:T(8,128)(2,1)S(1)} collective-permute-done((bf16[4,96,768]{2,1,0:T(8,128)(2,1)S(1)}, bf16[4,96,768]{2,1,0:T(8,128)(2,1)S(1)}, u32[]{:S(2)}, u32[]{:S(2)}) %collective-permute-start.24) | collective-permute-done | bytes 589856 | tf_op jit(solution)/shard_map/ppermute | solution.py:25
  354.5 6.5 %collective-permute-start.25 = (bf16[2,96,768]{2,1,0:T(8,128)(2,1)S(1)}, bf16[2,96,768]{2,1,0:T(8,128)(2,1)S(1)}, u32[]{:S(2)}, u32[]{:S(2)}) collective-permute-start(bf16[2,96,768]{2,1,0:T(8,128)(2,1)S(1)} %dynamic-slice_bitcast_fusion.1), channel_id=1, source_target_pairs={{0,8},{4,12},{8,0},{12,4},{16,24},{20,28},{24,16},{28,20},{1,9},{5... | collective-permute-start | bytes 884744 | tf_op jit(solution)/shard_map/ppermute | solution.py:25
  371.2 7.5 %collective-permute-done.26 = bf16[1,96,768]{2,1,0:T(8,128)(2,1)S(1)} collective-permute-done((bf16[1,96,768]{2,1,0:T(8,128)(2,1)S(1)}, bf16[1,96,768]{2,1,0:T(8,128)(2,1)S(1)}, u32[]{:S(2)}, u32[]{:S(2)}) %collective-permute-start.26) | collective-permute-done | bytes 147488 | tf_op jit(solution)/shard_map/ppermute | solution.py:25
  389.0 6.9 %collective-permute-done.27 = bf16[1,128,768]{2,1,0:T(8,128)(2,1)} collective-permute-done((bf16[1,128,768]{2,1,0:T(8,128)(2,1)}, bf16[1,128,768]{2,1,0:T(8,128)(2,1)}, u32[]{:S(2)}, u32[]{:S(2)}) %collective-permute-start.27) | collective-permute-done | bytes 196640 | tf_op jit(solution)/shard_map/ppermute | solution.py:25
  396.9 5.8 %collective-permute-start.28 = (bf16[2,128,768]{2,1,0:T(8,128)(2,1)S(1)}, bf16[2,128,768]{2,1,0:T(8,128)(2,1)S(1)}, u32[]{:S(2)}, u32[]{:S(2)}) collective-permute-start(bf16[2,128,768]{2,1,0:T(8,128)(2,1)S(1)} %pad_maximum_fusion.16), channel_id=1, source_target_pairs={{0,8},{4,12},{8,0},{12,4},{16,24},{20,28},{24,16},{28,20},{1,9},{5... | collective-permute-start | bytes 1179656 | tf_op jit(solution)/shard_map/ppermute | solution.py:25
  402.8 35.1 %collective-permute-done.28 = bf16[2,128,768]{2,1,0:T(8,128)(2,1)S(1)} collective-permute-done((bf16[2,128,768]{2,1,0:T(8,128)(2,1)S(1)}, bf16[2,128,768]{2,1,0:T(8,128)(2,1)S(1)}, u32[]{:S(2)}, u32[]{:S(2)}) %collective-permute-start.28) | collective-permute-done | bytes 393248 | tf_op jit(solution)/shard_map/ppermute | solution.py:25
  449.2 8.5 %collective-permute-done.29 = bf16[4,128,768]{2,1,0:T(8,128)(2,1)S(1)} collective-permute-done((bf16[4,128,768]{2,1,0:T(8,128)(2,1)S(1)}, bf16[4,128,768]{2,1,0:T(8,128)(2,1)S(1)}, u32[]{:S(2)}, u32[]{:S(2)}) %collective-permute-start.29) | collective-permute-done | bytes 786464 | tf_op jit(solution)/shard_map/ppermute | solution.py:25
  462.1 6.1 %collective-permute-done.16 = bf16[192,768]{1,0:T(8,128)(2,1)S(1)} collective-permute-done((bf16[192,768]{1,0:T(8,128)(2,1)S(1)}, bf16[192,768]{1,0:T(8,128)(2,1)S(1)}, u32[]{:S(2)}, u32[]{:S(2)}) %collective-permute-start.16) | collective-permute-done | bytes 294944 | tf_op jit(solution)/shard_map/ppermute | solution.py:25
  (551 shorter events, 210.8 us)
Async XLA Ops:
  0.6 34.3 %collective-permute-start = (bf16[768,768]{1,0:T(8,128)(2,1)}, bf16[768,768]{1,0:T(8,128)(2,1)}, u32[]{:S(2)}, u32[]{:S(2)}) collective-permute-start(bf16[768,768]{1,0:T(8,128)(2,1)} %bitcast.208), channel_id=1, source_target_pairs={{0,2},{1,3},{2,0},{3,1},{4,6},{5,7},{6,4},{7,5},{8,10},{9,11},{10,... | collective-permute-start | bytes 3538952 | tf_op jit(solution)/shard_map/ppermute | solution.py:25
  12.5 65.4 %all-to-all-start.2 = ((bf16[8,112,768]{2,1,0:T(8,128)(2,1)}), bf16[8,112,768]{2,1,0:T(8,128)(2,1)}, u32[]{:S(2)}, u32[]{:S(2)}) async-start(bf16[8,112,768]{2,1,0:T(8,128)(2,1)} %select_convert_fusion.1), calls=%async_computation.2 | async-start | bytes 2752512 | tf_op jit(solution)/shard_map/all_to_all | solution.py:376
  44.3 29.4 %collective-permute-start.3 = (bf16[768,768]{1,0:T(8,128)(2,1)}, bf16[768,768]{1,0:T(8,128)(2,1)S(1)}, u32[]{:S(2)}, u32[]{:S(2)}) collective-permute-start(bf16[768,768]{1,0:T(8,128)(2,1)} %bitcast.212), channel_id=1, source_target_pairs={{0,2},{1,3},{2,0},{3,1},{4,6},{5,7},{6,4},{7,5},{8,10},{9,11},{10,... | collective-permute-start | bytes 3538952 | tf_op jit(solution)/shard_map/ppermute | solution.py:25
  77.9 38.8 %all-to-all-start.1 = ((bf16[8,112,768]{2,1,0:T(8,128)(2,1)}), bf16[8,112,768]{2,1,0:T(8,128)(2,1)}, u32[]{:S(2)}, u32[]{:S(2)}) async-start(bf16[8,112,768]{2,1,0:T(8,128)(2,1)} %convolution_convert_fusion.1), calls=%async_computation.1 | async-start | bytes 2752512 | tf_op jit(solution)/shard_map/all_to_all | solution.py:376
  116.7 66.2 %all-to-all-start = ((bf16[8,224,768]{2,1,0:T(8,128)(2,1)}), bf16[8,224,768]{2,1,0:T(8,128)(2,1)}, u32[]{:S(2)}, u32[]{:S(2)}) async-start(bf16[8,224,768]{2,1,0:T(8,128)(2,1)} %pad_maximum_fusion.2), calls=%async_computation | async-start | bytes 5505024 | tf_op jit(solution)/shard_map/all_to_all | solution.py:376
  182.9 58.4 %all-to-all-start.4 = ((bf16[8,112,768]{2,1,0:T(8,128)(2,1)}), bf16[8,112,768]{2,1,0:T(8,128)(2,1)}, u32[]{:S(2)}, u32[]{:S(2)}) async-start(bf16[8,112,768]{2,1,0:T(8,128)(2,1)} %get-tuple-element.82), calls=%async_computation.4 | async-start | bytes 2752512 | tf_op jit(solution)/shard_map/all_to_all | solution.py:376
  246.5 38.7 %all-to-all-start.3 = ((bf16[8,112,768]{2,1,0:T(8,128)(2,1)}), bf16[8,112,768]{2,1,0:T(8,128)(2,1)}, u32[]{:S(2)}, u32[]{:S(2)}) async-start(bf16[8,112,768]{2,1,0:T(8,128)(2,1)} %get-tuple-element.81), calls=%async_computation.3 | async-start | bytes 2752512 | tf_op jit(solution)/shard_map/all_to_all | solution.py:376
  255.2 22.1 %collective-permute-start.31 = (bf16[768,768]{1,0:T(8,128)(2,1)}, bf16[768,768]{1,0:T(8,128)(2,1)S(1)}, u32[]{:S(2)}, u32[]{:S(2)}) collective-permute-start(bf16[768,768]{1,0:T(8,128)(2,1)} %add_convert_fusion.10), channel_id=1, source_target_pairs={{0,1},{1,0},{2,3},{3,2},{4,5},{5,4},{6,7},{7,6},{8,9},{9,8},{10,11... | collective-permute-start | bytes 3538952 | tf_op jit(solution)/shard_map/ppermute | solution.py:25
  262.6 70.2 %collective-permute-start.30 = (bf16[768,768]{1,0:T(8,128)(2,1)}, bf16[768,768]{1,0:T(8,128)(2,1)}, u32[]{:S(2)}, u32[]{:S(2)}) collective-permute-start(bf16[768,768]{1,0:T(8,128)(2,1)} %add_convert_fusion.12), channel_id=1, source_target_pairs={{0,1},{1,0},{2,3},{3,2},{4,5},{5,4},{6,7},{7,6},{8,9},{9,8},{10,11... | collective-permute-start | bytes 3538952 | tf_op jit(solution)/shard_map/ppermute | solution.py:25
  263.2 27.1 %collective-permute-start.34 = (bf16[768,768]{1,0:T(8,128)(2,1)}, bf16[768,768]{1,0:T(8,128)(2,1)}, u32[]{:S(2)}, u32[]{:S(2)}) collective-permute-start(bf16[768,768]{1,0:T(8,128)(2,1)} %add_convert_fusion.6), channel_id=1, source_target_pairs={{0,1},{1,0},{2,3},{3,2},{4,5},{5,4},{6,7},{7,6},{8,9},{9,8},{10,11... | collective-permute-start | bytes 3538952 | tf_op jit(solution)/shard_map/ppermute | solution.py:25
  263.2 97.7 %collective-permute-start.33 = (bf16[768,768]{1,0:T(8,128)(2,1)}, bf16[768,768]{1,0:T(8,128)(2,1)}, u32[]{:S(2)}, u32[]{:S(2)}) collective-permute-start(bf16[768,768]{1,0:T(8,128)(2,1)} %add_convert_fusion.8), channel_id=1, source_target_pairs={{0,1},{1,0},{2,3},{3,2},{4,5},{5,4},{6,7},{7,6},{8,9},{9,8},{10,11... | collective-permute-start | bytes 3538952 | tf_op jit(solution)/shard_map/ppermute | solution.py:25
  276.8 16.6 %collective-permute-start.18 = (bf16[384,768]{1,0:T(8,128)(2,1)}, bf16[384,768]{1,0:T(8,128)(2,1)}, u32[]{:S(2)}, u32[]{:S(2)}) collective-permute-start(bf16[384,768]{1,0:T(8,128)(2,1)} %constant_dynamic-slice_fusion.1), channel_id=1, source_target_pairs={{0,1},{1,0},{2,3},{3,2},{4,5},{5,4},{6,7},{7,6},{8,9},{9,8},{10,11... | collective-permute-start | bytes 1769480 | tf_op jit(solution)/shard_map/ppermute | solution.py:25
  278.8 54.5 %collective-permute-start.32 = (bf16[768,768]{1,0:T(8,128)(2,1)}, bf16[768,768]{1,0:T(8,128)(2,1)}, u32[]{:S(2)}, u32[]{:S(2)}) collective-permute-start(bf16[768,768]{1,0:T(8,128)(2,1)} %add_convert_fusion.4), channel_id=1, source_target_pairs={{0,2},{1,3},{2,0},{3,1},{4,6},{5,7},{6,4},{7,5},{8,10},{9,11},{10,... | collective-permute-start | bytes 3538952 | tf_op jit(solution)/shard_map/ppermute | solution.py:25
  290.3 24.0 %collective-permute-start.12 = (bf16[192,768]{1,0:T(8,128)(2,1)}, bf16[192,768]{1,0:T(8,128)(2,1)}, u32[]{:S(2)}, u32[]{:S(2)}) collective-permute-start(bf16[192,768]{1,0:T(8,128)(2,1)} %add_convert_fusion.18), channel_id=1, source_target_pairs={{0,2},{1,3},{2,0},{3,1},{4,6},{5,7},{6,4},{7,5},{8,10},{9,11},{10,... | collective-permute-start | bytes 884744 | tf_op jit(solution)/shard_map/ppermute | solution.py:25
  295.7 35.5 %collective-permute-start.19 = (bf16[384,768]{1,0:T(8,128)(2,1)}, bf16[384,768]{1,0:T(8,128)(2,1)}, u32[]{:S(2)}, u32[]{:S(2)}) collective-permute-start(bf16[384,768]{1,0:T(8,128)(2,1)} %add_convert_fusion.17), channel_id=1, source_target_pairs={{0,2},{1,3},{2,0},{3,1},{4,6},{5,7},{6,4},{7,5},{8,10},{9,11},{10,... | collective-permute-start | bytes 1769480 | tf_op jit(solution)/shard_map/ppermute | solution.py:25
  297.2 87.3 %all-to-all-start.5 = ((bf16[8,224,768]{2,1,0:T(8,128)(2,1)}), bf16[8,224,768]{2,1,0:T(8,128)(2,1)}, u32[]{:S(2)}, u32[]{:S(2)}) async-start(bf16[8,224,768]{2,1,0:T(8,128)(2,1)} %get-tuple-element.89), calls=%async_computation.5 | async-start | bytes 5505024 | tf_op jit(solution)/shard_map/all_to_all | solution.py:376
  317.4 43.6 %collective-permute-start.35 = (bf16[768,768]{1,0:T(8,128)(2,1)S(1)}, bf16[768,768]{1,0:T(8,128)(2,1)S(1)}, u32[]{:S(2)}, u32[]{:S(2)}) collective-permute-start(bf16[768,768]{1,0:T(8,128)(2,1)S(1)} %copy-done.58), channel_id=1, source_target_pairs={{0,2},{1,3},{2,0},{3,1},{4,6},{5,7},{6,4},{7,5},{8,10},{9,11},{10,... | collective-permute-start | bytes 3538952 | tf_op jit(solution)/shard_map/ppermute | solution.py:25
  332.8 48.5 %collective-permute-start.20 = (bf16[384,768]{1,0:T(8,128)(2,1)S(1)}, bf16[384,768]{1,0:T(8,128)(2,1)S(1)}, u32[]{:S(2)}, u32[]{:S(2)}) collective-permute-start(bf16[384,768]{1,0:T(8,128)(2,1)S(1)} %add_convert_fusion.16), channel_id=1, source_target_pairs={{0,1},{1,0},{2,3},{3,2},{4,5},{5,4},{6,7},{7,6},{8,9},{9,8},{10,11... | collective-permute-start | bytes 1769480 | tf_op jit(solution)/shard_map/ppermute | solution.py:25
  333.3 21.0 %collective-permute-start.24 = (bf16[4,96,768]{2,1,0:T(8,128)(2,1)S(1)}, bf16[4,96,768]{2,1,0:T(8,128)(2,1)S(1)}, u32[]{:S(2)}, u32[]{:S(2)}) collective-permute-start(bf16[4,96,768]{2,1,0:T(8,128)(2,1)S(1)} %dynamic-slice_bitcast_fusion), channel_id=1, source_target_pairs={{0,4},{4,0},{8,12},{12,8},{16,20},{20,16},{24,28},{28,24},{1,5},{5... | collective-permute-start | bytes 1769480 | tf_op jit(solution)/shard_map/ppermute | solution.py:25
  337.5 26.9 %collective-permute-start.22 = (bf16[392,768]{1,0:T(8,128)(2,1)S(1)}, bf16[392,768]{1,0:T(8,128)(2,1)S(1)}, u32[]{:S(2)}, u32[]{:S(2)}) collective-permute-start(bf16[392,768]{1,0:T(8,128)(2,1)S(1)} %add_convert_fusion.15), channel_id=1, source_target_pairs={{0,2},{1,3},{2,0},{3,1},{4,6},{5,7},{6,4},{7,5},{8,10},{9,11},{10,... | collective-permute-start | bytes 1806344 | tf_op jit(solution)/shard_map/ppermute | solution.py:25
  354.5 14.5 %collective-permute-start.25 = (bf16[2,96,768]{2,1,0:T(8,128)(2,1)S(1)}, bf16[2,96,768]{2,1,0:T(8,128)(2,1)S(1)}, u32[]{:S(2)}, u32[]{:S(2)}) collective-permute-start(bf16[2,96,768]{2,1,0:T(8,128)(2,1)S(1)} %dynamic-slice_bitcast_fusion.1), channel_id=1, source_target_pairs={{0,8},{4,12},{8,0},{12,4},{16,24},{20,28},{24,16},{28,20},{1,9},{5... | collective-permute-start | bytes 884744 | tf_op jit(solution)/shard_map/ppermute | solution.py:25
  384.5 97.3 %all-to-all-start.6 = ((bf16[8,192,768]{2,1,0:T(8,128)(2,1)}), bf16[8,192,768]{2,1,0:T(8,128)(2,1)}, u32[]{:S(2)}, u32[]{:S(2)}) async-start(bf16[8,192,768]{2,1,0:T(8,128)(2,1)} %pad_maximum_fusion.3), calls=%async_computation.6 | async-start | bytes 4718592 | tf_op jit(solution)/shard_map/all_to_all | solution.py:376
  396.9 40.9 %collective-permute-start.28 = (bf16[2,128,768]{2,1,0:T(8,128)(2,1)S(1)}, bf16[2,128,768]{2,1,0:T(8,128)(2,1)S(1)}, u32[]{:S(2)}, u32[]{:S(2)}) collective-permute-start(bf16[2,128,768]{2,1,0:T(8,128)(2,1)S(1)} %pad_maximum_fusion.16), channel_id=1, source_target_pairs={{0,8},{4,12},{8,0},{12,4},{16,24},{20,28},{24,16},{28,20},{1,9},{5... | collective-permute-start | bytes 1179656 | tf_op jit(solution)/shard_map/ppermute | solution.py:25
  438.9 18.8 %collective-permute-start.29 = (bf16[4,128,768]{2,1,0:T(8,128)(2,1)S(1)}, bf16[4,128,768]{2,1,0:T(8,128)(2,1)S(1)}, u32[]{:S(2)}, u32[]{:S(2)}) collective-permute-start(bf16[4,128,768]{2,1,0:T(8,128)(2,1)S(1)} %pad_maximum_fusion.9), channel_id=1, source_target_pairs={{0,4},{4,0},{8,12},{12,8},{16,20},{20,16},{24,28},{28,24},{1,5},{5... | collective-permute-start | bytes 2359304 | tf_op jit(solution)/shard_map/ppermute | solution.py:25
  (171 other events, 953.6 us)
